TPU v7x, 32 devices: a whole 2x2x4 slice. The times are simulated.
32 devices in a mesh: rep: 4 (over x, core), fsdp: 8 (over z, y).
Axes of the slice: x: 2, y: 2, z: 4, core: 2. Of those that a mesh axis runs over, the one named last changes fastest.
Arguments:
- normed: bfloat16 [16384, 4096], P(('rep', 'fsdp')), may hold values from -208 to 208
- cotangent: bfloat16 [16384, 2048], P(('rep', 'fsdp')), may hold values from -18 to 18
- inner_weight: float32 [4, 4096, 2048], P('rep', 'fsdp'), may hold values from -0.09865 to 0.09865
- adam_first: float32 [4, 4096, 2048], P('rep', 'fsdp'), may hold values from -0.00015258789 to 0.00015258789
- adam_second: float32 [4, 4096, 2048], P('rep', 'fsdp'), may hold values from 2.9802322e-08 to 4.7683716e-07
- anchor: float32 [4096, 2048], P('fsdp', 'rep'), may hold values from -0.09375 to 0.09375
- outer_moment: float32 [4096, 2048], P('fsdp', 'rep'), may hold values from -7.6293945e-05 to 7.6293945e-05
Outputs:
- input_grad: bfloat16 [16384, 4096], P(('rep', 'fsdp'))
- synced_weight: float32 [4096, 2048], P('fsdp')
- moment_out: float32 [4096, 2048], P('fsdp', 'rep')
All inputs are finite; a program needn't handle non-finite values.
Results may differ from a plain program's by a relative error of at most 0.007.
Values may be sent and summed in bfloat16 or wider, within the bound.
No kernel may reach another device: no remote copies, remote signals or barrier semaphores. Data moves between devices by JAX's collectives and lax.ppermute only.
A program may use at most 128 MiB of HBM per device.

v0:
```python
import jax
import jax.numpy as jnp
from jax import lax
from jax.sharding import PartitionSpec as P

BETA_ONE = 0.9
BETA_TWO = 0.95
ADAM_EPS = 1e-08
DECAY = 0.1
RATE_INNER = 0.0004
RATE_OUTER = 0.7
MOMENTUM = 0.9


def shards(normed, cotangent, inner_weight, adam_first, adam_second, anchor, outer_moment):
    weight = inner_weight[0]
    block_rows = cotangent.shape[0]
    group_rows = block_rows * lax.axis_size("fsdp")
    weight_half = weight.astype(jnp.bfloat16)
    image = lax.dot_general(
        cotangent,
        lax.all_gather(weight_half, "fsdp", axis=0, tiled=True),
        (((1,), (1,)), ((), ())),
        preferred_element_type=jnp.float32,
    )
    back = image.astype(jnp.bfloat16)
    summed = lax.psum_scatter(
        lax.dot_general(
            normed, cotangent, (((0,), (0,)), ((), ())), preferred_element_type=jnp.float32
        ).astype(jnp.bfloat16),
        "fsdp",
        scatter_dimension=0,
        tiled=True,
    ).astype(jnp.float32)
    gradient = summed / group_rows
    square_sum = lax.psum(jnp.sum(gradient * gradient), "fsdp")
    factor = jnp.minimum(1.0, 1.0 / (jnp.sqrt(square_sum) + 1e-06))
    clipped = gradient * factor
    first_new = BETA_ONE * adam_first[0] + (1.0 - BETA_ONE) * clipped
    second_new = BETA_TWO * adam_second[0] + (1.0 - BETA_TWO) * clipped * clipped
    updated = weight - RATE_INNER * (first_new / (jnp.sqrt(second_new) + ADAM_EPS) + DECAY * weight)
    updated_sum = lax.psum_scatter(updated, "rep", scatter_dimension=1, tiled=True)
    outer_step = anchor - updated_sum / lax.axis_size("rep")
    moment_out = MOMENTUM * outer_moment + outer_step
    anchor_next = anchor - RATE_OUTER * (outer_step + MOMENTUM * moment_out)
    synced_weight = lax.all_gather(
        anchor_next.astype(jnp.bfloat16), "rep", axis=1, tiled=True
    ).astype(anchor_next.dtype)
    return (back, synced_weight, moment_out)


def solution(mesh):
    placed = (
        P(("rep", "fsdp"), None),
        P(("rep", "fsdp"), None),
        P("rep", "fsdp", None),
        P("rep", "fsdp", None),
        P("rep", "fsdp", None),
        P("fsdp", "rep"),
        P("fsdp", "rep"),
    )
    return jax.shard_map(
        shards,
        mesh=mesh,
        in_specs=placed,
        out_specs=(P(("rep", "fsdp"), None), P("fsdp", None), P("fsdp", "rep")),
        check_vma=False,
    )
```

profile of v0, /device:TPU:0, one launch (start us, length us, event | category | flops | bytes accessed | tf_op | source)
XLA Modules:
  0.0 646.5 jit_solution(14217911728606509213)
XLA Ops:
  7.2 0.0 copy-start
  7.2 0.0 reduce-scatter.3.cloned.1.call-start
  7.2 1.5 copy-done
  8.8 14.6 %convolution_convert_fusion = bf16[4096,2048]{1,0:T(8,128)(2,1)} fusion(bf16[512,4096]{1,0:T(8,128)(2,1)} %param.7, bf16[512,2048]{1,0:T(8,128)(2,1)S(1)} %copy-done), kind=kOutput, calls=%fused_computation | convolution fusion | flops 8598323200 | bytes 23068672 | tf_op jit(solution)/shard_map/dot_general | solution.py:28
  23.4 0.0 reduce-scatter.3.cloned.1.call-update
  23.4 0.0 reduce-scatter.5.cloned.1.call-start
  23.5 285.1 %reduce-scatter.3.cloned.1.call-done = bf16[512,2048]{1,0:T(8,128)(2,1)} async-done(((bf16[4096,2048]{1,0:T(8,128)(2,1)}), bf16[512,2048]{1,0:T(8,128)(2,1)}) %reduce-scatter.3.cloned.1.call-update) | async-done | bytes 2097168 | tf_op jit(solution)/shard_map/reduce_scatter | solution.py:27
  308.5 3.3 fusion.7
  311.8 20.1 %psum.7 = f32[]{:T(128)} all-reduce(f32[]{:T(128)} %fusion.7), channel_id=1, replica_groups=mesh['rep'=4,'fsdp'=8] {'fsdp'}, use_global_device_ids=true, to_apply=%region_2.0 | all-reduce | flops 1 | bytes 8 | tf_op jit(solution)/shard_map/psum | solution.py:36
  332.6 8.2 %fusion.5 = f32[512,2048]{1,0:T(8,128)} fusion(bf16[512,2048]{1,0:T(8,128)(2,1)} %reduce-scatter.3.cloned.1.call-done, f32[1,512,2048]{2,1,0:T(8,128)} %param.9, f32[1,512,2048]{2,1,0:T(8,128)} %param.11, f32[1,512,2048]{2,1,0:T(8,128)} %param.10, f32[]{:T(128)S(6)} %mul.66), kind=kLoop, calls=%fused_computation.10 | loop fusion | flops 15728640 | bytes 18874372 | tf_op jit(solution)/shard_map/sub | solution.py:41
  340.8 0.0 reduce-scatter.5.cloned.1.call-update
  340.8 0.0 copy-start.1
  340.8 0.0 all-gather.3.cloned.1.call-start
  340.8 3.9 bitcast_convert_fusion
  344.8 0.0 all-gather.3.cloned.1.call-update
  344.8 0.2 all-gather.5.cloned.1.call-start
  345.0 37.7 %reduce-scatter.5.cloned.1.call-done = f32[512,512]{1,0:T(8,128)} async-done(((f32[512,2048]{1,0:T(8,128)}), f32[512,512]{1,0:T(8,128)}) %reduce-scatter.5.cloned.1.call-update) | async-done | bytes 1048592 | tf_op jit(solution)/shard_map/reduce_scatter | solution.py:42
  382.7 0.0 copy-done.1
  382.7 3.1 subtract_convert_fusion
  385.7 0.0 all-gather.5.cloned.1.call-update
  385.8 227.3 %all-gather.3.cloned.1.call-done = bf16[4096,2048]{1,0:T(8,128)(2,1)} async-done(((bf16[512,2048]{1,0:T(8,128)(2,1)}), bf16[4096,2048]{1,0:T(8,128)(2,1)}) %all-gather.3.cloned.1.call-update) | async-done | bytes 16777232 | tf_op jit(solution)/shard_map/all_gather | solution.py:22
  613.0 13.8 %convolution_convert_fusion.1 = bf16[512,4096]{1,0:T(8,128)(2,1)} fusion(bf16[512,2048]{1,0:T(8,128)(2,1)S(1)} %copy-done, bf16[4096,2048]{1,0:T(8,128)(2,1)} %all-gather.3.cloned.1.call-done), kind=kOutput, calls=%fused_computation.2 | convolution fusion | flops 8592031744 | bytes 23068672 | tf_op jit(solution)/shard_map/dot_general | solution.py:20
  626.8 9.0 %all-gather.5.cloned.1.call-done = bf16[512,2048]{1,0:T(8,128)(2,1)} async-done(((bf16[512,512]{1,0:T(8,128)(2,1)}), bf16[512,2048]{1,0:T(8,128)(2,1)}) %all-gather.5.cloned.1.call-update) | async-done | bytes 2097168 | tf_op jit(solution)/shard_map/all_gather | solution.py:46
  635.8 4.1 convert_element_type.23
Async XLA Ops:
  7.2 1.6 copy-start
  7.2 301.3 %reduce-scatter.3.cloned.1.call-start = ((), (), s32[]{:S(2)}) async-start(), calls=%async_computation.3 | async-start | bytes 18874368 | tf_op jit(solution)/shard_map/reduce_scatter | solution.py:27
  23.4 359.3 %reduce-scatter.5.cloned.1.call-start = ((), (), s32[]{:S(2)}) async-start(), calls=%async_computation.4 | async-start | bytes 5242880 | tf_op jit(solution)/shard_map/reduce_scatter | solution.py:42
  340.8 41.9 %copy-start.1 = (f32[512,512]{1,0:T(8,128)S(1)}, f32[512,512]{1,0:T(8,128)}, u32[]{:S(2)}) copy-start(f32[512,512]{1,0:T(8,128)} %param.12) | copy-start | bytes 3145732
  340.8 272.2 %all-gather.3.cloned.1.call-start = ((), (), s32[]{:S(2)}) async-start(), calls=%async_computation.2 | async-start | bytes 18874368 | tf_op jit(solution)/shard_map/all_gather | solution.py:22
  344.8 291.0 %all-gather.5.cloned.1.call-start = ((), (), s32[]{:S(2)}) async-start(), calls=%async_computation.5 | async-start | bytes 2621440 | tf_op jit(solution)/shard_map/all_gather | solution.py:46
Sparse Core Ops, SparseCore 0:
  23.5 284.9 reduce-scatter.2
  340.9 41.7 reduce-scatter.4
  385.4 227.6 all-gather.2
  615.0 20.7 all-gather.4
where the time goes:
time: 647 us; the launch traced here: 646 us
  waiting for transfers between devices  559 us (86%)
  matrix products  28.4 us (4%)
  other arithmetic  22.5 us (3%)
  blocking collectives  20.1 us (3%)
  between operations  14.5 us (2%)
    reduce_scatter x1, waiting for transfers between devices, shards(): lax.psum_scatter(lax.dot_general(normed, cotangent, (((0,), (0,)), ((), (...  285 us
    all_gather x1, waiting for transfers between devices, shards(): lax.all_gather(weight_half, 'fsdp', axis=0, tiled=True)  227 us
    reduce_scatter x1, waiting for transfers between devices, shards(): lax.psum_scatter(updated, 'rep', scatter_dimension=1, tiled=True)  37.7 us
    psum x1, blocking collectives, shards(): square_sum = lax.psum(jnp.sum(gradient * gradient), 'fsdp')  20.1 us
    dot_general x1, matrix products, shards(): lax.dot_general(normed, cotangent, (((0,), (0,)), ((), ())), preferred_el...  14.6 us
    dot_general x1, matrix products, shards(): lax.dot_general(cotangent, lax.all_gather(weight_half, 'fsdp', axis=0, ti...  13.8 us
  transfers between devices with their start and end apart: 4, of which 4 were waited for; matrix products, arithmetic and copies ran while one was open for 3% of the time, Pallas kernels for 0%

commit v1 on v0

v1 whole, which is shorter than its diff:
```python
import jax
import jax.numpy as jnp
from jax import lax
from jax.sharding import PartitionSpec as P

BETA_ONE = 0.9
BETA_TWO = 0.95
ADAM_EPS = 1e-08
DECAY = 0.1
RATE_INNER = 0.0004
RATE_OUTER = 0.7
MOMENTUM = 0.9

LINE = 4
PAIR = 2
BLOCK = LINE * PAIR
CHUNKS = 2
BF16 = jnp.bfloat16
F32 = jnp.float32


def dot(a, b, dims):
    return lax.dot_general(a, b, (dims, ((), ())), preferred_element_type=F32)


def shards(normed, cotangent, inner_weight, adam_first, adam_second, anchor, outer_moment):
    weight = inner_weight[0]
    tokens, model = normed.shape
    width = cotangent.shape[1]
    n = lax.axis_size("fsdp")
    reps = lax.axis_size("rep")
    outer = n // BLOCK
    rows = model // n
    unit = rows * outer
    me = lax.axis_index("fsdp")
    z, y = (me // PAIR) % LINE, me % PAIR
    middle = (z == 1) | (z == 2)

    across = [(f, f ^ 1) for f in range(n)]

    def along(hops):
        return [
            ((a * LINE + s) * PAIR + b, (a * LINE + t) * PAIR + b)
            for a in range(outer)
            for s, t in hops
            for b in range(PAIR)
        ]

    ends = along([(0, 1), (1, 0), (2, 3), (3, 2)])
    inward = along([(0, 1), (3, 2)])
    outward = along([(1, 0), (2, 3)])
    centre = along([(1, 2), (2, 1)])
    outer_groups = [[a * BLOCK + k for a in range(outer)] for k in range(BLOCK)]

    def send(value, pairs):
        return lax.ppermute(value, "fsdp", pairs)

    def columns(zz, yy):
        parts = [
            lax.dynamic_slice(normed, (0, ((a * LINE + zz) * PAIR + yy) * rows), (tokens, rows))
            for a in range(outer)
        ]
        return parts[0] if outer == 1 else jnp.concatenate(parts, axis=1)

    chunk = width // CHUNKS

    def cut(value, c):
        return value[:, c * chunk : (c + 1) * chunk]

    far, second, near = jnp.where(z < 2, 3, 0), jnp.where(z < 2, 2, 1), z ^ 1

    cot_other = send(cotangent, across)
    x_other = {}
    for name, zz in (("far", far), ("second", second), ("near", near), ("own", z)):
        x_other[name] = send(columns(zz, 1 - y), across)

    half = weight.astype(BF16)
    if outer > 1:
        half = lax.all_gather(half, "fsdp", axis=0, tiled=True, axis_index_groups=outer_groups)
    halves = unit // CHUNKS

    def gather(piece):
        one = send(piece, ends)
        mid = send(piece, centre)
        three = send(one, centre)
        two = mid + send(mid, outward)
        three_all = three + send(three, outward)
        return one, two, three_all

    gathered = [gather(half[c * halves : (c + 1) * halves]) for c in range(CHUNKS)]
    w_near, w_second, w_far = (
        jnp.concatenate([g[k] for g in gathered], axis=0) for k in range(3)
    )

    def partial(name, zz, c):
        return dot(columns(zz, y), cut(cotangent, c), ((0,), (0,))) + dot(
            x_other[name], cut(cot_other, c), ((0,), (0,))
        )

    def reduce(c):
        first = partial("far", far, c)
        r1 = send(first.astype(BF16), inward)
        r2a = send((first + r1.astype(F32)).astype(BF16), centre)
        next_ = partial("second", second, c)
        r2b = send(next_.astype(BF16), inward)
        last = partial("near", near, c)
        r3a = send((last + r2a.astype(F32)).astype(BF16), ends)
        r3b = send((next_ + r2b.astype(F32)).astype(BF16), centre)
        own = partial("own", z, c)
        return own + r3a.astype(F32) + r3b.astype(F32)

    summed = jnp.concatenate([reduce(c) for c in range(CHUNKS)], axis=1)
    if outer > 1:
        summed = lax.psum_scatter(
            summed.astype(BF16), "fsdp", scatter_dimension=0, tiled=True,
            axis_index_groups=outer_groups,
        ).astype(F32)

    back = jnp.zeros((tokens, model), BF16)
    for zz, w in ((z, half), (near, w_near), (second, w_second), (far, w_far)):
        mine = dot(cotangent, w, ((1,), (1,))).astype(BF16)
        theirs = dot(cot_other, w, ((1,), (1,))).astype(BF16)
        came = send(theirs, across)
        for yy, value in ((y, mine), (1 - y, came)):
            for a in range(outer):
                back = lax.dynamic_update_slice(
                    back,
                    value[:, a * rows : (a + 1) * rows],
                    (0, ((a * LINE + zz) * PAIR + yy) * rows),
                )

    rep = lax.axis_index("rep")
    weight_sum = lax.psum_scatter(weight, "rep", scatter_dimension=1, tiled=True)
    step_base = anchor - (1.0 - RATE_INNER * DECAY) * weight_sum / reps
    moment_base = MOMENTUM * outer_moment + step_base
    synced_base = anchor - RATE_OUTER * (step_base + MOMENTUM * moment_base)
    synced_base = lax.all_gather(synced_base.astype(BF16), "rep", axis=1, tiled=True)

    gradient = summed / (tokens * n)
    square_sum = lax.psum(jnp.sum(gradient * gradient), "fsdp")
    factor = jnp.minimum(1.0, 1.0 / (jnp.sqrt(square_sum) + 1e-06))
    clipped = gradient * factor
    first_new = BETA_ONE * adam_first[0] + (1.0 - BETA_ONE) * clipped
    second_new = BETA_TWO * adam_second[0] + (1.0 - BETA_TWO) * clipped * clipped
    update = (first_new / (jnp.sqrt(second_new) + ADAM_EPS)).astype(BF16)

    core = rep % 2
    quarter = width // reps
    swap_core = [(r, r ^ 1) for r in range(reps)]
    swap_x = [(r, r ^ 2) for r in range(reps)]

    def pick(value, low):
        return jnp.where(
            low == 0, value[:, 0 * quarter : 1 * quarter], value[:, 1 * quarter : 2 * quarter]
        )

    def take_parity(value, which):
        return jnp.concatenate(
            [pick(value[:, : 2 * quarter], which), pick(value[:, 2 * quarter :], which)], axis=1
        )

    came = lax.ppermute(take_parity(update, 1 - core), "rep", swap_core)
    chip = (take_parity(update, core).astype(F32) + came.astype(F32)).astype(BF16)
    other = lax.ppermute(chip, "rep", swap_x)
    total = chip.astype(F32) + other.astype(F32)
    total_half = total.astype(BF16)
    total_other = lax.ppermute(total_half, "rep", swap_core)
    even = jnp.where(core == 0, total_half, total_other)
    odd = jnp.where(core == 0, total_other, total_half)
    full = jnp.concatenate(
        [even[:, :quarter], odd[:, :quarter], even[:, quarter:], odd[:, quarter:]], axis=1
    )
    scale = RATE_INNER / reps
    mine = jnp.where(rep // 2 == 0, total[:, :quarter], total[:, quarter:])
    moment_out = moment_base + scale * mine
    synced = synced_base.astype(F32) - (RATE_OUTER * (1.0 + MOMENTUM) * scale) * full.astype(F32)
    return (back, synced, moment_out)


def solution(mesh):
    placed = (
        P(("rep", "fsdp"), None),
        P(("rep", "fsdp"), None),
        P("rep", "fsdp", None),
        P("rep", "fsdp", None),
        P("rep", "fsdp", None),
        P("fsdp", "rep"),
        P("fsdp", "rep"),
    )
    return jax.shard_map(
        shards,
        mesh=mesh,
        in_specs=placed,
        out_specs=(P(("rep", "fsdp"), None), P("fsdp", None), P("fsdp", "rep")),
        check_vma=False,
    )
```

time: 647 us -> 418 us (0.65)
  waiting for transfers between devices: 559 us -> 216 us
  starting transfers between devices: 0.34 us -> 47.9 us
  local copies, waits for them, and re-layouts: 1.55 us -> 30.5 us
  other arithmetic: 22.5 us -> 38.2 us
  matrix products: 28.4 us -> 39.8 us
  blocking collectives: 20.1 us -> 29.6 us
    reduce_scatter x2 -> x1, waiting for transfers between devices: 323 us -> 0.01 us  [shards(): lax.psum_scatter(weight, 'rep', scatter_dimension=1, tiled=True)]
    all_gather x2 -> x1, waiting for transfers between devices: 236 us -> 0.01 us  [shards(): lax.all_gather(synced_base.astype(BF16), 'rep', axis=1, tiled=True)]
    ppermute x0 -> x32, waiting for transfers between devices: none -> 216 us  [the longest x29 216 us: send(): return lax.ppermute(value, 'fsdp', pairs)]
    ppermute x0 -> x32, starting transfers between devices: none -> 47.9 us  [the longest x29 46.2 us: send(): return lax.ppermute(value, 'fsdp', pairs)]
    add x0 -> x8, other arithmetic: none -> 16.6 us  [the longest x2 5.15 us: gather(): two = mid + send(mid, outward)]
    dot_general x2 -> x24, matrix products: 28.4 us -> 39.8 us  [dot(): return lax.dot_general(a, b, (dims, ((), ())), preferred_element_type=F32)]
    psum x1, blocking collectives: 20.1 us -> 29.6 us  [shards(): square_sum = lax.psum(jnp.sum(gradient * gradient), 'fsdp')]
    dynamic_update_slice x0 -> x7, local copies, waits for them, and re-layouts: none -> 7.97 us  [shards(): lax.dynamic_update_slice(back, value[:, a * rows:(a + 1) * rows], (0, ((a...]
  transfers between devices with their start and end apart: 4 -> 34, of which waited for: 4 -> 12; matrix products, arithmetic and copies ran while one was open for 3% -> 24% of each run, Pallas kernels for 0% -> 0%
where the time goes in v1:
time: 418 us; the launch traced here: 417 us
  waiting for transfers between devices  216 us (52%)
  starting transfers between devices  47.9 us (11%)
  matrix products  39.8 us (10%)
  other arithmetic  38.2 us (9%)
  local copies, waits for them, and re-layouts  30.5 us (7%)
  blocking collectives  29.6 us (7%)
  between operations  15.3 us (4%)
    ppermute x29, waiting for transfers between devices, send(): return lax.ppermute(value, 'fsdp', pairs)  216 us
    ppermute x29, starting transfers between devices, send(): return lax.ppermute(value, 'fsdp', pairs)  46.2 us
    dot_general x24, matrix products, dot(): return lax.dot_general(a, b, (dims, ((), ())), preferred_element_type=F32)  39.8 us
    psum x1, blocking collectives, shards(): square_sum = lax.psum(jnp.sum(gradient * gradient), 'fsdp')  29.6 us
  transfers between devices with their start and end apart: 34, of which 12 were waited for; matrix products, arithmetic and copies ran while one was open for 24% of the time, Pallas kernels for 0%

profile of v1, /device:TPU:0, one launch (start us, length us, event | category | flops | bytes accessed | tf_op | source)
XLA Modules:
  0.0 417.2 jit_solution(7803249239796284819)
XLA Ops:
  7.2 3.0 collective-permute-start
  10.2 2.5 bitcast_convert_fusion
  16.3 3.0 constant_dynamic-slice_fusion.3
  21.9 3.4 fusion.34
  25.4 2.3 fusion.42
  27.7 2.5 fusion.36
  33.9 45.6 %collective-permute-done.17 = bf16[512,512]{1,0:T(8,128)(2,1)} collective-permute-done((bf16[512,512]{1,0:T(8,128)(2,1)}, bf16[512,512]{1,0:T(8,128)(2,1)}, u32[]{:S(2)}, u32[]{:S(2)}) %collective-permute-start.17) | collective-permute-done | bytes 524320 | tf_op jit(solution)/shard_map/ppermute | solution.py:56
  81.3 4.2 %collective-permute-start.24 = (bf16[512,1024]{1,0:T(8,128)(2,1)S(1)}, bf16[512,1024]{1,0:T(8,128)(2,1)S(1)}, u32[]{:S(2)}, u32[]{:S(2)}) collective-permute-start(bf16[512,1024]{1,0:T(8,128)(2,1)S(1)} %get-tuple-element.25), channel_id=1, source_target_pairs={{0,2},{1,3},{6,4},{7,5},{8,10},{9,11},{14,12},{15,13},{16,18},{17,... | collective-permute-start | bytes 3145736 | tf_op jit(solution)/shard_map/ppermute | solution.py:56
  91.5 17.5 %collective-permute-done.24 = bf16[512,1024]{1,0:T(8,128)(2,1)S(1)} collective-permute-done((bf16[512,1024]{1,0:T(8,128)(2,1)S(1)}, bf16[512,1024]{1,0:T(8,128)(2,1)S(1)}, u32[]{:S(2)}, u32[]{:S(2)}) %collective-permute-start.24) | collective-permute-done | bytes 1048608 | tf_op jit(solution)/shard_map/ppermute | solution.py:56
  109.0 4.4 %collective-permute-start.22 = (bf16[512,1024]{1,0:T(8,128)(2,1)S(1)}, bf16[512,1024]{1,0:T(8,128)(2,1)S(1)}, u32[]{:S(2)}, u32[]{:S(2)}) collective-permute-start(bf16[512,1024]{1,0:T(8,128)(2,1)S(1)} %get-tuple-element.27), channel_id=1, source_target_pairs={{0,2},{1,3},{6,4},{7,5},{8,10},{9,11},{14,12},{15,13},{16,18},{17,... | collective-permute-start | bytes 3145736 | tf_op jit(solution)/shard_map/ppermute | solution.py:56
  115.3 16.2 %collective-permute-done.18 = bf16[512,1024]{1,0:T(8,128)(2,1)S(1)} collective-permute-done((bf16[512,1024]{1,0:T(8,128)(2,1)S(1)}, bf16[512,1024]{1,0:T(8,128)(2,1)S(1)}, u32[]{:S(2)}, u32[]{:S(2)}) %collective-permute-start.18) | collective-permute-done | bytes 1048608 | tf_op jit(solution)/shard_map/ppermute | solution.py:56
  133.5 20.5 %collective-permute-done.27 = bf16[512,1024]{1,0:T(8,128)(2,1)S(1)} collective-permute-done((bf16[512,1024]{1,0:T(8,128)(2,1)S(1)}, bf16[512,1024]{1,0:T(8,128)(2,1)S(1)}, u32[]{:S(2)}, u32[]{:S(2)}) %collective-permute-start.27) | collective-permute-done | bytes 1048608 | tf_op jit(solution)/shard_map/ppermute | solution.py:56
  157.4 16.2 %collective-permute-done.22 = bf16[512,1024]{1,0:T(8,128)(2,1)S(1)} collective-permute-done((bf16[512,1024]{1,0:T(8,128)(2,1)S(1)}, bf16[512,1024]{1,0:T(8,128)(2,1)S(1)}, u32[]{:S(2)}, u32[]{:S(2)}) %collective-permute-start.22) | collective-permute-done | bytes 1048608 | tf_op jit(solution)/shard_map/ppermute | solution.py:56
  173.7 2.5 collective-permute-start.26
  177.9 2.8 collective-permute-start.20
  183.9 16.3 %collective-permute-done.26 = bf16[512,1024]{1,0:T(8,128)(2,1)S(1)} collective-permute-done((bf16[512,1024]{1,0:T(8,128)(2,1)S(1)}, bf16[512,1024]{1,0:T(8,128)(2,1)S(1)}, u32[]{:S(2)}, u32[]{:S(2)}) %collective-permute-start.26) | collective-permute-done | bytes 1048608 | tf_op jit(solution)/shard_map/ppermute | solution.py:56
  204.7 18.0 %collective-permute-done.20 = bf16[512,1024]{1,0:T(8,128)(2,1)S(1)} collective-permute-done((bf16[512,1024]{1,0:T(8,128)(2,1)S(1)}, bf16[512,1024]{1,0:T(8,128)(2,1)S(1)}, u32[]{:S(2)}, u32[]{:S(2)}) %collective-permute-start.20) | collective-permute-done | bytes 1048608 | tf_op jit(solution)/shard_map/ppermute | solution.py:56
  226.5 29.6 %psum.7 = f32[]{:T(128)} all-reduce(f32[]{:T(128)} %multiply_reduce_fusion), channel_id=1, replica_groups=mesh['rep'=4,'fsdp'=8] {'fsdp'}, use_global_device_ids=true, to_apply=%region_2.3 | all-reduce | flops 1 | bytes 8 | tf_op jit(solution)/shard_map/psum | solution.py:140
  256.8 5.9 %fusion.4 = bf16[512,2048]{1,0:T(8,128)(2,1)S(1)} fusion(f32[1,512,2048]{2,1,0:T(8,128)} %param.11, f32[1,512,2048]{2,1,0:T(8,128)} %param.10, f32[512,1024]{1,0:T(8,128)} %copy-done.4, f32[512,1024]{1,0:T(8,128)} %copy-done.5, f32[]{:T(128)S(6)} %mul.154), kind=kLoop, calls=%fused_computation.9 | loop fusion | flops 12582912 | bytes 14680068 | tf_op jit(solution)/shard_map/convert_element_type | solution.py:145
  264.0 2.6 broadcast_in_dim.3
  283.5 14.3 %collective-permute-done.8 = bf16[256,2048]{1,0:T(8,128)(2,1)S(1)} collective-permute-done((bf16[256,2048]{1,0:T(8,128)(2,1)}, bf16[256,2048]{1,0:T(8,128)(2,1)S(1)}, u32[]{:S(2)}, u32[]{:S(2)}) %collective-permute-start.8) | collective-permute-done | bytes 1048608 | tf_op jit(solution)/shard_map/ppermute | solution.py:56
  298.6 2.6 add.195
  303.3 16.6 %collective-permute-done.6 = bf16[256,2048]{1,0:T(8,128)(2,1)S(1)} collective-permute-done((bf16[256,2048]{1,0:T(8,128)(2,1)}, bf16[256,2048]{1,0:T(8,128)(2,1)S(1)}, u32[]{:S(2)}, u32[]{:S(2)}) %collective-permute-start.6) | collective-permute-done | bytes 1048608 | tf_op jit(solution)/shard_map/ppermute | solution.py:56
  320.7 2.6 add.194
  325.1 4.3 %fusion.21 = (f32[512,512]{1,0:T(8,128)}, bf16[512,512]{1,0:T(8,128)(2,1)}) fusion(f32[512,1024]{1,0:T(8,128)} %get-tuple-element.9, f32[512,512]{1,0:T(8,128)} %param.12, f32[512,512]{1,0:T(8,128)} %reduce-scatter.2.cloned.1.call-done, f32[512,512]{1,0:T(8,128)} %param.13, pred[]{:T(512)S(6)} %eq.19), kind=kLoop, calls=%fused_computation.47 | loop fusion | flops 3145728 | bytes 6815745 | tf_op jit(solution)/shard_map/add | solution.py:175
  329.5 3.8 fusion.18
  341.5 4.3 %fusion.19 = bf16[512,512]{0,1:T(8,128)(2,1)} fusion(bf16[512,2048]{1,0:T(8,128)(2,1)} %param.8, bf16[256,2048]{1,0:T(8,128)(2,1)} %add.195, bf16[256,2048]{1,0:T(8,128)(2,1)} %add.194), kind=kOutput, calls=%fused_computation.44 | convolution fusion | flops 1078198272 | bytes 4718592 | tf_op jit(solution)/shard_map/dot_general | solution.py:23
  357.5 5.3 %collective-permute-done.13 = bf16[256,2048]{1,0:T(8,128)(2,1)} collective-permute-done((bf16[256,2048]{1,0:T(8,128)(2,1)}, bf16[256,2048]{1,0:T(8,128)(2,1)}, u32[]{:S(2)}, u32[]{:S(2)}) %collective-permute-start.13) | collective-permute-done | bytes 1048608 | tf_op jit(solution)/shard_map/ppermute | solution.py:56
  364.7 18.7 %collective-permute-done.11 = bf16[256,2048]{1,0:T(8,128)(2,1)} collective-permute-done((bf16[256,2048]{1,0:T(8,128)(2,1)}, bf16[256,2048]{1,0:T(8,128)(2,1)}, u32[]{:S(2)}, u32[]{:S(2)}) %collective-permute-start.11) | collective-permute-done | bytes 1048608 | tf_op jit(solution)/shard_map/ppermute | solution.py:56
  385.4 2.2 fusion.16
  391.6 10.6 %collective-permute-done.14 = bf16[512,512]{0,1:T(8,128)(2,1)S(1)} collective-permute-done((bf16[512,512]{0,1:T(8,128)(2,1)}, bf16[512,512]{0,1:T(8,128)(2,1)S(1)}, u32[]{:S(2)}, u32[]{:S(2)}) %collective-permute-start.14) | collective-permute-done | bytes 524320 | tf_op jit(solution)/shard_map/ppermute | solution.py:56
  405.8 4.6 %multiply_subtract_fusion = f32[512,2048]{1,0:T(8,128)} fusion(bf16[512,2048]{1,0:T(8,128)(2,1)} %all-gather.2.cloned.1.call-done, bf16[512,512]{1,0:T(8,128)(2,1)} %get-tuple-element.31, bf16[512,512]{1,0:T(8,128)(2,1)S(1)} %get-tuple-element.20, bf16[512,512]{1,0:T(8,128)(2,1)} %get-tuple-element.32, bf16[512,512]{1,0:T(8,128)(2,1)S(1)} %get-tuple-element.19), kind=kLoop, calls=%fused_computation.7 | loop fusion | flops 11534336 | bytes 8388608 | tf_op jit(solution)/shard_map/sub | solution.py:176
  (136 shorter events, 92.9 us)
Async XLA Ops:
  7.2 317.9 %reduce-scatter.2.cloned.1.call-start = ((), (), s32[]{:S(2)}) async-start(), calls=%async_computation.1 | async-start | bytes 5242880 | tf_op jit(solution)/shard_map/reduce_scatter | solution.py:133
  7.2 72.3 %collective-permute-start = (bf16[512,2048]{1,0:T(8,128)(2,1)}, bf16[512,2048]{1,0:T(8,128)(2,1)S(1)}, u32[]{:S(2)}, u32[]{:S(2)}) collective-permute-start(bf16[512,2048]{1,0:T(8,128)(2,1)} %param.8), channel_id=1, source_target_pairs={{0,1},{1,0},{2,3},{3,2},{4,5},{5,4},{6,7},{7,6},{8,9},{9,8},{10,11... | collective-permute-start | bytes 6291464 | tf_op jit(solution)/shard_map/ppermute | solution.py:56
  14.8 260.6 %collective-permute-start.3 = (bf16[256,2048]{1,0:T(8,128)(2,1)}, bf16[256,2048]{1,0:T(8,128)(2,1)}, u32[]{:S(2)}, u32[]{:S(2)}) collective-permute-start(bf16[256,2048]{1,0:T(8,128)(2,1)} %get-tuple-element.17), channel_id=1, source_target_pairs={{0,2},{1,3},{2,0},{3,1},{4,6},{5,7},{6,4},{7,5},{8,10},{9,11},{10,... | collective-permute-start | bytes 3145736 | tf_op jit(solution)/shard_map/ppermute | solution.py:56
  19.3 69.4 %collective-permute-start.21 = (bf16[512,512]{1,0:T(8,128)(2,1)}, bf16[512,512]{1,0:T(8,128)(2,1)S(1)}, u32[]{:S(2)}, u32[]{:S(2)}) collective-permute-start(bf16[512,512]{1,0:T(8,128)(2,1)} %get-tuple-element.6), channel_id=1, source_target_pairs={{0,1},{1,0},{2,3},{3,2},{4,5},{5,4},{6,7},{7,6},{8,9},{9,8},{10,11... | collective-permute-start | bytes 1572872 | tf_op jit(solution)/shard_map/ppermute | solution.py:56
  19.8 59.7 %collective-permute-start.17 = (bf16[512,512]{1,0:T(8,128)(2,1)}, bf16[512,512]{1,0:T(8,128)(2,1)}, u32[]{:S(2)}, u32[]{:S(2)}) collective-permute-start(bf16[512,512]{1,0:T(8,128)(2,1)} %get-tuple-element.4), channel_id=1, source_target_pairs={{0,1},{1,0},{2,3},{3,2},{4,5},{5,4},{6,7},{7,6},{8,9},{9,8},{10,11... | collective-permute-start | bytes 1572872 | tf_op jit(solution)/shard_map/ppermute | solution.py:56
  21.3 92.5 %collective-permute-start.16 = (bf16[512,512]{1,0:T(8,128)(2,1)}, bf16[512,512]{1,0:T(8,128)(2,1)S(1)}, u32[]{:S(2)}, u32[]{:S(2)}) collective-permute-start(bf16[512,512]{1,0:T(8,128)(2,1)} %get-tuple-element.5), channel_id=1, source_target_pairs={{0,1},{1,0},{2,3},{3,2},{4,5},{5,4},{6,7},{7,6},{8,9},{9,8},{10,11... | collective-permute-start | bytes 1572872 | tf_op jit(solution)/shard_map/ppermute | solution.py:56
  21.8 383.9 %all-gather.2.cloned.1.call-start = ((), (), s32[]{:S(2)}) async-start(), calls=%async_computation.2 | async-start | bytes 2621440 | tf_op jit(solution)/shard_map/all_gather | solution.py:137
  81.3 27.8 %collective-permute-start.24 = (bf16[512,1024]{1,0:T(8,128)(2,1)S(1)}, bf16[512,1024]{1,0:T(8,128)(2,1)S(1)}, u32[]{:S(2)}, u32[]{:S(2)}) collective-permute-start(bf16[512,1024]{1,0:T(8,128)(2,1)S(1)} %get-tuple-element.25), channel_id=1, source_target_pairs={{0,2},{1,3},{6,4},{7,5},{8,10},{9,11},{14,12},{15,13},{16,18},{17,... | collective-permute-start | bytes 3145736 | tf_op jit(solution)/shard_map/ppermute | solution.py:56
  87.3 44.2 %collective-permute-start.18 = (bf16[512,1024]{1,0:T(8,128)(2,1)S(1)}, bf16[512,1024]{1,0:T(8,128)(2,1)S(1)}, u32[]{:S(2)}, u32[]{:S(2)}) collective-permute-start(bf16[512,1024]{1,0:T(8,128)(2,1)S(1)} %get-tuple-element.29), channel_id=1, source_target_pairs={{0,2},{1,3},{6,4},{7,5},{8,10},{9,11},{14,12},{15,13},{16,18},{17,... | collective-permute-start | bytes 3145736 | tf_op jit(solution)/shard_map/ppermute | solution.py:56
  89.4 64.6 %collective-permute-start.27 = (bf16[512,1024]{1,0:T(8,128)(2,1)S(1)}, bf16[512,1024]{1,0:T(8,128)(2,1)S(1)}, u32[]{:S(2)}, u32[]{:S(2)}) collective-permute-start(bf16[512,1024]{1,0:T(8,128)(2,1)S(1)} %get-tuple-element.23), channel_id=1, source_target_pairs={{0,2},{1,3},{6,4},{7,5},{8,10},{9,11},{14,12},{15,13},{16,18},{17,... | collective-permute-start | bytes 3145736 | tf_op jit(solution)/shard_map/ppermute | solution.py:56
  109.0 64.6 %collective-permute-start.22 = (bf16[512,1024]{1,0:T(8,128)(2,1)S(1)}, bf16[512,1024]{1,0:T(8,128)(2,1)S(1)}, u32[]{:S(2)}, u32[]{:S(2)}) collective-permute-start(bf16[512,1024]{1,0:T(8,128)(2,1)S(1)} %get-tuple-element.27), channel_id=1, source_target_pairs={{0,2},{1,3},{6,4},{7,5},{8,10},{9,11},{14,12},{15,13},{16,18},{17,... | collective-permute-start | bytes 3145736 | tf_op jit(solution)/shard_map/ppermute | solution.py:56
  113.9 42.0 %collective-permute-start.25 = (bf16[512,1024]{1,0:T(8,128)(2,1)S(1)}, bf16[512,1024]{1,0:T(8,128)(2,1)S(1)}, u32[]{:S(2)}, u32[]{:S(2)}) collective-permute-start(bf16[512,1024]{1,0:T(8,128)(2,1)S(1)} %add_convert_fusion.3), channel_id=1, source_target_pairs={{2,4},{3,5},{4,2},{5,3},{10,12},{11,13},{12,10},{13,11},{18,20},{1... | collective-permute-start | bytes 3145736 | tf_op jit(solution)/shard_map/ppermute | solution.py:56
  131.9 44.6 %collective-permute-start.19 = (bf16[512,1024]{1,0:T(8,128)(2,1)S(1)}, bf16[512,1024]{1,0:T(8,128)(2,1)S(1)}, u32[]{:S(2)}, u32[]{:S(2)}) collective-permute-start(bf16[512,1024]{1,0:T(8,128)(2,1)S(1)} %add_convert_fusion.6), channel_id=1, source_target_pairs={{2,4},{3,5},{4,2},{5,3},{10,12},{11,13},{12,10},{13,11},{18,20},{1... | collective-permute-start | bytes 3145736 | tf_op jit(solution)/shard_map/ppermute | solution.py:56
  154.0 23.9 %collective-permute-start.15 = (bf16[512,512]{1,0:T(8,128)(2,1)S(1)}, bf16[512,512]{1,0:T(8,128)(2,1)S(1)}, u32[]{:S(2)}, u32[]{:S(2)}) collective-permute-start(bf16[512,512]{1,0:T(8,128)(2,1)S(1)} %copy-done.15), channel_id=1, source_target_pairs={{0,1},{1,0},{2,3},{3,2},{4,5},{5,4},{6,7},{7,6},{8,9},{9,8},{10,11... | collective-permute-start | bytes 1572872 | tf_op jit(solution)/shard_map/ppermute | solution.py:56
  155.9 26.4 %collective-permute-start.28 = (bf16[512,1024]{1,0:T(8,128)(2,1)S(1)}, bf16[512,1024]{1,0:T(8,128)(2,1)S(1)}, u32[]{:S(2)}, u32[]{:S(2)}) collective-permute-start(bf16[512,1024]{1,0:T(8,128)(2,1)S(1)} %add_convert_fusion.1), channel_id=1, source_target_pairs={{2,4},{3,5},{4,2},{5,3},{10,12},{11,13},{12,10},{13,11},{18,20},{1... | collective-permute-start | bytes 3145736 | tf_op jit(solution)/shard_map/ppermute | solution.py:56
  173.7 26.6 %collective-permute-start.26 = (bf16[512,1024]{1,0:T(8,128)(2,1)S(1)}, bf16[512,1024]{1,0:T(8,128)(2,1)S(1)}, u32[]{:S(2)}, u32[]{:S(2)}) collective-permute-start(bf16[512,1024]{1,0:T(8,128)(2,1)S(1)} %add_convert_fusion.2), channel_id=1, source_target_pairs={{0,2},{1,3},{2,0},{3,1},{4,6},{5,7},{6,4},{7,5},{8,10},{9,11},{10,... | collective-permute-start | bytes 3145736 | tf_op jit(solution)/shard_map/ppermute | solution.py:56
  176.5 26.4 %collective-permute-start.23 = (bf16[512,1024]{1,0:T(8,128)(2,1)S(1)}, bf16[512,1024]{1,0:T(8,128)(2,1)S(1)}, u32[]{:S(2)}, u32[]{:S(2)}) collective-permute-start(bf16[512,1024]{1,0:T(8,128)(2,1)S(1)} %add_convert_fusion.4), channel_id=1, source_target_pairs={{2,4},{3,5},{4,2},{5,3},{10,12},{11,13},{12,10},{13,11},{18,20},{1... | collective-permute-start | bytes 3145736 | tf_op jit(solution)/shard_map/ppermute | solution.py:56
  177.9 44.8 %collective-permute-start.20 = (bf16[512,1024]{1,0:T(8,128)(2,1)S(1)}, bf16[512,1024]{1,0:T(8,128)(2,1)S(1)}, u32[]{:S(2)}, u32[]{:S(2)}) collective-permute-start(bf16[512,1024]{1,0:T(8,128)(2,1)S(1)} %add_convert_fusion.5), channel_id=1, source_target_pairs={{0,2},{1,3},{2,0},{3,1},{4,6},{5,7},{6,4},{7,5},{8,10},{9,11},{10,... | collective-permute-start | bytes 3145736 | tf_op jit(solution)/shard_map/ppermute | solution.py:56
  182.3 87.5 %collective-permute-start.7 = (bf16[256,2048]{1,0:T(8,128)(2,1)}, bf16[256,2048]{1,0:T(8,128)(2,1)}, u32[]{:S(2)}, u32[]{:S(2)}) collective-permute-start(bf16[256,2048]{1,0:T(8,128)(2,1)} %get-tuple-element.17), channel_id=1, source_target_pairs={{2,4},{3,5},{4,2},{5,3},{10,12},{11,13},{12,10},{13,11},{18,20},{1... | collective-permute-start | bytes 3145736 | tf_op jit(solution)/shard_map/ppermute | solution.py:56
  200.2 70.8 %collective-permute-start.2 = (bf16[256,2048]{1,0:T(8,128)(2,1)}, bf16[256,2048]{1,0:T(8,128)(2,1)}, u32[]{:S(2)}, u32[]{:S(2)}) collective-permute-start(bf16[256,2048]{1,0:T(8,128)(2,1)} %get-tuple-element.18), channel_id=1, source_target_pairs={{0,2},{1,3},{2,0},{3,1},{4,6},{5,7},{6,4},{7,5},{8,10},{9,11},{10,... | collective-permute-start | bytes 3145736 | tf_op jit(solution)/shard_map/ppermute | solution.py:56
  203.0 71.0 %collective-permute-start.5 = (bf16[256,2048]{1,0:T(8,128)(2,1)}, bf16[256,2048]{1,0:T(8,128)(2,1)}, u32[]{:S(2)}, u32[]{:S(2)}) collective-permute-start(bf16[256,2048]{1,0:T(8,128)(2,1)} %get-tuple-element.18), channel_id=1, source_target_pairs={{2,4},{3,5},{4,2},{5,3},{10,12},{11,13},{12,10},{13,11},{18,20},{1... | collective-permute-start | bytes 3145736 | tf_op jit(solution)/shard_map/ppermute | solution.py:56
  269.8 28.0 %collective-permute-start.8 = (bf16[256,2048]{1,0:T(8,128)(2,1)}, bf16[256,2048]{1,0:T(8,128)(2,1)S(1)}, u32[]{:S(2)}, u32[]{:S(2)}) collective-permute-start(bf16[256,2048]{1,0:T(8,128)(2,1)} %collective-permute-done.7), channel_id=1, source_target_pairs={{2,0},{3,1},{4,6},{5,7},{10,8},{11,9},{12,14},{13,15},{18,16},{19,... | collective-permute-start | bytes 3145736 | tf_op jit(solution)/shard_map/ppermute | solution.py:56
  272.4 63.4 %collective-permute-start.10 = (bf16[256,2048]{1,0:T(8,128)(2,1)}, bf16[256,2048]{1,0:T(8,128)(2,1)}, u32[]{:S(2)}, u32[]{:S(2)}) collective-permute-start(bf16[256,2048]{1,0:T(8,128)(2,1)} %collective-permute-done.2), channel_id=1, source_target_pairs={{2,4},{3,5},{4,2},{5,3},{10,12},{11,13},{12,10},{13,11},{18,20},{1... | collective-permute-start | bytes 3145736 | tf_op jit(solution)/shard_map/ppermute | solution.py:56
  274.0 45.9 %collective-permute-start.6 = (bf16[256,2048]{1,0:T(8,128)(2,1)}, bf16[256,2048]{1,0:T(8,128)(2,1)S(1)}, u32[]{:S(2)}, u32[]{:S(2)}) collective-permute-start(bf16[256,2048]{1,0:T(8,128)(2,1)} %collective-permute-done.5), channel_id=1, source_target_pairs={{2,0},{3,1},{4,6},{5,7},{10,8},{11,9},{12,14},{13,15},{18,16},{19,... | collective-permute-start | bytes 3145736 | tf_op jit(solution)/shard_map/ppermute | solution.py:56
  275.3 59.2 %collective-permute-start.12 = (bf16[256,2048]{1,0:T(8,128)(2,1)}, bf16[256,2048]{1,0:T(8,128)(2,1)}, u32[]{:S(2)}, u32[]{:S(2)}) collective-permute-start(bf16[256,2048]{1,0:T(8,128)(2,1)} %collective-permute-done.3), channel_id=1, source_target_pairs={{2,4},{3,5},{4,2},{5,3},{10,12},{11,13},{12,10},{13,11},{18,20},{1... | collective-permute-start | bytes 3145736 | tf_op jit(solution)/shard_map/ppermute | solution.py:56
  278.6 44.7 %collective-permute-start.30 = (bf16[512,1024]{1,0:T(8,128)(2,1)S(1)}, bf16[512,1024]{1,0:T(8,128)(2,1)S(1)}, u32[]{:S(2)}, u32[]{:S(2)}) collective-permute-start(bf16[512,1024]{1,0:T(8,128)(2,1)S(1)} %add_convert_fusion), channel_id=1, source_target_pairs={{0,16},{8,24},{16,0},{24,8},{1,17},{9,25},{17,1},{25,9},{2,18},{10... | collective-permute-start | bytes 3145736 | tf_op jit(solution)/shard_map/ppermute | solution.py:164
  297.8 54.2 %collective-permute-start.1 = (bf16[512,512]{1,0:T(8,128)(2,1)}, bf16[512,512]{1,0:T(8,128)(2,1)}, u32[]{:S(2)}, u32[]{:S(2)}) collective-permute-start(bf16[512,512]{1,0:T(8,128)(2,1)} %convolution_convert_fusion.2), channel_id=1, source_target_pairs={{0,1},{1,0},{2,3},{3,2},{4,5},{5,4},{6,7},{7,6},{8,9},{9,8},{10,11... | collective-permute-start | bytes 1572872 | tf_op jit(solution)/shard_map/ppermute | solution.py:56
  319.9 28.0 %collective-permute-start.4 = (bf16[512,512]{0,1:T(8,128)(2,1)}, bf16[512,512]{0,1:T(8,128)(2,1)}, u32[]{:S(2)}, u32[]{:S(2)}) collective-permute-start(bf16[512,512]{0,1:T(8,128)(2,1)} %fusion.15), channel_id=1, source_target_pairs={{0,1},{1,0},{2,3},{3,2},{4,5},{5,4},{6,7},{7,6},{8,9},{9,8},{10,11... | collective-permute-start | bytes 1572872 | tf_op jit(solution)/shard_map/ppermute | solution.py:56
  333.2 16.7 %collective-permute-start.9 = (bf16[512,512]{0,1:T(8,128)(2,1)}, bf16[512,512]{0,1:T(8,128)(2,1)}, u32[]{:S(2)}, u32[]{:S(2)}) collective-permute-start(bf16[512,512]{0,1:T(8,128)(2,1)} %fusion.18), channel_id=1, source_target_pairs={{0,1},{1,0},{2,3},{3,2},{4,5},{5,4},{6,7},{7,6},{8,9},{9,8},{10,11... | collective-permute-start | bytes 1572872 | tf_op jit(solution)/shard_map/ppermute | solution.py:56
  334.5 28.3 %collective-permute-start.13 = (bf16[256,2048]{1,0:T(8,128)(2,1)}, bf16[256,2048]{1,0:T(8,128)(2,1)}, u32[]{:S(2)}, u32[]{:S(2)}) collective-permute-start(bf16[256,2048]{1,0:T(8,128)(2,1)} %collective-permute-done.12), channel_id=1, source_target_pairs={{2,0},{3,1},{4,6},{5,7},{10,8},{11,9},{12,14},{13,15},{18,16},{19,... | collective-permute-start | bytes 3145736 | tf_op jit(solution)/shard_map/ppermute | solution.py:56
  335.8 47.6 %collective-permute-start.11 = (bf16[256,2048]{1,0:T(8,128)(2,1)}, bf16[256,2048]{1,0:T(8,128)(2,1)}, u32[]{:S(2)}, u32[]{:S(2)}) collective-permute-start(bf16[256,2048]{1,0:T(8,128)(2,1)} %collective-permute-done.10), channel_id=1, source_target_pairs={{2,0},{3,1},{4,6},{5,7},{10,8},{11,9},{12,14},{13,15},{18,16},{19,... | collective-permute-start | bytes 3145736 | tf_op jit(solution)/shard_map/ppermute | solution.py:56
  385.4 17.8 %collective-permute-start.31 = (bf16[512,1024]{1,0:T(8,128)(2,1)S(1)}, bf16[512,1024]{1,0:T(8,128)(2,1)}, u32[]{:S(2)}, u32[]{:S(2)}) collective-permute-start(bf16[512,1024]{1,0:T(8,128)(2,1)S(1)} %get-tuple-element.10), channel_id=1, source_target_pairs={{0,8},{8,0},{16,24},{24,16},{1,9},{9,1},{17,25},{25,17},{2,10},{10... | collective-permute-start | bytes 3145736 | tf_op jit(solution)/shard_map/ppermute | solution.py:167
  (18 other events, 145.3 us)
Sparse Core Ops, SparseCore 0:
  22.0 44.7 reduce-scatter.1
  329.6 20.9 all-gather.1

commit v2 on v0

v2 whole, which is shorter than its diff:
```python
import functools

import jax
import jax.numpy as jnp
from jax import lax
from jax.experimental import pallas as pl
from jax.experimental.pallas import tpu as pltpu
from jax.sharding import PartitionSpec as P

BETA_ONE = 0.9
BETA_TWO = 0.95
ADAM_EPS = 1e-08
DECAY = 0.1
RATE_INNER = 0.0004
RATE_OUTER = 0.7
MOMENTUM = 0.9

LINE = 4
PAIR = 2
BLOCK = LINE * PAIR
BF16 = jnp.bfloat16
F32 = jnp.float32


VMEM_BYTES = 40 * 1024 * 1024


def dot(a, b, dims):
    return lax.dot_general(a, b, (dims, ((), ())), preferred_element_type=F32)


def call(body, grid, prefetch, in_specs, out_specs, out_shape, scratch, aliases, flops, args):
    moved = sum(v.size * v.dtype.itemsize for v in jax.tree.leaves(out_shape))
    return pl.pallas_call(
        body,
        grid_spec=pltpu.PrefetchScalarGridSpec(
            num_scalar_prefetch=1,
            grid=grid,
            in_specs=in_specs,
            out_specs=out_specs,
            scratch_shapes=scratch,
        ),
        out_shape=out_shape,
        input_output_aliases=aliases,
        compiler_params=pltpu.CompilerParams(vmem_limit_bytes=VMEM_BYTES),
        cost_estimate=pl.CostEstimate(
            flops=flops, bytes_accessed=4 * moved, transcendentals=0
        ),
    )(prefetch, *args)


def pick_body(axis, at_ref, *refs):
    del at_ref
    out_ref, offset = refs[-1], 0
    for ref in refs[:-1]:
        size = ref.shape[axis]
        if axis:
            out_ref[:, offset : offset + size] = ref[...]
        else:
            out_ref[offset : offset + size, :] = ref[...]
        offset += size


def pick(blocks, axis):
    height = blocks[0][0].shape[0]
    sizes = [width for _, width, _ in blocks]
    shape = (height, sum(sizes)) if axis else (height * len(blocks), sizes[0])
    return call(
        functools.partial(pick_body, axis),
        (1,),
        jnp.stack([jnp.int32(i) for _, _, i in blocks]),
        [
            pl.BlockSpec((height, width), functools.partial(lambda k, j, at: (0, at[k]), k))
            for k, width in enumerate(sizes)
        ],
        pl.BlockSpec(shape, lambda j, at: (0, 0)),
        jax.ShapeDtypeStruct(shape, blocks[0][0].dtype),
        [],
        {},
        0,
        [v for v, _, _ in blocks],
    )


def product_body(chunks, added, split, at_ref, x_ref, x_other_ref, *refs):
    del at_ref
    own, other = refs[0:chunks], refs[chunks : 2 * chunks]
    came, outs = refs[2 * chunks : 2 * chunks + added], refs[2 * chunks + added :]
    for c in range(chunks):
        value = dot(x_ref[...], own[c][...], ((0,), (0,)))
        value = value + dot(x_other_ref[...], other[c][...], ((0,), (0,)))
        for ref in came:
            value = value + ref[...].astype(F32)
        if split:
            outs[c][...] = value.astype(outs[c].dtype)
        else:
            width = value.shape[1]
            outs[0][:, c * width : (c + 1) * width] = value.astype(outs[0].dtype)


def product(x, at, x_other, other_at, cot, cot_other, chunks, quarter, unit, came, dtype, split):
    tokens = x.shape[0]
    count = len(chunks)
    narrow = pl.BlockSpec((unit, quarter), lambda h, at: (0, h))
    shape = jax.ShapeDtypeStruct((unit, 2 * quarter), dtype)
    if split:
        out_specs, out_shape = [narrow] * count, [shape] * count
    else:
        out_specs = pl.BlockSpec((unit, count * quarter), lambda h, at: (0, h))
        out_shape = jax.ShapeDtypeStruct((unit, 2 * count * quarter), dtype)
    return call(
        functools.partial(product_body, count, len(came), split),
        (2,),
        jnp.stack([at, jnp.int32(other_at)]).astype(jnp.int32),
        [
            pl.BlockSpec((tokens, unit), lambda h, at: (0, at[0])),
            pl.BlockSpec((tokens, unit), lambda h, at: (0, at[1])),
            *[
                pl.BlockSpec(
                    (tokens, quarter), functools.partial(lambda c, h, at: (0, c + 2 * h), c)
                )
                for c in chunks
            ],
            *([pl.BlockSpec((tokens, quarter), lambda h, at: (0, h))] * count),
            *([narrow] * len(came)),
        ],
        out_specs,
        out_shape,
        [],
        {},
        8 * tokens * unit * quarter * count,
        (x, x_other, *([cot] * count), *(cot_other[c] for c in chunks), *came),
    )


def image_body(pieces, held, at_ref, c_ref, *refs):
    del at_ref
    others, refs = refs[:2], refs[2:]
    weights, refs = refs[:pieces], refs[pieces:]
    back_ref, theirs_ref = refs[held:]
    w = weights[0][...]
    for ref in weights[1:]:
        w = w + ref[...]
    quarter = others[0].shape[1] // 2
    back_ref[...] = dot(c_ref[...], w, ((1,), (1,))).astype(back_ref.dtype)
    value = None
    for c, ref in enumerate(others):
        for h in range(2):
            q = c + 2 * h
            term = dot(
                ref[:, h * quarter : (h + 1) * quarter],
                w[:, q * quarter : (q + 1) * quarter],
                ((1,), (1,)),
            )
            value = term if value is None else value + term
    theirs_ref[...] = value.astype(theirs_ref.dtype)


def image(back, theirs, cot, cot_other, weights, at, rows, slots, slot, model):
    tokens, width = cot.shape
    unit = weights[0].shape[0]
    step = min(rows, 256)
    each = rows // step
    wide = pl.BlockSpec((tokens, width), lambda t, at: (0, 0))
    half = pl.BlockSpec((tokens, width // 2), lambda t, at: (0, 0))
    held = [v for v in (back, theirs) if v is not None]
    base = 1 + 1 + 2 + len(weights)
    aliases = {}
    for i, v in enumerate(held):
        aliases[base + i] = 0 if v is back else 1
    return call(
        functools.partial(image_body, len(weights), len(held)),
        (unit // step,),
        at.astype(jnp.int32)[None],
        [
            wide,
            half,
            half,
            *[pl.BlockSpec((step, width), lambda t, at: (t, 0)) for _ in weights],
            *[pl.BlockSpec(memory_space=pl.ANY) for _ in held],
        ],
        [
            pl.BlockSpec(
                (tokens, step), lambda t, at: (0, (t // each * BLOCK + at[0]) * each + t % each)
            ),
            pl.BlockSpec((tokens, step), lambda t, at: (0, slot * (unit // step) + t)),
        ],
        [
            jax.ShapeDtypeStruct((tokens, model), BF16),
            jax.ShapeDtypeStruct((tokens, slots * unit), BF16),
        ],
        [],
        aliases,
        4 * tokens * unit * width,
        (cot, *cot_other, *weights, *held),
    )


def place_body(at_ref, came_ref, held_ref, back_ref):
    del at_ref, held_ref
    back_ref[...] = came_ref[...]


def place(back, came, ats, rows):
    tokens, size = came.shape
    unit = size // len(ats)
    step = rows
    each = unit // step
    return call(
        place_body,
        (size // step,),
        jnp.stack(ats).astype(jnp.int32),
        [
            pl.BlockSpec((tokens, step), lambda t, at: (0, t)),
            pl.BlockSpec(memory_space=pl.ANY),
        ],
        pl.BlockSpec((tokens, step), lambda t, at: (0, t % each * BLOCK + at[t // each])),
        jax.ShapeDtypeStruct(back.shape, back.dtype),
        [],
        {2: 0},
        0,
        (came, back),
    )


class Order:
    def __init__(self):
        self.last = None

    def tie(self, value):
        if self.last is None:
            return value
        return lax.optimization_barrier((value, self.last))[0]

    def start(self, value, pairs, axis="fsdp"):
        return lax.ppermute(self.tie(value), axis, pairs)

    def done(self, value):
        self.last = self.tie(value)
        return self.last


def shards(normed, cotangent, inner_weight, adam_first, adam_second, anchor, outer_moment):
    weight = inner_weight[0]
    tokens, model = normed.shape
    width = cotangent.shape[1]
    n = lax.axis_size("fsdp")
    reps = lax.axis_size("rep")
    outer = n // BLOCK
    rows = model // n
    me = lax.axis_index("fsdp")
    z, y = (me // PAIR) % LINE, me % PAIR
    rep = lax.axis_index("rep")
    core = rep % 2
    quarter = width // reps

    across = [(f, f ^ 1) for f in range(n)]

    def along(hops):
        return [
            ((a * LINE + s) * PAIR + b, (a * LINE + t) * PAIR + b)
            for a in range(outer)
            for s, t in hops
            for b in range(PAIR)
        ]

    ends = along([(0, 1), (1, 0), (2, 3), (3, 2)])
    inward = along([(0, 1), (3, 2)])
    outward = along([(1, 0), (2, 3)])
    centre = along([(1, 2), (2, 1)])
    outer_groups = [[a * BLOCK + k for a in range(outer)] for k in range(BLOCK)]
    swap = {k: [(r, r ^ k) for r in range(reps)] for k in range(1, reps)}

    def columns(zz, yy):
        parts = [
            lax.dynamic_slice(normed, (0, ((a * LINE + zz) * PAIR + yy) * rows), (tokens, rows))
            for a in range(outer)
        ]
        return parts[0] if outer == 1 else jnp.concatenate(parts, axis=1)

    def owned(value, r):
        return lax.dynamic_slice(value, (0, r * quarter), (value.shape[0], quarter))

    order = Order()
    start, done = order.start, order.done
    both = range(2)
    unit = rows * outer

    far, second, near = jnp.where(z < 2, 3, 0), jnp.where(z < 2, 2, 1), z ^ 1

    def column_blocks(zz, yy):
        return [(normed, rows, (a * LINE + zz) * PAIR + yy) for a in range(outer)]

    def chunk_blocks(c):
        return [(cotangent, quarter, q) for q in range(c, reps, 2)]

    state = (adam_first[0], adam_second[0], weight)

    def start_state(k, which):
        r = order.tie(rep ^ k)
        return start(pick([(state[i], quarter, r) for i in which], 0), swap[k], "rep")

    half = weight.astype(BF16)
    if outer > 1:
        half = lax.all_gather(half, "fsdp", axis=0, tiled=True, axis_index_groups=outer_groups)
    w_near = start(half, ends)
    w_mid = start(half, centre)
    cot_other = [
        start(pick(chunk_blocks(0) + column_blocks(far, 1 - y), 1), across), None
    ]
    x_at = 2 * quarter // unit
    first_one = done(start_state(1, (0,)))
    other = order.tie(1 - y)
    cot_other[1] = start(pick(chunk_blocks(1) + column_blocks(second, other), 1), across)
    moments = {2: start_state(2, (0, 1, 2))}

    def partial(zz, x_other, other_at, chunks, came=(), dtype=BF16, split=True):
        own = (normed, zz * PAIR + y) if outer == 1 else (columns(zz, y), 0 * zz)
        return product(
            *own, x_other, other_at, cotangent, cot_other, chunks, quarter, unit, came, dtype,
            split,
        )

    def plus(value, came):
        return (value.astype(F32) + came.astype(F32)).astype(BF16)

    r1, r2a, r3a, r3b = ([None, None] for _ in range(4))
    p_far, p_near = [None, None], [None, None]

    cot_other[0] = done(cot_other[0])
    (p_far[0],) = partial(far, cot_other[0], x_at, (0,))
    r1[0] = start(p_far[0], inward)
    other = order.tie(1 - y)
    x_rest = start(pick(column_blocks(near, other) + column_blocks(z, other), 1), across)
    w_near = done(w_near)
    w_across = start(w_near, centre)
    w_mid = done(w_mid)
    w_out = start(w_mid, outward)
    cot_other[1] = done(cot_other[1])
    (p_far[1],) = partial(far, cot_other[0], x_at, (1,))
    r1[1] = start(p_far[1], inward)
    p_second = partial(second, cot_other[1], x_at, (0, 1), split=False)
    r2b = start(p_second, inward)

    def images(back, theirs, weights, zz, slots, slot):
        return image(
            back, theirs, cotangent, cot_other, weights, order.tie(zz) * PAIR + y, rows,
            slots, slot, model,
        )

    r1[0] = done(r1[0])
    r2a[0] = start(plus(p_far[0], r1[0]), centre)
    back, theirs = images(None, None, (half,), z, 3, 0)
    back, theirs = images(back, theirs, (w_near,), near, 3, 1)
    moments[2] = done(moments[2])
    moments[3] = start_state(3, (0, 1, 2))
    moments[1] = start_state(1, (1, 2))
    r1[1] = done(r1[1])
    r2a[1] = start(plus(p_far[1], r1[1]), centre)
    w_across = done(w_across)
    w_last = start(w_across, outward)
    w_out = done(w_out)
    back, theirs = images(back, theirs, (w_mid, w_out), second, 3, 2)
    came_early = start(theirs, across)
    x_rest = done(x_rest)
    p_own = partial(order.tie(z), x_rest, 1, (0, 1), (), F32)
    r2a[0] = done(r2a[0])
    (p_near[0],) = partial(near, x_rest, 0, (0,), (r2a[0],))
    r3a[0] = start(p_near[0], ends)
    moments[1] = done(moments[1])
    r2b = done(r2b)

    def of_chunk(value, c):
        return [value[:, q * quarter : (q + 1) * quarter] for q in range(c, reps, 2)]

    for c in both:
        sums = [plus(v, came) for v, came in zip(of_chunk(p_second, c), of_chunk(r2b, c))]
        r3b[c] = start(jnp.concatenate(sums, axis=1), centre)
    r2a[1] = done(r2a[1])
    (p_near[1],) = partial(near, x_rest, 0, (1,), (r2a[1],))
    r3a[1] = start(p_near[1], ends)
    w_last = done(w_last)
    back, theirs = images(back, None, (w_across, w_last), far, 1, 0)
    came_late = start(theirs, across)
    moments[3] = done(moments[3])

    def pieces(value):
        return [value[i * rows : (i + 1) * rows] for i in range(value.shape[0] // rows)]

    moments = {
        1: [first_one, *pieces(moments[1])], 2: pieces(moments[2]), 3: pieces(moments[3])
    }
    came_early = done(came_early)
    other_y = [zz * PAIR + 1 - y for zz in (z, near, second)]
    back = done(place(back, came_early, other_y, rows))

    chips = range(reps // 2)
    hops = {
        2: lambda c: [(x * 2 + c, (x ^ 1) * 2 + c) for x in chips],
        3: lambda c: [(x * 2 + 1 - c, (x ^ 1) * 2 + c) for x in chips],
        1: lambda c: [(x * 2 + 1 - c, x * 2 + c) for x in chips],
    }
    squares, sent, own_gradient = [], [], []
    for c in both:
        r3a[c] = done(r3a[c])
        r3b[c] = done(r3b[c])
        total = p_own[c] + r3a[c].astype(F32) + r3b[c].astype(F32)
        if outer > 1:
            total = lax.psum_scatter(
                total.astype(BF16), "fsdp", scatter_dimension=0, tiled=True,
                axis_index_groups=outer_groups,
            ).astype(F32)
        gradient = total / (tokens * n)
        squares.append(jnp.sum(gradient * gradient))
        narrow = gradient.astype(BF16)
        here = owned(narrow, rep // 2)
        there = owned(narrow, 1 - rep // 2)
        sent.append(
            {
                2: start(there, hops[2](c), "rep"),
                3: start(there, hops[3](c), "rep"),
                1: start(here, hops[1](c), "rep"),
            }
        )
        own_gradient.append(owned(narrow, rep // 2))
        if c == 0:
            back = done(place(back, done(came_late), [far * PAIR + 1 - y], rows))

    square = jnp.broadcast_to(squares[0] + squares[1], (reps * n, 128))
    square = lax.all_to_all(order.tie(square), ("rep", "fsdp"), 0, 0, tiled=True)
    square = jnp.sum(square[:, 0].reshape(reps, n), axis=1)
    factors = jnp.minimum(1.0, 1.0 / (jnp.sqrt(square) + 1e-06))

    def update(gradient, first, second_moment, k):
        clipped = gradient.astype(F32) * lax.dynamic_index_in_dim(factors, rep ^ k, 0, False)
        first_new = BETA_ONE * first + (1.0 - BETA_ONE) * clipped
        second_new = BETA_TWO * second_moment + (1.0 - BETA_TWO) * clipped * clipped
        return first_new / (jnp.sqrt(second_new) + ADAM_EPS)

    update_sum = update(
        jnp.where(core == 0, own_gradient[0], own_gradient[1]),
        owned(adam_first[0], rep), owned(adam_second[0], rep), 0,
    )
    weight_sum = owned(weight, rep)
    for k in (1, 2, 3):
        came = [done(sent[c][k]) for c in both]
        first, second_moment, other_weight = moments[k]
        update_sum = update_sum + update(
            jnp.where(core == 0, came[0], came[1]), first, second_moment, k
        )
        weight_sum = weight_sum + other_weight
    updated_sum = (1.0 - RATE_INNER * DECAY) * weight_sum - RATE_INNER * update_sum
    outer_step = anchor - updated_sum / reps
    moment_out = MOMENTUM * outer_moment + outer_step
    synced = (anchor - RATE_OUTER * (outer_step + MOMENTUM * moment_out)).astype(BF16)

    quarters = {0: synced}
    quarters[2] = start(synced, swap[2], "rep")
    quarters[1] = start(synced, swap[1], "rep")
    quarters[1] = done(quarters[1])
    quarters[2] = done(quarters[2])
    quarters[3] = start(quarters[2], swap[1], "rep")
    whole = jnp.zeros((rows, width), F32)
    for k in (0, 1, 2, 3):
        whole = lax.dynamic_update_slice(
            whole, quarters[k].astype(F32), (0, (rep ^ k) * quarter)
        )
    return (back, whole, moment_out)


def solution(mesh):
    placed = (
        P(("rep", "fsdp"), None),
        P(("rep", "fsdp"), None),
        P("rep", "fsdp", None),
        P("rep", "fsdp", None),
        P("rep", "fsdp", None),
        P("fsdp", "rep"),
        P("fsdp", "rep"),
    )
    return jax.shard_map(
        shards,
        mesh=mesh,
        in_specs=placed,
        out_specs=(P(("rep", "fsdp"), None), P("fsdp", None), P("fsdp", "rep")),
        check_vma=False,
    )
```

time: 647 us -> 314 us (0.49)
  waiting for transfers between devices: 559 us -> 94.7 us
  starting transfers between devices: 0.34 us -> 76.5 us
  Pallas kernels: 0 us -> 68.2 us
  local copies, waits for them, and re-layouts: 1.55 us -> 36.7 us
  matrix products: 28.4 us -> 0 us
  blocking collectives: 20.1 us -> 0 us
  between operations: 14.5 us -> 2.3 us
  other arithmetic: 22.5 us -> 34.1 us
    reduce_scatter x2 -> x0, waiting for transfers between devices: 323 us -> none  [the longest x1 285 us: shards(): lax.psum_scatter(lax.dot_general(normed, cotangent, (((0,), (0,)), ((), (...]
    all_gather x2 -> x0, waiting for transfers between devices: 236 us -> none  [the longest x1 227 us: shards(): lax.all_gather(weight_half, 'fsdp', axis=0, tiled=True)]
    ppermute x0 -> x32, waiting for transfers between devices: none -> 83.4 us  [start(): return lax.ppermute(self.tie(value), axis, pairs)]
    ppermute x0 -> x32, starting transfers between devices: none -> 72.1 us  [start(): return lax.ppermute(self.tie(value), axis, pairs)]
    pallas_call x0 -> x19, Pallas kernels: none -> 68.2 us  [call(): pl.pallas_call(body, grid_spec=pltpu.PrefetchScalarGridSpec(num_scalar_pr...]
    unnamed x4 -> x54, local copies, waits for them, and re-layouts: 1.55 us -> 30.8 us
    dot_general x2 -> x0, matrix products: 28.4 us -> none  [the longest x1 14.6 us: shards(): lax.dot_general(normed, cotangent, (((0,), (0,)), ((), ())), preferred_el...]
    psum x1 -> x0, blocking collectives: 20.1 us -> none  [shards(): square_sum = lax.psum(jnp.sum(gradient * gradient), 'fsdp')]
  transfers between devices with their start and end apart: 4 -> 33, of which waited for: 4 -> 8; matrix products, arithmetic and copies ran while one was open for 3% -> 8% of each run, Pallas kernels for 0% -> 22%
where the time goes in v2:
time: 314 us; the launch traced here: 313 us
  waiting for transfers between devices  94.7 us (30%)
  starting transfers between devices  76.5 us (24%)
  Pallas kernels  68.2 us (22%)
  local copies, waits for them, and re-layouts  36.7 us (12%)
  other arithmetic  34.1 us (11%)
    ppermute x32, waiting for transfers between devices, start(): return lax.ppermute(self.tie(value), axis, pairs)  83.4 us
    ppermute x32, starting transfers between devices, start(): return lax.ppermute(self.tie(value), axis, pairs)  72.1 us
    pallas_call x19, Pallas kernels, call(): pl.pallas_call(body, grid_spec=pltpu.PrefetchScalarGridSpec(num_scalar_pr...  68.2 us
    unnamed x54, local copies, waits for them, and re-layouts  30.8 us
    dynamic_update_slice x4, other arithmetic, shards(): lax.dynamic_update_slice(whole, quarters[k].astype(F32), (0, (rep ^ k) *...  13.2 us
    all_to_all x1, waiting for transfers between devices, shards(): lax.all_to_all(order.tie(square), ('rep', 'fsdp'), 0, 0, tiled=True)  11.3 us
    convert_element_type x3, other arithmetic, plus(): return (value.astype(F32) + came.astype(F32)).astype(BF16)  9.28 us
  transfers between devices with their start and end apart: 33, of which 8 were waited for; matrix products, arithmetic and copies ran while one was open for 8% of the time, Pallas kernels for 22%

profile of v2, /device:TPU:0, one launch (start us, length us, event | category | flops | bytes accessed | tf_op | source)
XLA Modules:
  0.0 312.6 jit_solution(8305019670392924138)
XLA Ops:
  6.8 3.0 collective-permute-start
  15.1 3.8 %shard_map.98 = f32[1536,512]{1,0:T(8,128)} custom-call(s32[3]{0:T(128)S(1)} %stack.94.at_ref, f32[512,2048]{1,0:T(8,128)S(1)} %bitcast.56, f32[512,2048]{1,0:T(8,128)S(1)} %bitcast.58, f32[512,2048]{1,0:T(8,128)} %bitcast.52), custom_call_target="tpu_custom_call" | custom-call | bytes 12582912 | tf_op jit(solution)/shard_map/pallas_call | solution.py:34
  30.3 31.8 %collective-permute-done.1.x_other_ref.refs_1_.refs_2_.refs_0_ = bf16[512,1536]{1,0:T(8,128)(2,1)} collective-permute-done((bf16[512,1536]{1,0:T(8,128)(2,1)}, bf16[512,1536]{1,0:T(8,128)(2,1)}, u32[]{:S(2)}, u32[]{:S(2)}) %collective-permute-start.1) | collective-permute-done | bytes 1572896 | tf_op jit(solution)/shard_map/ppermute | solution.py:236
  64.3 3.4 %shard_map.99 = bf16[512,1024]{1,0:T(8,128)(2,1)S(1)} custom-call(s32[2]{0:T(128)S(1)} %get-tuple-element.179.at_ref, bf16[512,4096]{1,0:T(8,128)(2,1)S(1)} %copy-done.2, bf16[512,1536]{1,0:T(8,128)(2,1)} %collective-permute-done.1.x_other_ref.refs_1_.refs_2_.refs_0_, bf16[512,2048]{1,0:T(8,128)(2,1)S(1)} %copy-done, ...), custom_call_target="tpu_custom_call" | custom-call | flops 1073741824 | bytes 4194304 | tf_op jit(solution)/shard_map/pallas_call | solution.py:34
  67.7 3.4 %collective-permute-start.8 = (bf16[512,1024]{1,0:T(8,128)(2,1)S(1)}, bf16[512,1024]{1,0:T(8,128)(2,1)}, u32[]{:S(2)}, u32[]{:S(2)}) collective-permute-start(bf16[512,1024]{1,0:T(8,128)(2,1)S(1)} %shard_map.99), channel_id=1, source_target_pairs={{0,2},{1,3},{6,4},{7,5},{8,10},{9,11},{14,12},{15,13},{16,18},{17,... | collective-permute-start | bytes 3145736 | tf_op jit(solution)/shard_map/ppermute | solution.py:236
  73.1 21.0 %collective-permute-done.4.refs_1_.x_other_ref.refs_3_ = bf16[512,1536]{1,0:T(8,128)(2,1)} collective-permute-done((bf16[512,1536]{1,0:T(8,128)(2,1)}, bf16[512,1536]{1,0:T(8,128)(2,1)}, u32[]{:S(2)}, u32[]{:S(2)}) %collective-permute-start.4) | collective-permute-done | bytes 1572896 | tf_op jit(solution)/shard_map/ppermute | solution.py:236
  95.4 4.2 %shard_map.97 = bf16[512,1024]{1,0:T(8,128)(2,1)} custom-call(s32[2]{0:T(128)S(1)} %get-tuple-element.179.at_ref, bf16[512,4096]{1,0:T(8,128)(2,1)S(1)} %copy-done.2, bf16[512,1536]{1,0:T(8,128)(2,1)} %collective-permute-done.1.x_other_ref.refs_1_.refs_2_.refs_0_, bf16[512,2048]{1,0:T(8,128)(2,1)S(1)} %copy-done, ...), custom_call_target="tpu_custom_call" | custom-call | flops 1073741824 | bytes 4194304 | tf_op jit(solution)/shard_map/pallas_call | solution.py:34
  99.6 6.9 %collective-permute-start.6 = (bf16[512,1024]{1,0:T(8,128)(2,1)}, bf16[512,1024]{1,0:T(8,128)(2,1)}, u32[]{:S(2)}, u32[]{:S(2)}) collective-permute-start(bf16[512,1024]{1,0:T(8,128)(2,1)} %shard_map.97), channel_id=1, source_target_pairs={{0,2},{1,3},{6,4},{7,5},{8,10},{9,11},{14,12},{15,13},{16,18},{17,... | collective-permute-start | bytes 3145736 | tf_op jit(solution)/shard_map/ppermute | solution.py:236
  116.2 5.6 %shard_map.100 = bf16[512,2048]{1,0:T(8,128)(2,1)} custom-call(s32[2]{0:T(128)S(1)} %get-tuple-element.178.at_ref, bf16[512,4096]{1,0:T(8,128)(2,1)S(1)} %copy-done.4, bf16[512,1536]{1,0:T(8,128)(2,1)} %collective-permute-done.4.refs_1_.x_other_ref.refs_3_, bf16[512,2048]{1,0:T(8,128)(2,1)S(1)} %copy-done, bf16[512,2048]{1,0:T(8,128)(2,1)S(1)} %copy-done, ...), custom_call_target="tpu_custom_call" | custom-call | flops 2147483648 | bytes 8388608 | tf_op jit(solution)/shard_map/pallas_call | solution.py:34
  121.9 4.6 %collective-permute-done.6 = bf16[512,1024]{1,0:T(8,128)(2,1)} collective-permute-done((bf16[512,1024]{1,0:T(8,128)(2,1)}, bf16[512,1024]{1,0:T(8,128)(2,1)}, u32[]{:S(2)}, u32[]{:S(2)}) %collective-permute-start.6) | collective-permute-done | bytes 1048608 | tf_op jit(solution)/shard_map/ppermute | solution.py:236
  126.5 5.7 %collective-permute-start.11 = (bf16[512,2048]{1,0:T(8,128)(2,1)}, bf16[512,2048]{1,0:T(8,128)(2,1)}, u32[]{:S(2)}, u32[]{:S(2)}) collective-permute-start(bf16[512,2048]{1,0:T(8,128)(2,1)} %shard_map.100), channel_id=1, source_target_pairs={{0,2},{1,3},{6,4},{7,5},{8,10},{9,11},{14,12},{15,13},{16,18},{17,... | collective-permute-start | bytes 6291464 | tf_op jit(solution)/shard_map/ppermute | solution.py:236
  140.8 3.8 %shard_map.108 = f32[1536,512]{1,0:T(8,128)} custom-call(s32[3]{0:T(128)S(1)} %stack.108.at_ref, f32[512,2048]{1,0:T(8,128)S(1)} %bitcast.57, f32[512,2048]{1,0:T(8,128)S(1)} %bitcast.60, f32[512,2048]{1,0:T(8,128)} %bitcast.53), custom_call_target="tpu_custom_call" | custom-call | bytes 12582912 | tf_op jit(solution)/shard_map/pallas_call | solution.py:34
  144.6 5.3 %shard_map.103 = (bf16[512,4096]{1,0:T(8,128)(2,1)}, bf16[512,1536]{1,0:T(8,128)(2,1)}) custom-call(s32[1]{0:T(128)} %bitcast.15.at_ref, bf16[512,2048]{1,0:T(8,128)(2,1)S(1)} %copy-done, bf16[512,1536]{1,0:T(8,128)(2,1)} %collective-permute-done.1.x_other_ref.refs_1_.refs_2_.refs_0_, bf16[512,1536]{1,0:T(8,128)(2,1)} %collective-permute-done.4.refs_1_.x_other_ref.refs_3_, ...), custom_call_target="tpu_custom_call" | custom-call | flops 2147483648 | bytes 23068672 | tf_op jit(solution)/shard_map/pallas_call | solution.py:34
  151.2 5.4 %shard_map.104 = (bf16[512,4096]{1,0:T(8,128)(2,1)}, bf16[512,1536]{1,0:T(8,128)(2,1)}) custom-call(s32[1]{0:T(128)} %bitcast.14.at_ref, bf16[512,2048]{1,0:T(8,128)(2,1)S(1)} %copy-done, bf16[512,1536]{1,0:T(8,128)(2,1)} %collective-permute-done.1.x_other_ref.refs_1_.refs_2_.refs_0_, ...), custom_call_target="tpu_custom_call", output_to_operand_aliasing={{0}: (5, {}), {1}: (6, {})} | custom-call | flops 2147483648 | bytes 23068672 | tf_op jit(solution)/shard_map/pallas_call | solution.py:34
  156.6 5.7 %shard_map.105 = (bf16[512,4096]{1,0:T(8,128)(2,1)}, bf16[512,1536]{1,0:T(8,128)(2,1)}) custom-call(s32[1]{0:T(128)} %bitcast.13.at_ref, bf16[512,2048]{1,0:T(8,128)(2,1)S(1)} %copy-done, bf16[512,1536]{1,0:T(8,128)(2,1)} %collective-permute-done.1.x_other_ref.refs_1_.refs_2_.refs_0_, ...), custom_call_target="tpu_custom_call", output_to_operand_aliasing={{0}: (6, {}), {1}: (7, {})} | custom-call | flops 2147483648 | bytes 23068672 | tf_op jit(solution)/shard_map/pallas_call | solution.py:34
  163.8 2.9 add_convert_fusion.1
  170.8 4.1 %shard_map.107 = bf16[512,1024]{1,0:T(8,128)(2,1)} custom-call(s32[2]{0:T(128)S(1)} %pad_add_fusion.6.at_ref, bf16[512,4096]{1,0:T(8,128)(2,1)S(1)} %copy-done.5, bf16[512,1024]{1,0:T(8,128)(2,1)S(1)} %collective-permute-done.14.x_other_ref, bf16[512,2048]{1,0:T(8,128)(2,1)S(1)} %copy-done, ...), custom_call_target="tpu_custom_call" | custom-call | flops 1073741824 | bytes 4194304 | tf_op jit(solution)/shard_map/pallas_call | solution.py:34
  174.9 5.8 %collective-permute-start.18 = (bf16[512,1024]{1,0:T(8,128)(2,1)}, bf16[512,1024]{1,0:T(8,128)(2,1)}, u32[]{:S(2)}, u32[]{:S(2)}) collective-permute-start(bf16[512,1024]{1,0:T(8,128)(2,1)} %shard_map.107), channel_id=1, source_target_pairs={{0,2},{1,3},{2,0},{3,1},{4,6},{5,7},{6,4},{7,5},{8,10},{9,11},{10,... | collective-permute-start | bytes 3145736 | tf_op jit(solution)/shard_map/ppermute | solution.py:236
  180.7 3.7 %add_convert_fusion.3 = (bf16[512,512]{1,0:T(8,128)(2,1)}, bf16[512,512]{1,0:T(8,128)(2,1)}, bf16[512,512]{1,0:T(8,128)(2,1)S(1)}, bf16[512,512]{1,0:T(8,128)(2,1)S(1)}) fusion(bf16[512,2048]{1,0:T(8,128)(2,1)} %shard_map.100, bf16[512,2048]{1,0:T(8,128)(2,1)} %collective-permute-done.11), kind=kLoop, calls=%fused_computation.46 | loop fusion | flops 4194304 | bytes 6291456 | tf_op jit(solution)/shard_map/convert_element_type | solution.py:325
  191.7 4.1 %shard_map.112 = bf16[512,1024]{1,0:T(8,128)(2,1)} custom-call(s32[2]{0:T(128)S(1)} %pad_add_fusion.6.at_ref, bf16[512,4096]{1,0:T(8,128)(2,1)S(1)} %copy-done.6, bf16[512,1024]{1,0:T(8,128)(2,1)S(1)} %collective-permute-done.14.x_other_ref, bf16[512,2048]{1,0:T(8,128)(2,1)S(1)} %copy-done, ...), custom_call_target="tpu_custom_call" | custom-call | flops 1073741824 | bytes 4194304 | tf_op jit(solution)/shard_map/pallas_call | solution.py:34
  195.8 3.7 %collective-permute-done.19.came_ref = bf16[512,1536]{1,0:T(8,128)(2,1)} collective-permute-done((bf16[512,1536]{1,0:T(8,128)(2,1)}, bf16[512,1536]{1,0:T(8,128)(2,1)}, u32[]{:S(2)}, u32[]{:S(2)}) %collective-permute-start.19) | collective-permute-done | bytes 1572896 | tf_op jit(solution)/shard_map/ppermute | solution.py:236
  201.4 11.4 %collective-permute-start.21 = (bf16[512,1024]{1,0:T(8,128)(2,1)}, bf16[512,1024]{1,0:T(8,128)(2,1)}, u32[]{:S(2)}, u32[]{:S(2)}) collective-permute-start(bf16[512,1024]{1,0:T(8,128)(2,1)} %shard_map.112), channel_id=1, source_target_pairs={{0,2},{1,3},{2,0},{3,1},{4,6},{5,7},{6,4},{7,5},{8,10},{9,11},{10,... | collective-permute-start | bytes 3145736 | tf_op jit(solution)/shard_map/ppermute | solution.py:236
  213.0 5.6 %shard_map.106 = (bf16[512,4096]{1,0:T(8,128)(2,1)}, bf16[512,512]{1,0:T(8,128)(2,1)}) custom-call(s32[1]{0:T(128)} %bitcast.12.at_ref, bf16[512,2048]{1,0:T(8,128)(2,1)S(1)} %copy-done, bf16[512,1536]{1,0:T(8,128)(2,1)} %collective-permute-done.1.x_other_ref.refs_1_.refs_2_.refs_0_, ...), custom_call_target="tpu_custom_call", output_to_operand_aliasing={{0}: (6, {})} | custom-call | flops 2147483648 | bytes 18874368 | tf_op jit(solution)/shard_map/pallas_call | solution.py:34
  219.2 4.9 %shard_map.111 = (f32[512,1024]{1,0:T(8,128)S(1)}, f32[512,1024]{1,0:T(8,128)S(1)}) custom-call(s32[2]{0:T(128)S(1)} %pad_add_fusion.8.at_ref, bf16[512,4096]{1,0:T(8,128)(2,1)} %x_ref.11, bf16[512,1024]{1,0:T(8,128)(2,1)S(1)} %collective-permute-done.14.x_other_ref, bf16[512,2048]{1,0:T(8,128)(2,1)S(1)} %copy-done, bf16[512,2048]{1,0:T(8,128)(2,1)S(1)} %copy-done, ...), custom_call_target="tpu_custom_call" | custom-call | flops 2147483648 | bytes 16777216 | tf_op jit(solution)/shard_map/pallas_call | solution.py:34
  225.4 3.9 %shard_map.109.held_ref = bf16[512,4096]{1,0:T(8,128)(2,1)} custom-call(s32[3]{0:T(128)S(1)} %pad_add_fusion.7.at_ref, bf16[512,1536]{1,0:T(8,128)(2,1)} %collective-permute-done.19.came_ref, bf16[512,4096]{1,0:T(8,128)(2,1)} %get-tuple-element.131.held_ref), custom_call_target="tpu_custom_call", output_to_operand_aliasing={{}: (2, {})} | custom-call | bytes 16777216 | tf_op jit(solution)/shard_map/pallas_call | solution.py:34
  229.4 2.9 fusion.25
  236.5 8.7 %collective-permute-done.21 = bf16[512,1024]{1,0:T(8,128)(2,1)} collective-permute-done((bf16[512,1024]{1,0:T(8,128)(2,1)}, bf16[512,1024]{1,0:T(8,128)(2,1)}, u32[]{:S(2)}, u32[]{:S(2)}) %collective-permute-start.21) | collective-permute-done | bytes 1048608 | tf_op jit(solution)/shard_map/ppermute | solution.py:236
  255.5 5.8 %collective-permute-start.28 = (bf16[512,512]{1,0:T(8,128)(2,1)}, bf16[512,512]{1,0:T(8,128)(2,1)}, u32[]{:S(2)}, u32[]{:S(2)}) collective-permute-start(bf16[512,512]{1,0:T(8,128)(2,1)} %get-tuple-element.151), channel_id=1, source_target_pairs={{0,24},{16,8},{1,25},{17,9},{2,26},{18,10},{3,27},{19,11},{4,28},{... | collective-permute-start | bytes 1572872 | tf_op jit(solution)/shard_map/ppermute | solution.py:236
  263.3 4.4 %all-to-all-start = ((f32[32,1,128]{2,1,0:T(1,128)}), f32[32,1,128]{2,1,0:T(1,128)S(1)}, u32[]{:S(2)}, u32[]{:S(2)}) async-start(f32[32,1,128]{2,1,0:T(1,128)} %bitcast.23), calls=%async_computation | async-start | bytes 32768 | tf_op jit(solution)/shard_map/all_to_all | solution.py:430
  267.7 11.3 %all-to-all-done = f32[32,1,128]{2,1,0:T(1,128)S(1)} async-done(((f32[32,1,128]{2,1,0:T(1,128)}), f32[32,1,128]{2,1,0:T(1,128)S(1)}, u32[]{:S(2)}, u32[]{:S(2)}) %all-to-all-start) | async-done | bytes 16416 | tf_op jit(solution)/shard_map/all_to_all | solution.py:430
  284.7 9.9 %convert_dynamic-update-slice_fusion.3 = (f32[512,2048]{1,0:T(8,128)}, bf16[512,512]{1,0:T(8,128)(2,1)}, f32[512,512]{1,0:T(8,128)}) fusion(f32[512,2048]{1,0:T(8,128)} %broadcast_in_dim.22, s32[]{:T(128)S(6)} %select_n.97, f32[512,512]{1,0:T(8,128)S(1)} %copy-done.19, f32[512,512]{1,0:T(8,128)S(1)} %copy-done.20, f32[1536,512]{1,0:T(8,128)} %collective-permute-done.20, ...), kind=kLoop, calls=%fused_computation.42 | loop fusion | flops 17563648 | bytes 21497860 | tf_op jit(solution)/shard_map/dynamic_update_slice | solution.py:465
  296.8 12.4 %collective-permute-done.30 = bf16[512,512]{1,0:T(8,128)(2,1)S(1)} collective-permute-done((bf16[512,512]{1,0:T(8,128)(2,1)}, bf16[512,512]{1,0:T(8,128)(2,1)S(1)}, u32[]{:S(2)}, u32[]{:S(2)}) %collective-permute-start.30) | collective-permute-done | bytes 524320 | tf_op jit(solution)/shard_map/ppermute | solution.py:236
  (137 shorter events, 90.9 us)
Async XLA Ops:
  2.9 6.9 %collective-permute-start.2 = (f32[512,512]{1,0:T(8,128)S(1)}, f32[512,512]{1,0:T(8,128)S(1)}, u32[]{:S(2)}, u32[]{:S(2)}) collective-permute-start(f32[512,512]{1,0:T(8,128)S(1)} %shard_map.95), channel_id=1, source_target_pairs={{0,8},{8,0},{16,24},{24,16},{1,9},{9,1},{17,25},{25,17},{2,10},{10... | collective-permute-start | bytes 3145736 | tf_op jit(solution)/shard_map/ppermute | solution.py:236
  6.8 64.4 %collective-permute-start = (bf16[512,2048]{1,0:T(8,128)(2,1)}, bf16[512,2048]{1,0:T(8,128)(2,1)}, u32[]{:S(2)}, u32[]{:S(2)}) collective-permute-start(bf16[512,2048]{1,0:T(8,128)(2,1)} %bitcast_convert_fusion.refs_2_), channel_id=1, source_target_pairs={{0,2},{1,3},{2,0},{3,1},{4,6},{5,7},{6,4},{7,5},{8,10},{9,11},{10,... | collective-permute-start | bytes 6291464 | tf_op jit(solution)/shard_map/ppermute | solution.py:236
  18.9 92.1 %collective-permute-start.7 = (f32[1536,512]{1,0:T(8,128)}, f32[1536,512]{1,0:T(8,128)}, u32[]{:S(2)}, u32[]{:S(2)}) collective-permute-start(f32[1536,512]{1,0:T(8,128)} %shard_map.98), channel_id=1, source_target_pairs={{0,16},{8,24},{16,0},{24,8},{1,17},{9,25},{17,1},{25,9},{2,18},{10... | collective-permute-start | bytes 9437192 | tf_op jit(solution)/shard_map/ppermute | solution.py:236
  24.5 37.7 %collective-permute-start.1 = (bf16[512,1536]{1,0:T(8,128)(2,1)}, bf16[512,1536]{1,0:T(8,128)(2,1)}, u32[]{:S(2)}, u32[]{:S(2)}) collective-permute-start(bf16[512,1536]{1,0:T(8,128)(2,1)} %shard_map.94), channel_id=1, source_target_pairs={{0,1},{1,0},{2,3},{3,2},{4,5},{5,4},{6,7},{7,6},{8,9},{9,8},{10,11... | collective-permute-start | bytes 4718600 | tf_op jit(solution)/shard_map/ppermute | solution.py:236
  26.0 47.1 %collective-permute-start.5 = (bf16[512,2048]{1,0:T(8,128)(2,1)}, bf16[512,2048]{1,0:T(8,128)(2,1)}, u32[]{:S(2)}, u32[]{:S(2)}) collective-permute-start(bf16[512,2048]{1,0:T(8,128)(2,1)} %bitcast_convert_fusion.refs_2_), channel_id=1, source_target_pairs={{2,4},{3,5},{4,2},{5,3},{10,12},{11,13},{12,10},{13,11},{18,20},{1... | collective-permute-start | bytes 6291464 | tf_op jit(solution)/shard_map/ppermute | solution.py:236
  29.8 64.3 %collective-permute-start.4 = (bf16[512,1536]{1,0:T(8,128)(2,1)}, bf16[512,1536]{1,0:T(8,128)(2,1)}, u32[]{:S(2)}, u32[]{:S(2)}) collective-permute-start(bf16[512,1536]{1,0:T(8,128)(2,1)} %shard_map.96), channel_id=1, source_target_pairs={{0,1},{1,0},{2,3},{3,2},{4,5},{5,4},{6,7},{7,6},{8,9},{9,8},{10,11... | collective-permute-start | bytes 4718600 | tf_op jit(solution)/shard_map/ppermute | solution.py:236
  67.7 41.7 %collective-permute-start.8 = (bf16[512,1024]{1,0:T(8,128)(2,1)S(1)}, bf16[512,1024]{1,0:T(8,128)(2,1)}, u32[]{:S(2)}, u32[]{:S(2)}) collective-permute-start(bf16[512,1024]{1,0:T(8,128)(2,1)S(1)} %shard_map.99), channel_id=1, source_target_pairs={{0,2},{1,3},{6,4},{7,5},{8,10},{9,11},{14,12},{15,13},{16,18},{17,... | collective-permute-start | bytes 3145736 | tf_op jit(solution)/shard_map/ppermute | solution.py:236
  71.1 73.4 %collective-permute-start.3 = (bf16[512,2048]{1,0:T(8,128)(2,1)}, bf16[512,2048]{1,0:T(8,128)(2,1)}, u32[]{:S(2)}, u32[]{:S(2)}) collective-permute-start(bf16[512,2048]{1,0:T(8,128)(2,1)} %collective-permute-done.refs_2_), channel_id=1, source_target_pairs={{2,4},{3,5},{4,2},{5,3},{10,12},{11,13},{12,10},{13,11},{18,20},{1... | collective-permute-start | bytes 6291464 | tf_op jit(solution)/shard_map/ppermute | solution.py:236
  94.1 55.8 %collective-permute-start.15 = (bf16[512,2048]{1,0:T(8,128)(2,1)}, bf16[512,2048]{1,0:T(8,128)(2,1)}, u32[]{:S(2)}, u32[]{:S(2)}) collective-permute-start(bf16[512,2048]{1,0:T(8,128)(2,1)} %collective-permute-done.5.refs_2_), channel_id=1, source_target_pairs={{2,0},{3,1},{4,6},{5,7},{10,8},{11,9},{12,14},{13,15},{18,16},{19,... | collective-permute-start | bytes 6291464 | tf_op jit(solution)/shard_map/ppermute | solution.py:236
  99.6 26.9 %collective-permute-start.6 = (bf16[512,1024]{1,0:T(8,128)(2,1)}, bf16[512,1024]{1,0:T(8,128)(2,1)}, u32[]{:S(2)}, u32[]{:S(2)}) collective-permute-start(bf16[512,1024]{1,0:T(8,128)(2,1)} %shard_map.97), channel_id=1, source_target_pairs={{0,2},{1,3},{6,4},{7,5},{8,10},{9,11},{14,12},{15,13},{16,18},{17,... | collective-permute-start | bytes 3145736 | tf_op jit(solution)/shard_map/ppermute | solution.py:236
  109.4 25.4 %collective-permute-start.14 = (bf16[512,1024]{1,0:T(8,128)(2,1)S(1)}, bf16[512,1024]{1,0:T(8,128)(2,1)S(1)}, u32[]{:S(2)}, u32[]{:S(2)}) collective-permute-start(bf16[512,1024]{1,0:T(8,128)(2,1)S(1)} %shard_map.102), channel_id=1, source_target_pairs={{0,1},{1,0},{2,3},{3,2},{4,5},{5,4},{6,7},{7,6},{8,9},{9,8},{10,11... | collective-permute-start | bytes 3145736 | tf_op jit(solution)/shard_map/ppermute | solution.py:236
  115.3 51.4 %collective-permute-start.12 = (f32[1024,512]{1,0:T(8,128)}, f32[1024,512]{1,0:T(8,128)}, u32[]{:S(2)}, u32[]{:S(2)}) collective-permute-start(f32[1024,512]{1,0:T(8,128)} %shard_map.101), channel_id=1, source_target_pairs={{0,8},{8,0},{16,24},{24,16},{1,9},{9,1},{17,25},{25,17},{2,10},{10... | collective-permute-start | bytes 6291464 | tf_op jit(solution)/shard_map/ppermute | solution.py:236
  126.5 48.5 %collective-permute-start.11 = (bf16[512,2048]{1,0:T(8,128)(2,1)}, bf16[512,2048]{1,0:T(8,128)(2,1)}, u32[]{:S(2)}, u32[]{:S(2)}) collective-permute-start(bf16[512,2048]{1,0:T(8,128)(2,1)} %shard_map.100), channel_id=1, source_target_pairs={{0,2},{1,3},{6,4},{7,5},{8,10},{9,11},{14,12},{15,13},{16,18},{17,... | collective-permute-start | bytes 6291464 | tf_op jit(solution)/shard_map/ppermute | solution.py:236
  134.8 27.5 %collective-permute-start.13 = (bf16[512,1024]{1,0:T(8,128)(2,1)}, bf16[512,1024]{1,0:T(8,128)(2,1)}, u32[]{:S(2)}, u32[]{:S(2)}) collective-permute-start(bf16[512,1024]{1,0:T(8,128)(2,1)} %add_convert_fusion), channel_id=1, source_target_pairs={{2,4},{3,5},{4,2},{5,3},{10,12},{11,13},{12,10},{13,11},{18,20},{1... | collective-permute-start | bytes 3145736 | tf_op jit(solution)/shard_map/ppermute | solution.py:236
  144.6 74.1 %collective-permute-start.20 = (f32[1536,512]{1,0:T(8,128)}, f32[1536,512]{1,0:T(8,128)}, u32[]{:S(2)}, u32[]{:S(2)}) collective-permute-start(f32[1536,512]{1,0:T(8,128)} %shard_map.108), channel_id=1, source_target_pairs={{0,24},{8,16},{16,8},{24,0},{1,25},{9,17},{17,9},{25,1},{2,26},{10... | collective-permute-start | bytes 9437192 | tf_op jit(solution)/shard_map/ppermute | solution.py:236
  149.9 51.5 %collective-permute-start.9 = (bf16[512,2048]{1,0:T(8,128)(2,1)}, bf16[512,2048]{1,0:T(8,128)(2,1)}, u32[]{:S(2)}, u32[]{:S(2)}) collective-permute-start(bf16[512,2048]{1,0:T(8,128)(2,1)} %collective-permute-done.3.refs_2_), channel_id=1, source_target_pairs={{2,0},{3,1},{4,6},{5,7},{10,8},{11,9},{12,14},{13,15},{18,16},{19,... | collective-permute-start | bytes 6291464 | tf_op jit(solution)/shard_map/ppermute | solution.py:236
  162.3 37.3 %collective-permute-start.19 = (bf16[512,1536]{1,0:T(8,128)(2,1)}, bf16[512,1536]{1,0:T(8,128)(2,1)}, u32[]{:S(2)}, u32[]{:S(2)}) collective-permute-start(bf16[512,1536]{1,0:T(8,128)(2,1)} %get-tuple-element.126), channel_id=1, source_target_pairs={{0,1},{1,0},{2,3},{3,2},{4,5},{5,4},{6,7},{7,6},{8,9},{9,8},{10,11... | collective-permute-start | bytes 4718600 | tf_op jit(solution)/shard_map/ppermute | solution.py:236
  166.8 18.7 %collective-permute-start.10 = (bf16[512,1024]{1,0:T(8,128)(2,1)}, bf16[512,1024]{1,0:T(8,128)(2,1)}, u32[]{:S(2)}, u32[]{:S(2)}) collective-permute-start(bf16[512,1024]{1,0:T(8,128)(2,1)} %add_convert_fusion.1), channel_id=1, source_target_pairs={{2,4},{3,5},{4,2},{5,3},{10,12},{11,13},{12,10},{13,11},{18,20},{1... | collective-permute-start | bytes 3145736 | tf_op jit(solution)/shard_map/ppermute | solution.py:236
  174.9 54.4 %collective-permute-start.18 = (bf16[512,1024]{1,0:T(8,128)(2,1)}, bf16[512,1024]{1,0:T(8,128)(2,1)}, u32[]{:S(2)}, u32[]{:S(2)}) collective-permute-start(bf16[512,1024]{1,0:T(8,128)(2,1)} %shard_map.107), channel_id=1, source_target_pairs={{0,2},{1,3},{2,0},{3,1},{4,6},{5,7},{6,4},{7,5},{8,10},{9,11},{10,... | collective-permute-start | bytes 3145736 | tf_op jit(solution)/shard_map/ppermute | solution.py:236
  185.5 43.8 %collective-permute-start.17 = (bf16[512,1024]{1,0:T(8,128)(2,1)}, bf16[512,1024]{1,0:T(8,128)(2,1)}, u32[]{:S(2)}, u32[]{:S(2)}) collective-permute-start(bf16[512,1024]{1,0:T(8,128)(2,1)} %pad_maximum_fusion), channel_id=1, source_target_pairs={{2,4},{3,5},{4,2},{5,3},{10,12},{11,13},{12,10},{13,11},{18,20},{1... | collective-permute-start | bytes 3145736 | tf_op jit(solution)/shard_map/ppermute | solution.py:236
  199.6 45.7 %collective-permute-start.22 = (bf16[512,1024]{1,0:T(8,128)(2,1)}, bf16[512,1024]{1,0:T(8,128)(2,1)}, u32[]{:S(2)}, u32[]{:S(2)}) collective-permute-start(bf16[512,1024]{1,0:T(8,128)(2,1)} %pad_maximum_fusion.1), channel_id=1, source_target_pairs={{2,4},{3,5},{4,2},{5,3},{10,12},{11,13},{12,10},{13,11},{18,20},{1... | collective-permute-start | bytes 3145736 | tf_op jit(solution)/shard_map/ppermute | solution.py:236
  201.4 43.8 %collective-permute-start.21 = (bf16[512,1024]{1,0:T(8,128)(2,1)}, bf16[512,1024]{1,0:T(8,128)(2,1)}, u32[]{:S(2)}, u32[]{:S(2)}) collective-permute-start(bf16[512,1024]{1,0:T(8,128)(2,1)} %shard_map.112), channel_id=1, source_target_pairs={{0,2},{1,3},{2,0},{3,1},{4,6},{5,7},{6,4},{7,5},{8,10},{9,11},{10,... | collective-permute-start | bytes 3145736 | tf_op jit(solution)/shard_map/ppermute | solution.py:236
  218.6 15.8 %collective-permute-start.16 = (bf16[512,512]{1,0:T(8,128)(2,1)}, bf16[512,512]{1,0:T(8,128)(2,1)}, u32[]{:S(2)}, u32[]{:S(2)}) collective-permute-start(bf16[512,512]{1,0:T(8,128)(2,1)} %get-tuple-element.122), channel_id=1, source_target_pairs={{0,1},{1,0},{2,3},{3,2},{4,5},{5,4},{6,7},{7,6},{8,9},{9,8},{10,11... | collective-permute-start | bytes 1572872 | tf_op jit(solution)/shard_map/ppermute | solution.py:236
  233.1 22.4 %collective-permute-start.23 = (bf16[512,512]{1,0:T(8,128)(2,1)S(1)}, bf16[512,512]{1,0:T(8,128)(2,1)S(1)}, u32[]{:S(2)}, u32[]{:S(2)}) collective-permute-start(bf16[512,512]{1,0:T(8,128)(2,1)S(1)} %get-tuple-element.145), channel_id=1, source_target_pairs={{8,0},{24,16},{9,1},{25,17},{10,2},{26,18},{11,3},{27,19},{12,4},{... | collective-permute-start | bytes 1572872 | tf_op jit(solution)/shard_map/ppermute | solution.py:236
  248.9 31.1 %collective-permute-start.24 = (bf16[512,512]{1,0:T(8,128)(2,1)S(1)}, bf16[512,512]{1,0:T(8,128)(2,1)S(1)}, u32[]{:S(2)}, u32[]{:S(2)}) collective-permute-start(bf16[512,512]{1,0:T(8,128)(2,1)S(1)} %get-tuple-element.147), channel_id=1, source_target_pairs={{0,8},{16,24},{1,9},{17,25},{2,10},{18,26},{3,11},{19,27},{4,12},{... | collective-permute-start | bytes 1572872 | tf_op jit(solution)/shard_map/ppermute | solution.py:236
  250.7 29.3 %collective-permute-start.25 = (bf16[512,512]{1,0:T(8,128)(2,1)}, bf16[512,512]{1,0:T(8,128)(2,1)S(1)}, u32[]{:S(2)}, u32[]{:S(2)}) collective-permute-start(bf16[512,512]{1,0:T(8,128)(2,1)} %get-tuple-element.149), channel_id=1, source_target_pairs={{0,16},{16,0},{1,17},{17,1},{2,18},{18,2},{3,19},{19,3},{4,20},{20... | collective-permute-start | bytes 1572872 | tf_op jit(solution)/shard_map/ppermute | solution.py:236
  253.5 26.6 %collective-permute-start.26 = (bf16[512,512]{1,0:T(8,128)(2,1)}, bf16[512,512]{1,0:T(8,128)(2,1)S(1)}, u32[]{:S(2)}, u32[]{:S(2)}) collective-permute-start(bf16[512,512]{1,0:T(8,128)(2,1)} %get-tuple-element.151), channel_id=1, source_target_pairs={{8,24},{24,8},{9,25},{25,9},{10,26},{26,10},{11,27},{27,11},{12,28... | collective-permute-start | bytes 1572872 | tf_op jit(solution)/shard_map/ppermute | solution.py:236
  254.2 25.9 %collective-permute-start.27 = (bf16[512,512]{1,0:T(8,128)(2,1)}, bf16[512,512]{1,0:T(8,128)(2,1)}, u32[]{:S(2)}, u32[]{:S(2)}) collective-permute-start(bf16[512,512]{1,0:T(8,128)(2,1)} %get-tuple-element.149), channel_id=1, source_target_pairs={{8,16},{24,0},{9,17},{25,1},{10,18},{26,2},{11,19},{27,3},{12,20},... | collective-permute-start | bytes 1572872 | tf_op jit(solution)/shard_map/ppermute | solution.py:236
  255.5 24.6 %collective-permute-start.28 = (bf16[512,512]{1,0:T(8,128)(2,1)}, bf16[512,512]{1,0:T(8,128)(2,1)}, u32[]{:S(2)}, u32[]{:S(2)}) collective-permute-start(bf16[512,512]{1,0:T(8,128)(2,1)} %get-tuple-element.151), channel_id=1, source_target_pairs={{0,24},{16,8},{1,25},{17,9},{2,26},{18,10},{3,27},{19,11},{4,28},{... | collective-permute-start | bytes 1572872 | tf_op jit(solution)/shard_map/ppermute | solution.py:236
  263.3 15.8 %all-to-all-start = ((f32[32,1,128]{2,1,0:T(1,128)}), f32[32,1,128]{2,1,0:T(1,128)S(1)}, u32[]{:S(2)}, u32[]{:S(2)}) async-start(f32[32,1,128]{2,1,0:T(1,128)} %bitcast.23), calls=%async_computation | async-start | bytes 32768 | tf_op jit(solution)/shard_map/all_to_all | solution.py:430
  294.7 14.6 %collective-permute-start.30 = (bf16[512,512]{1,0:T(8,128)(2,1)}, bf16[512,512]{1,0:T(8,128)(2,1)S(1)}, u32[]{:S(2)}, u32[]{:S(2)}) collective-permute-start(bf16[512,512]{1,0:T(8,128)(2,1)} %get-tuple-element.155), channel_id=1, source_target_pairs={{0,16},{8,24},{16,0},{24,8},{1,17},{9,25},{17,1},{25,9},{2,18},{10... | collective-permute-start | bytes 1572872 | tf_op jit(solution)/shard_map/ppermute | solution.py:236
  309.3 2.2 collective-permute-start.31
  (28 other events, 116.9 us)

commit v3 on v2

--- a/solution.py
+++ b/solution.py
@@ -22,7 +22,7 @@
 F32 = jnp.float32
 
 
-VMEM_BYTES = 40 * 1024 * 1024
+VMEM_BYTES = 60 * 1024 * 1024
 
 
 def dot(a, b, dims):
@@ -133,66 +133,81 @@
     )
 
 
-def image_body(pieces, held, at_ref, c_ref, *refs):
+def image_body(groups, steps, held, at_ref, c_ref, *refs):
     del at_ref
     others, refs = refs[:2], refs[2:]
-    weights, refs = refs[:pieces], refs[pieces:]
+    weights, refs = refs[: sum(groups)], refs[sum(groups) :]
     back_ref, theirs_ref = refs[held:]
-    w = weights[0][...]
-    for ref in weights[1:]:
-        w = w + ref[...]
-    quarter = others[0].shape[1] // 2
-    back_ref[...] = dot(c_ref[...], w, ((1,), (1,))).astype(back_ref.dtype)
-    value = None
-    for c, ref in enumerate(others):
-        for h in range(2):
-            q = c + 2 * h
-            term = dot(
-                ref[:, h * quarter : (h + 1) * quarter],
-                w[:, q * quarter : (q + 1) * quarter],
-                ((1,), (1,)),
-            )
-            value = term if value is None else value + term
-    theirs_ref[...] = value.astype(theirs_ref.dtype)
-
-
-def image(back, theirs, cot, cot_other, weights, at, rows, slots, slot, model):
+    quarter = c_ref.shape[1] // 4
+
+    def multiply(refs):
+        w = refs[0][...]
+        for ref in refs[1:]:
+            w = w + ref[...]
+        back_ref[...] = dot(c_ref[...], w, ((1,), (1,))).astype(back_ref.dtype)
+        value = None
+        for c, ref in enumerate(others):
+            for h in range(2):
+                q = c + 2 * h
+                term = dot(
+                    ref[:, h * quarter : (h + 1) * quarter],
+                    w[:, q * quarter : (q + 1) * quarter],
+                    ((1,), (1,)),
+                )
+                value = term if value is None else value + term
+        theirs_ref[...] = value.astype(theirs_ref.dtype)
+
+    offset = 0
+    for g, size in enumerate(groups):
+        pl.when(pl.program_id(0) // steps == g)(
+            functools.partial(multiply, weights[offset : offset + size])
+        )
+        offset += size
+
+
+def image(back, cot, cot_other, groups, ats, rows, model):
     tokens, width = cot.shape
-    unit = weights[0].shape[0]
+    unit = groups[0][0].shape[0]
     step = min(rows, 256)
     each = rows // step
-    wide = pl.BlockSpec((tokens, width), lambda t, at: (0, 0))
+    steps = unit // step
     half = pl.BlockSpec((tokens, width // 2), lambda t, at: (0, 0))
-    held = [v for v in (back, theirs) if v is not None]
-    base = 1 + 1 + 2 + len(weights)
-    aliases = {}
-    for i, v in enumerate(held):
-        aliases[base + i] = 0 if v is back else 1
+    held = [] if back is None else [back]
+    flat = [w for group in groups for w in group]
+
+    def weight_spec(g):
+        return pl.BlockSpec(
+            (step, width), lambda t, at: (jnp.clip(t - g * steps, 0, steps - 1), 0)
+        )
+
     return call(
-        functools.partial(image_body, len(weights), len(held)),
-        (unit // step,),
-        at.astype(jnp.int32)[None],
-        [
-            wide,
+        functools.partial(image_body, [len(g) for g in groups], steps, len(held)),
+        (len(groups) * steps,),
+        jnp.stack(ats).astype(jnp.int32),
+        [
+            pl.BlockSpec((tokens, width), lambda t, at: (0, 0)),
             half,
             half,
-            *[pl.BlockSpec((step, width), lambda t, at: (t, 0)) for _ in weights],
+            *[weight_spec(g) for g, group in enumerate(groups) for _ in group],
             *[pl.BlockSpec(memory_space=pl.ANY) for _ in held],
         ],
         [
             pl.BlockSpec(
-                (tokens, step), lambda t, at: (0, (t // each * BLOCK + at[0]) * each + t % each)
+                (tokens, step),
+                lambda t, at: (
+                    0, (t % steps // each * BLOCK + at[t // steps]) * each + t % each
+                ),
             ),
-            pl.BlockSpec((tokens, step), lambda t, at: (0, slot * (unit // step) + t)),
+            pl.BlockSpec((tokens, step), lambda t, at: (0, t)),
         ],
         [
             jax.ShapeDtypeStruct((tokens, model), BF16),
-            jax.ShapeDtypeStruct((tokens, slots * unit), BF16),
+            jax.ShapeDtypeStruct((tokens, len(groups) * unit), BF16),
         ],
         [],
-        aliases,
-        4 * tokens * unit * width,
-        (cot, *cot_other, *weights, *held),
+        {4 + len(flat): 0} if held else {},
+        4 * tokens * unit * width * len(groups),
+        (cot, *cot_other, *flat, *held),
     )
 
 
@@ -233,7 +248,8 @@
         return lax.optimization_barrier((value, self.last))[0]
 
     def start(self, value, pairs, axis="fsdp"):
-        return lax.ppermute(self.tie(value), axis, pairs)
+        self.last = self.tie(value)
+        return lax.ppermute(self.last, axis, pairs)
 
     def done(self, value):
         self.last = self.tie(value)
@@ -294,25 +310,28 @@
     def chunk_blocks(c):
         return [(cotangent, quarter, q) for q in range(c, reps, 2)]
 
-    state = (adam_first[0], adam_second[0], weight)
-
-    def start_state(k, which):
-        r = order.tie(rep ^ k)
-        return start(pick([(state[i], quarter, r) for i in which], 0), swap[k], "rep")
-
     half = weight.astype(BF16)
     if outer > 1:
         half = lax.all_gather(half, "fsdp", axis=0, tiled=True, axis_index_groups=outer_groups)
-    w_near = start(half, ends)
-    w_mid = start(half, centre)
-    cot_other = [
-        start(pick(chunk_blocks(0) + column_blocks(far, 1 - y), 1), across), None
-    ]
+    w_near = lax.ppermute(half, "fsdp", ends)
+    w_mid = lax.ppermute(half, "fsdp", centre)
+    early = pick(chunk_blocks(0) + column_blocks(far, 1 - y), 1)
+    cot_other = [lax.ppermute(early, "fsdp", across), None]
     x_at = 2 * quarter // unit
-    first_one = done(start_state(1, (0,)))
+
+    chip_at = rep // 2
+    order.last = (half, early)
+    mate = order.tie(1 - core)
+    blocks = [(weight, quarter, 2 * x + mate) for x in range(reps // 2)]
+    w_mate = done(lax.ppermute(pick(blocks, 1), "rep", swap[1]))
     other = order.tie(1 - y)
-    cot_other[1] = start(pick(chunk_blocks(1) + column_blocks(second, other), 1), across)
-    moments = {2: start_state(2, (0, 1, 2))}
+    cot_other[1] = lax.ppermute(
+        pick(chunk_blocks(1) + column_blocks(second, other), 1), "fsdp", across
+    )
+    w_chip, w_there = (
+        owned(weight, 2 * x + core) + owned(w_mate, x) for x in (chip_at, 1 - chip_at)
+    )
+    w_x = lax.ppermute(w_there, "rep", swap[2])
 
     def partial(zz, x_other, other_at, chunks, came=(), dtype=BF16, split=True):
         own = (normed, zz * PAIR + y) if outer == 1 else (columns(zz, y), 0 * zz)
@@ -327,47 +346,42 @@
     r1, r2a, r3a, r3b = ([None, None] for _ in range(4))
     p_far, p_near = [None, None], [None, None]
 
+    def images(back, groups, blocks):
+        ats = [order.tie(zz) * PAIR + y for zz in blocks]
+        return image(back, cotangent, cot_other, groups, ats, rows, model)
+
     cot_other[0] = done(cot_other[0])
     (p_far[0],) = partial(far, cot_other[0], x_at, (0,))
     r1[0] = start(p_far[0], inward)
-    other = order.tie(1 - y)
-    x_rest = start(pick(column_blocks(near, other) + column_blocks(z, other), 1), across)
     w_near = done(w_near)
+    w_x = done(w_x)
     w_across = start(w_near, centre)
     w_mid = done(w_mid)
     w_out = start(w_mid, outward)
+    other = order.tie(1 - y)
+    x_rest = start(pick(column_blocks(near, other) + column_blocks(z, other), 1), across)
     cot_other[1] = done(cot_other[1])
     (p_far[1],) = partial(far, cot_other[0], x_at, (1,))
     r1[1] = start(p_far[1], inward)
-    p_second = partial(second, cot_other[1], x_at, (0, 1), split=False)
-    r2b = start(p_second, inward)
-
-    def images(back, theirs, weights, zz, slots, slot):
-        return image(
-            back, theirs, cotangent, cot_other, weights, order.tie(zz) * PAIR + y, rows,
-            slots, slot, model,
-        )
-
     r1[0] = done(r1[0])
     r2a[0] = start(plus(p_far[0], r1[0]), centre)
-    back, theirs = images(None, None, (half,), z, 3, 0)
-    back, theirs = images(back, theirs, (w_near,), near, 3, 1)
-    moments[2] = done(moments[2])
-    moments[3] = start_state(3, (0, 1, 2))
-    moments[1] = start_state(1, (1, 2))
+    p_second = partial(order.tie(second), cot_other[1], x_at, (0, 1), split=False)
+    r2b = start(p_second, inward)
     r1[1] = done(r1[1])
     r2a[1] = start(plus(p_far[1], r1[1]), centre)
     w_across = done(w_across)
     w_last = start(w_across, outward)
     w_out = done(w_out)
-    back, theirs = images(back, theirs, (w_mid, w_out), second, 3, 2)
+
+    back, theirs = images(
+        None, ((half,), (w_near,), (w_mid, w_out)), (z, near, second)
+    )
     came_early = start(theirs, across)
     x_rest = done(x_rest)
-    p_own = partial(order.tie(z), x_rest, 1, (0, 1), (), F32)
     r2a[0] = done(r2a[0])
     (p_near[0],) = partial(near, x_rest, 0, (0,), (r2a[0],))
     r3a[0] = start(p_near[0], ends)
-    moments[1] = done(moments[1])
+    p_own = partial(order.tie(z), x_rest, 1, (0, 1), (), F32)
     r2b = done(r2b)
 
     def of_chunk(value, c):
@@ -380,27 +394,13 @@
     (p_near[1],) = partial(near, x_rest, 0, (1,), (r2a[1],))
     r3a[1] = start(p_near[1], ends)
     w_last = done(w_last)
-    back, theirs = images(back, None, (w_across, w_last), far, 1, 0)
+    back, theirs = images(back, ((w_across, w_last),), (far,))
     came_late = start(theirs, across)
-    moments[3] = done(moments[3])
-
-    def pieces(value):
-        return [value[i * rows : (i + 1) * rows] for i in range(value.shape[0] // rows)]
-
-    moments = {
-        1: [first_one, *pieces(moments[1])], 2: pieces(moments[2]), 3: pieces(moments[3])
-    }
     came_early = done(came_early)
     other_y = [zz * PAIR + 1 - y for zz in (z, near, second)]
     back = done(place(back, came_early, other_y, rows))
 
-    chips = range(reps // 2)
-    hops = {
-        2: lambda c: [(x * 2 + c, (x ^ 1) * 2 + c) for x in chips],
-        3: lambda c: [(x * 2 + 1 - c, (x ^ 1) * 2 + c) for x in chips],
-        1: lambda c: [(x * 2 + 1 - c, x * 2 + c) for x in chips],
-    }
-    squares, sent, own_gradient = [], [], []
+    squares, gradient = [], []
     for c in both:
         r3a[c] = done(r3a[c])
         r3b[c] = done(r3b[c])
@@ -410,45 +410,36 @@
                 total.astype(BF16), "fsdp", scatter_dimension=0, tiled=True,
                 axis_index_groups=outer_groups,
             ).astype(F32)
-        gradient = total / (tokens * n)
-        squares.append(jnp.sum(gradient * gradient))
-        narrow = gradient.astype(BF16)
-        here = owned(narrow, rep // 2)
-        there = owned(narrow, 1 - rep // 2)
-        sent.append(
-            {
-                2: start(there, hops[2](c), "rep"),
-                3: start(there, hops[3](c), "rep"),
-                1: start(here, hops[1](c), "rep"),
-            }
-        )
-        own_gradient.append(owned(narrow, rep // 2))
+        gradient.append(total / (tokens * n))
+        squares.append(jnp.sum(gradient[c] * gradient[c]))
         if c == 0:
             back = done(place(back, done(came_late), [far * PAIR + 1 - y], rows))
 
-    square = jnp.broadcast_to(squares[0] + squares[1], (reps * n, 128))
-    square = lax.all_to_all(order.tie(square), ("rep", "fsdp"), 0, 0, tiled=True)
-    square = jnp.sum(square[:, 0].reshape(reps, n), axis=1)
-    factors = jnp.minimum(1.0, 1.0 / (jnp.sqrt(square) + 1e-06))
-
-    def update(gradient, first, second_moment, k):
-        clipped = gradient.astype(F32) * lax.dynamic_index_in_dim(factors, rep ^ k, 0, False)
+    square = jnp.broadcast_to(squares[0] + squares[1], (n, 128))
+    square = lax.all_to_all(square, "fsdp", 0, 0, tiled=True)
+    factor = jnp.minimum(1.0, 1.0 / (jnp.sqrt(jnp.sum(square[:, 0])) + 1e-06))
+
+    def update(parity):
+        quarters = [2 * x + parity for x in range(reps // 2)]
+        first, second_moment = (
+            jnp.concatenate([owned(v[0], q) for q in quarters], axis=1)
+            for v in (adam_first, adam_second)
+        )
+        clipped = jnp.where(parity == 0, gradient[0], gradient[1]) * factor
         first_new = BETA_ONE * first + (1.0 - BETA_ONE) * clipped
         second_new = BETA_TWO * second_moment + (1.0 - BETA_TWO) * clipped * clipped
-        return first_new / (jnp.sqrt(second_new) + ADAM_EPS)
-
-    update_sum = update(
-        jnp.where(core == 0, own_gradient[0], own_gradient[1]),
-        owned(adam_first[0], rep), owned(adam_second[0], rep), 0,
-    )
-    weight_sum = owned(weight, rep)
-    for k in (1, 2, 3):
-        came = [done(sent[c][k]) for c in both]
-        first, second_moment, other_weight = moments[k]
-        update_sum = update_sum + update(
-            jnp.where(core == 0, came[0], came[1]), first, second_moment, k
-        )
-        weight_sum = weight_sum + other_weight
+        return (first_new / (jnp.sqrt(second_new) + ADAM_EPS)).astype(BF16)
+
+    u_mate = start(update(1 - core), swap[1], "rep")
+    u_own = update(core)
+    u_mate = done(u_mate)
+    u_here, u_there = (
+        (owned(u_own, x).astype(F32) + owned(u_mate, x).astype(F32)) for x in (chip_at, 1 - chip_at)
+    )
+    u_x = start(u_there.astype(BF16), swap[2], "rep")
+    u_x = done(u_x)
+    update_sum = u_here + u_x.astype(F32)
+    weight_sum = w_chip + w_x
     updated_sum = (1.0 - RATE_INNER * DECAY) * weight_sum - RATE_INNER * update_sum
     outer_step = anchor - updated_sum / reps
     moment_out = MOMENTUM * outer_moment + outer_step
@@ -460,11 +451,18 @@
     quarters[1] = done(quarters[1])
     quarters[2] = done(quarters[2])
     quarters[3] = start(quarters[2], swap[1], "rep")
-    whole = jnp.zeros((rows, width), F32)
-    for k in (0, 1, 2, 3):
-        whole = lax.dynamic_update_slice(
-            whole, quarters[k].astype(F32), (0, (rep ^ k) * quarter)
-        )
+    even = {k: jnp.where(core == 0, quarters[k], quarters[k ^ 1]) for k in (0, 2)}
+    odd = {k: jnp.where(core == 0, quarters[k ^ 1], quarters[k]) for k in (0, 2)}
+    first_chip = rep // 2 == 0
+    whole = jnp.concatenate(
+        [
+            jnp.where(first_chip, even[0], even[2]),
+            jnp.where(first_chip, odd[0], odd[2]),
+            jnp.where(first_chip, even[2], even[0]),
+            jnp.where(first_chip, odd[2], odd[0]),
+        ],
+        axis=1,
+    ).astype(F32)
     return (back, whole, moment_out)
 
 

time: 314 us -> 283 us (0.901)
  local copies, waits for them, and re-layouts: 36.7 us -> 10.7 us
  starting transfers between devices: 76.5 us -> 64.9 us
  other arithmetic: 34.1 us -> 40.6 us
    unnamed x54 -> x22, local copies, waits for them, and re-layouts: 30.8 us -> 3.18 us
    ppermute x32 -> x26, starting transfers between devices: 72.1 us -> 56.1 us  [the longest x20 47.2 us: start(): return lax.ppermute(self.last, axis, pairs)]
    dynamic_update_slice x4 -> x0, other arithmetic: 13.2 us -> none  [shards(): lax.dynamic_update_slice(whole, quarters[k].astype(F32), (0, (rep ^ k) *...]
    all_to_all x1, waiting for transfers between devices: 11.3 us -> 0.01 us  [shards(): square = lax.all_to_all(square, 'fsdp', 0, 0, tiled=True)]
    ppermute x32 -> x26, waiting for transfers between devices: 83.4 us -> 92.2 us  [the longest x20 49.5 us: start(): return lax.ppermute(self.last, axis, pairs)]
    convert_element_type x2 -> x4, other arithmetic: 5.71 us -> 13.4 us  [the longest x1 6.58 us: update(): return (first_new / (jnp.sqrt(second_new) + ADAM_EPS)).astype(BF16)]
    reduce_sum x1 -> x3, other arithmetic: 0.12 us -> 6.45 us  [the longest x2 5.79 us: shards(): squares.append(jnp.sum(gradient[c] * gradient[c]))]
    dynamic_slice x2 -> x1, local copies, waits for them, and re-layouts: 1.79 us -> 6.9 us  [owned(): return lax.dynamic_slice(value, (0, r * quarter), (value.shape[0], quarter))]
  transfers between devices with their start and end apart: 33 -> 27, of which waited for: 8 -> 11; matrix products, arithmetic and copies ran while one was open for 8% -> 9% of each run, Pallas kernels for 22% -> 23%
where the time goes in v3:
time: 283 us; the launch traced here: 282 us
  waiting for transfers between devices  92.2 us (33%)
  Pallas kernels  70.8 us (25%)
  starting transfers between devices  64.9 us (23%)
  other arithmetic  40.6 us (14%)
  local copies, waits for them, and re-layouts  10.7 us (4%)
    pallas_call x14, Pallas kernels, call(): pl.pallas_call(body, grid_spec=pltpu.PrefetchScalarGridSpec(num_scalar_pr...  70.8 us
    ppermute x20, waiting for transfers between devices, start(): return lax.ppermute(self.last, axis, pairs)  49.5 us
    ppermute x20, starting transfers between devices, start(): return lax.ppermute(self.last, axis, pairs)  47.2 us
    ppermute x1, waiting for transfers between devices, shards(): cot_other = [lax.ppermute(early, 'fsdp', across), None]  24.2 us
    ppermute x1, waiting for transfers between devices, shards(): lax.ppermute(pick(chunk_blocks(1) + column_blocks(second, other), 1), 'fs...  16.9 us
    all_to_all x1, starting transfers between devices, shards(): square = lax.all_to_all(square, 'fsdp', 0, 0, tiled=True)  8.82 us
    dynamic_slice x1, local copies, waits for them, and re-layouts, owned(): return lax.dynamic_slice(value, (0, r * quarter), (value.shape[0], quarter))  6.9 us
    convert_element_type x1, other arithmetic, update(): return (first_new / (jnp.sqrt(second_new) + ADAM_EPS)).astype(BF16)  6.58 us
  transfers between devices with their start and end apart: 27, of which 11 were waited for; matrix products, arithmetic and copies ran while one was open for 9% of the time, Pallas kernels for 23%

profile of v3, /device:TPU:0, one launch (start us, length us, event | category | flops | bytes accessed | tf_op | source)
XLA Modules:
  0.0 282.1 jit_solution(16348872568536671217)
XLA Ops:
  0.7 3.8 %bitcast_convert_fusion.refs_2_ = bf16[512,2048]{1,0:T(8,128)(2,1)} fusion(f32[1,512,2048]{2,1,0:T(8,128)} %param.9), kind=kLoop, calls=%fused_computation.68 | loop fusion | flops 1048576 | bytes 6291456 | tf_op jit(solution)/shard_map/convert_element_type | solution.py:313
  5.1 3.3 %shard_map.94 = bf16[512,1536]{1,0:T(8,128)(2,1)} custom-call(s32[3]{0:T(128)} %pad_add_fusion.2.at_ref, bf16[512,2048]{1,0:T(8,128)(2,1)} %refs_1_.9, bf16[512,2048]{1,0:T(8,128)(2,1)} %refs_1_.9, bf16[512,4096]{1,0:T(8,128)(2,1)} %x_ref.11), custom_call_target="tpu_custom_call" | custom-call | bytes 6291456 | tf_op jit(solution)/shard_map/pallas_call | solution.py:34
  9.0 3.7 %shard_map.95 = f32[512,1024]{1,0:T(8,128)} custom-call(s32[2]{0:T(128)} %pad_add_fusion.3.at_ref, f32[512,2048]{1,0:T(8,128)} %bitcast.51, f32[512,2048]{1,0:T(8,128)} %bitcast.52), custom_call_target="tpu_custom_call" | custom-call | bytes 8388608 | tf_op jit(solution)/shard_map/pallas_call | solution.py:34
  19.2 2.7 bitcast_add_fusion.1
  24.1 3.3 %shard_map.97 = bf16[512,1536]{1,0:T(8,128)(2,1)} custom-call(s32[3]{0:T(128)} %pad_add_fusion.4.at_ref, bf16[512,2048]{1,0:T(8,128)(2,1)} %refs_1_.9, bf16[512,2048]{1,0:T(8,128)(2,1)} %refs_1_.9, bf16[512,4096]{1,0:T(8,128)(2,1)} %x_ref.11), custom_call_target="tpu_custom_call" | custom-call | bytes 6291456 | tf_op jit(solution)/shard_map/pallas_call | solution.py:34
  28.9 24.2 %collective-permute-done.1.x_other_ref.refs_1_.refs_2_.refs_0_ = bf16[512,1536]{1,0:T(8,128)(2,1)S(1)} collective-permute-done((bf16[512,1536]{1,0:T(8,128)(2,1)}, bf16[512,1536]{1,0:T(8,128)(2,1)S(1)}, u32[]{:S(2)}, u32[]{:S(2)}) %collective-permute-start.1) | collective-permute-done | bytes 1572896 | tf_op jit(solution)/shard_map/ppermute | solution.py:319
  54.2 4.5 %shard_map.96 = bf16[512,1024]{1,0:T(8,128)(2,1)} custom-call(s32[2]{0:T(128)} %pad_add_fusion.1.at_ref, bf16[512,4096]{1,0:T(8,128)(2,1)} %x_ref.11, bf16[512,1536]{1,0:T(8,128)(2,1)} %copy-done, bf16[512,2048]{1,0:T(8,128)(2,1)} %refs_1_.9, bf16[512,1536]{1,0:T(8,128)(2,1)} %copy-done), custom_call_target="tpu_custom_call" | custom-call | flops 1073741824 | bytes 4194304 | tf_op jit(solution)/shard_map/pallas_call | solution.py:34
  66.3 2.9 %shard_map.98 = bf16[512,1024]{1,0:T(8,128)(2,1)} custom-call(s32[2]{0:T(128)} %pad_add_fusion.5.at_ref, bf16[512,4096]{1,0:T(8,128)(2,1)} %x_ref.11, bf16[512,4096]{1,0:T(8,128)(2,1)} %x_ref.11), custom_call_target="tpu_custom_call" | custom-call | bytes 4194304 | tf_op jit(solution)/shard_map/pallas_call | solution.py:34
  69.2 16.9 %collective-permute-done.5.refs_1_.x_other_ref.refs_3_ = bf16[512,1536]{1,0:T(8,128)(2,1)S(1)} collective-permute-done((bf16[512,1536]{1,0:T(8,128)(2,1)}, bf16[512,1536]{1,0:T(8,128)(2,1)S(1)}, u32[]{:S(2)}, u32[]{:S(2)}) %collective-permute-start.5) | collective-permute-done | bytes 1572896 | tf_op jit(solution)/shard_map/ppermute | solution.py:328
  87.3 4.5 %shard_map.99 = bf16[512,1024]{1,0:T(8,128)(2,1)} custom-call(s32[2]{0:T(128)} %pad_add_fusion.1.at_ref, bf16[512,4096]{1,0:T(8,128)(2,1)} %x_ref.11, bf16[512,1536]{1,0:T(8,128)(2,1)} %copy-done, bf16[512,2048]{1,0:T(8,128)(2,1)} %refs_1_.9, bf16[512,1536]{1,0:T(8,128)(2,1)} %copy-done.1), custom_call_target="tpu_custom_call" | custom-call | flops 1073741824 | bytes 4194304 | tf_op jit(solution)/shard_map/pallas_call | solution.py:34
  91.8 3.2 %collective-permute-start.7 = (bf16[512,1024]{1,0:T(8,128)(2,1)}, bf16[512,1024]{1,0:T(8,128)(2,1)}, u32[]{:S(2)}, u32[]{:S(2)}) collective-permute-start(bf16[512,1024]{1,0:T(8,128)(2,1)} %shard_map.99), channel_id=1, source_target_pairs={{0,2},{1,3},{6,4},{7,5},{8,10},{9,11},{14,12},{15,13},{16,18},{17,... | collective-permute-start | bytes 3145736 | tf_op jit(solution)/shard_map/ppermute | solution.py:252
  97.0 6.5 %shard_map.100 = bf16[512,2048]{1,0:T(8,128)(2,1)} custom-call(s32[2]{0:T(128)} %pad_add_fusion.at_ref, bf16[512,4096]{1,0:T(8,128)(2,1)} %x_ref.11, bf16[512,1536]{1,0:T(8,128)(2,1)} %copy-done.1, bf16[512,2048]{1,0:T(8,128)(2,1)} %refs_1_.9, bf16[512,2048]{1,0:T(8,128)(2,1)} %refs_1_.9, bf16[512,1536]{1,0:T(8,128)(2,1)} %copy-done, bf16[512,1536]{1,0:T(8,128)(2,1)} %copy-done.1), custom_call_target="tpu_custom_call" | custom-call | flops 2147483648 | bytes 8388608 | tf_op jit(solution)/shard_map/pallas_call | solution.py:34
  103.5 2.7 collective-permute-start.13
  107.9 10.0 %collective-permute-done.7 = bf16[512,1024]{1,0:T(8,128)(2,1)} collective-permute-done((bf16[512,1024]{1,0:T(8,128)(2,1)}, bf16[512,1024]{1,0:T(8,128)(2,1)}, u32[]{:S(2)}, u32[]{:S(2)}) %collective-permute-start.7) | collective-permute-done | bytes 1048608 | tf_op jit(solution)/shard_map/ppermute | solution.py:252
  125.7 13.5 %shard_map.101 = (bf16[512,4096]{1,0:T(8,128)(2,1)}, bf16[512,1536]{1,0:T(8,128)(2,1)}) custom-call(s32[3]{0:T(128)} %pad_add_fusion.7.at_ref, bf16[512,2048]{1,0:T(8,128)(2,1)} %refs_1_.9, bf16[512,1536]{1,0:T(8,128)(2,1)} %copy-done, bf16[512,1536]{1,0:T(8,128)(2,1)} %copy-done.1, bf16[512,2048]{1,0:T(8,128)(2,1)} %bitcast_convert_fusion.refs_2_, ...), custom_call_target="tpu_custom_call" | custom-call | flops 6442450944 | bytes 23068672 | tf_op jit(solution)/shard_map/pallas_call | solution.py:34
  141.7 5.0 %shard_map.102 = bf16[512,1024]{1,0:T(8,128)(2,1)} custom-call(s32[2]{0:T(128)} %pad_add_fusion.6.at_ref, bf16[512,4096]{1,0:T(8,128)(2,1)} %x_ref.11, bf16[512,1024]{1,0:T(8,128)(2,1)} %copy-done.2, bf16[512,2048]{1,0:T(8,128)(2,1)} %refs_1_.9, bf16[512,1536]{1,0:T(8,128)(2,1)} %copy-done, bf16[512,1024]{1,0:T(8,128)(2,1)} %collective-permute-done.14.refs_2_), custom_call_target="tpu_custom_call" | custom-call | flops 1073741824 | bytes 4194304 | tf_op jit(solution)/shard_map/pallas_call | solution.py:34
  146.7 13.2 %collective-permute-start.17 = (bf16[512,1024]{1,0:T(8,128)(2,1)}, bf16[512,1024]{1,0:T(8,128)(2,1)}, u32[]{:S(2)}, u32[]{:S(2)}) collective-permute-start(bf16[512,1024]{1,0:T(8,128)(2,1)} %shard_map.102), channel_id=1, source_target_pairs={{0,2},{1,3},{2,0},{3,1},{4,6},{5,7},{6,4},{7,5},{8,10},{9,11},{10,... | collective-permute-start | bytes 3145736 | tf_op jit(solution)/shard_map/ppermute | solution.py:252
  159.9 3.0 %collective-permute-done.13 = bf16[512,2048]{1,0:T(8,128)(2,1)} collective-permute-done((bf16[512,2048]{1,0:T(8,128)(2,1)}, bf16[512,2048]{1,0:T(8,128)(2,1)}, u32[]{:S(2)}, u32[]{:S(2)}) %collective-permute-start.13) | collective-permute-done | bytes 2097184 | tf_op jit(solution)/shard_map/ppermute | solution.py:252
  167.3 4.9 %shard_map.103 = bf16[512,1024]{1,0:T(8,128)(2,1)} custom-call(s32[2]{0:T(128)} %pad_add_fusion.6.at_ref, bf16[512,4096]{1,0:T(8,128)(2,1)} %x_ref.11, bf16[512,1024]{1,0:T(8,128)(2,1)} %copy-done.2, bf16[512,2048]{1,0:T(8,128)(2,1)} %refs_1_.9, bf16[512,1536]{1,0:T(8,128)(2,1)} %copy-done.1, bf16[512,1024]{1,0:T(8,128)(2,1)} %collective-permute-done.12.refs_2_), custom_call_target="tpu_custom_call" | custom-call | flops 1073741824 | bytes 4194304 | tf_op jit(solution)/shard_map/pallas_call | solution.py:34
  172.2 7.7 %collective-permute-start.19 = (bf16[512,1024]{1,0:T(8,128)(2,1)}, bf16[512,1024]{1,0:T(8,128)(2,1)}, u32[]{:S(2)}, u32[]{:S(2)}) collective-permute-start(bf16[512,1024]{1,0:T(8,128)(2,1)} %shard_map.103), channel_id=1, source_target_pairs={{0,2},{1,3},{2,0},{3,1},{4,6},{5,7},{6,4},{7,5},{8,10},{9,11},{10,... | collective-permute-start | bytes 3145736 | tf_op jit(solution)/shard_map/ppermute | solution.py:252
  182.2 6.3 %shard_map.104 = (bf16[512,4096]{1,0:T(8,128)(2,1)}, bf16[512,512]{1,0:T(8,128)(2,1)}) custom-call(s32[1]{0:T(128)} %bitcast.15.at_ref, bf16[512,2048]{1,0:T(8,128)(2,1)} %refs_1_.9, bf16[512,1536]{1,0:T(8,128)(2,1)} %copy-done, bf16[512,1536]{1,0:T(8,128)(2,1)} %copy-done.1, ...), custom_call_target="tpu_custom_call", output_to_operand_aliasing={{0}: (6, {})} | custom-call | flops 2147483648 | bytes 18874368 | tf_op jit(solution)/shard_map/pallas_call | solution.py:34
  190.7 6.4 %shard_map.107 = (f32[512,1024]{1,0:T(8,128)}, f32[512,1024]{1,0:T(8,128)}) custom-call(s32[2]{0:T(128)} %pad_add_fusion.9.at_ref, bf16[512,4096]{1,0:T(8,128)(2,1)} %x_ref.11, bf16[512,1024]{1,0:T(8,128)(2,1)} %copy-done.2, bf16[512,2048]{1,0:T(8,128)(2,1)} %refs_1_.9, bf16[512,2048]{1,0:T(8,128)(2,1)} %refs_1_.9, bf16[512,1536]{1,0:T(8,128)(2,1)} %copy-done, ...), custom_call_target="tpu_custom_call" | custom-call | flops 2147483648 | bytes 16777216 | tf_op jit(solution)/shard_map/pallas_call | solution.py:34
  197.1 4.2 %shard_map.105.held_ref = bf16[512,4096]{1,0:T(8,128)(2,1)} custom-call(s32[3]{0:T(128)} %pad_add_fusion.8.at_ref, bf16[512,1536]{1,0:T(8,128)(2,1)} %collective-permute-done.18.came_ref, bf16[512,4096]{1,0:T(8,128)(2,1)} %get-tuple-element.107.held_ref), custom_call_target="tpu_custom_call", output_to_operand_aliasing={{}: (2, {})} | custom-call | bytes 16777216 | tf_op jit(solution)/shard_map/pallas_call | solution.py:34
  206.4 6.7 %collective-permute-done.19 = bf16[512,1024]{1,0:T(8,128)(2,1)} collective-permute-done((bf16[512,1024]{1,0:T(8,128)(2,1)}, bf16[512,1024]{1,0:T(8,128)(2,1)}, u32[]{:S(2)}, u32[]{:S(2)}) %collective-permute-start.19) | collective-permute-done | bytes 1048608 | tf_op jit(solution)/shard_map/ppermute | solution.py:252
  213.1 3.4 %multiply_reduce_fusion = f32[]{:T(128)} fusion(bf16[512,1024]{1,0:T(8,128)(2,1)} %collective-permute-done.20, f32[512,1024]{1,0:T(8,128)} %get-tuple-element.115, bf16[512,1024]{1,0:T(8,128)(2,1)} %collective-permute-done.19), kind=kLoop, calls=%fused_computation.17 | loop fusion | flops 3670015 | bytes 4194308 | tf_op jit(solution)/shard_map/reduce_sum | solution.py:414
  218.3 8.8 %all-to-all-start = ((f32[8,1,128]{2,1,0:T(1,128)}), f32[8,1,128]{2,1,0:T(1,128)S(1)}, u32[]{:S(2)}, u32[]{:S(2)}) async-start(f32[8,1,128]{2,1,0:T(1,128)} %broadcast_in_dim.3), calls=%async_computation | async-start | bytes 8192 | tf_op jit(solution)/shard_map/all_to_all | solution.py:419
  227.2 6.9 %dynamic-slice_bitcast_fusion.5 = (f32[512,512]{1,0:T(8,128)}, f32[512,512]{1,0:T(8,128)}, f32[512,512]{1,0:T(8,128)}, f32[512,512]{1,0:T(8,128)}, f32[512,512]{...) fusion(f32[1,512,2048]{2,1,0:T(8,128)} %param.11, s32[]{:T(128)S(6)} %select_n.127, ...), kind=kLoop, calls=%fused_computation.42 | loop fusion | bytes 16777232 | tf_op jit(solution)/shard_map/dynamic_slice | solution.py:298
  235.4 6.6 %fusion.11 = (bf16[512,1024]{1,0:T(8,128)(2,1)S(1)}, bf16[512,1024]{1,0:T(8,128)(2,1)S(1)}) fusion(f32[512,512]{1,0:T(8,128)} %get-tuple-element.136, f32[512,512]{1,0:T(8,128)} %get-tuple-element.135, f32[512,512]{1,0:T(8,128)} %get-tuple-element.151, f32[512,512]{1,0:T(8,128)} %get-tuple-element.152, f32[]{:T(128)S(6)} %min.3, pred[]{:T(512)S(6)} %eq.18, ...), kind=kLoop, calls=%fused_computation.24 | loop fusion | flops 19922944 | bytes 18874374 | tf_op jit(solution)/shard_map/convert_element_type | solution.py:431
  242.1 2.6 collective-permute-done.21
  246.5 12.5 %collective-permute-done.22 = bf16[512,512]{1,0:T(8,128)(2,1)S(1)} collective-permute-done((bf16[512,512]{1,0:T(8,128)(2,1)S(1)}, bf16[512,512]{1,0:T(8,128)(2,1)S(1)}, u32[]{:S(2)}, u32[]{:S(2)}) %collective-permute-start.22) | collective-permute-done | bytes 524320 | tf_op jit(solution)/shard_map/ppermute | solution.py:252
  259.0 4.1 %subtract_convert_fusion = (bf16[512,512]{1,0:T(8,128)(2,1)S(1)}, f32[512,512]{1,0:T(8,128)}) fusion(f32[512,512]{1,0:T(8,128)S(1)} %copy-done.8, f32[512,512]{1,0:T(8,128)} %param.13, bf16[512,512]{1,0:T(8,128)(2,1)S(1)} %collective-permute-done.22, bf16[512,1024]{1,0:T(8,128)(2,1)S(1)} %collective-permute-done.21, s32[]{:T(128)S(6)} %select_n.126, ...), kind=kLoop, calls=%fused_computation.34 | loop fusion | flops 4980736 | bytes 8388616 | tf_op jit(solution)/shard_map/convert_element_type | solution.py:446
  265.0 12.4 %collective-permute-done.24 = bf16[512,512]{1,0:T(8,128)(2,1)S(1)} collective-permute-done((bf16[512,512]{1,0:T(8,128)(2,1)S(1)}, bf16[512,512]{1,0:T(8,128)(2,1)S(1)}, u32[]{:S(2)}, u32[]{:S(2)}) %collective-permute-start.24) | collective-permute-done | bytes 524320 | tf_op jit(solution)/shard_map/ppermute | solution.py:252
  (84 shorter events, 59.0 us)
Async XLA Ops:
  12.6 6.6 %collective-permute-start.2 = (f32[512,1024]{1,0:T(8,128)}, f32[512,1024]{1,0:T(8,128)}, u32[]{:S(2)}, u32[]{:S(2)}) collective-permute-start(f32[512,1024]{1,0:T(8,128)} %shard_map.95), channel_id=1, source_target_pairs={{0,8},{8,0},{16,24},{24,16},{1,9},{9,1},{17,25},{25,17},{2,10},{10... | collective-permute-start | bytes 6291464 | tf_op jit(solution)/shard_map/ppermute | solution.py:326
  13.1 49.2 %collective-permute-start = (bf16[512,2048]{1,0:T(8,128)(2,1)}, bf16[512,2048]{1,0:T(8,128)(2,1)}, u32[]{:S(2)}, u32[]{:S(2)}) collective-permute-start(bf16[512,2048]{1,0:T(8,128)(2,1)} %bitcast_convert_fusion.refs_2_), channel_id=1, source_target_pairs={{0,2},{1,3},{2,0},{3,1},{4,6},{5,7},{6,4},{7,5},{8,10},{9,11},{10,... | collective-permute-start | bytes 6291464 | tf_op jit(solution)/shard_map/ppermute | solution.py:316
  15.7 37.4 %collective-permute-start.1 = (bf16[512,1536]{1,0:T(8,128)(2,1)}, bf16[512,1536]{1,0:T(8,128)(2,1)S(1)}, u32[]{:S(2)}, u32[]{:S(2)}) collective-permute-start(bf16[512,1536]{1,0:T(8,128)(2,1)} %shard_map.94), channel_id=1, source_target_pairs={{0,1},{1,0},{2,3},{3,2},{4,5},{5,4},{6,7},{7,6},{8,9},{9,8},{10,11... | collective-permute-start | bytes 4718600 | tf_op jit(solution)/shard_map/ppermute | solution.py:319
  17.2 47.2 %collective-permute-start.6 = (bf16[512,2048]{1,0:T(8,128)(2,1)}, bf16[512,2048]{1,0:T(8,128)(2,1)}, u32[]{:S(2)}, u32[]{:S(2)}) collective-permute-start(bf16[512,2048]{1,0:T(8,128)(2,1)} %bitcast_convert_fusion.refs_2_), channel_id=1, source_target_pairs={{2,4},{3,5},{4,2},{5,3},{10,12},{11,13},{12,10},{13,11},{18,20},{1... | collective-permute-start | bytes 6291464 | tf_op jit(solution)/shard_map/ppermute | solution.py:317
  21.9 40.3 %collective-permute-start.3 = (f32[512,512]{1,0:T(8,128)}, f32[512,512]{1,0:T(8,128)}, u32[]{:S(2)}, u32[]{:S(2)}) collective-permute-start(f32[512,512]{1,0:T(8,128)} %bitcast_add_fusion.1), channel_id=1, source_target_pairs={{0,16},{8,24},{16,0},{24,8},{1,17},{9,25},{17,1},{25,9},{2,18},{10... | collective-permute-start | bytes 3145736 | tf_op jit(solution)/shard_map/ppermute | solution.py:334
  27.4 58.7 %collective-permute-start.5 = (bf16[512,1536]{1,0:T(8,128)(2,1)}, bf16[512,1536]{1,0:T(8,128)(2,1)S(1)}, u32[]{:S(2)}, u32[]{:S(2)}) collective-permute-start(bf16[512,1536]{1,0:T(8,128)(2,1)} %shard_map.97), channel_id=1, source_target_pairs={{0,1},{1,0},{2,3},{3,2},{4,5},{5,4},{6,7},{7,6},{8,9},{9,8},{10,11... | collective-permute-start | bytes 4718600 | tf_op jit(solution)/shard_map/ppermute | solution.py:328
  58.8 36.2 %collective-permute-start.8 = (bf16[512,1024]{1,0:T(8,128)(2,1)}, bf16[512,1024]{1,0:T(8,128)(2,1)S(1)}, u32[]{:S(2)}, u32[]{:S(2)}) collective-permute-start(bf16[512,1024]{1,0:T(8,128)(2,1)} %shard_map.96), channel_id=1, source_target_pairs={{0,2},{1,3},{6,4},{7,5},{8,10},{9,11},{14,12},{15,13},{16,18},{17,... | collective-permute-start | bytes 3145736 | tf_op jit(solution)/shard_map/ppermute | solution.py:252
  62.3 58.2 %collective-permute-start.4 = (bf16[512,2048]{1,0:T(8,128)(2,1)}, bf16[512,2048]{1,0:T(8,128)(2,1)}, u32[]{:S(2)}, u32[]{:S(2)}) collective-permute-start(bf16[512,2048]{1,0:T(8,128)(2,1)} %collective-permute-done.refs_3_), channel_id=1, source_target_pairs={{2,4},{3,5},{4,2},{5,3},{10,12},{11,13},{12,10},{13,11},{18,20},{1... | collective-permute-start | bytes 6291464 | tf_op jit(solution)/shard_map/ppermute | solution.py:252
  64.3 59.1 %collective-permute-start.11 = (bf16[512,2048]{1,0:T(8,128)(2,1)}, bf16[512,2048]{1,0:T(8,128)(2,1)}, u32[]{:S(2)}, u32[]{:S(2)}) collective-permute-start(bf16[512,2048]{1,0:T(8,128)(2,1)} %collective-permute-done.6.refs_4_), channel_id=1, source_target_pairs={{2,0},{3,1},{4,6},{5,7},{10,8},{11,9},{12,14},{13,15},{18,16},{19,... | collective-permute-start | bytes 6291464 | tf_op jit(solution)/shard_map/ppermute | solution.py:252
  69.2 25.8 %copy-start.6 = (bf16[512,1024]{1,0:T(8,128)(2,1)S(1)}, bf16[512,1024]{1,0:T(8,128)(2,1)}, u32[]{:S(2)}) copy-start(bf16[512,1024]{1,0:T(8,128)(2,1)} %shard_map.96) | copy-start | bytes 3145732
  91.8 26.0 %collective-permute-start.7 = (bf16[512,1024]{1,0:T(8,128)(2,1)}, bf16[512,1024]{1,0:T(8,128)(2,1)}, u32[]{:S(2)}, u32[]{:S(2)}) collective-permute-start(bf16[512,1024]{1,0:T(8,128)(2,1)} %shard_map.99), channel_id=1, source_target_pairs={{0,2},{1,3},{6,4},{7,5},{8,10},{9,11},{14,12},{15,13},{16,18},{17,... | collective-permute-start | bytes 3145736 | tf_op jit(solution)/shard_map/ppermute | solution.py:252
  97.0 9.2 %copy-start.9 = (bf16[512,1024]{1,0:T(8,128)(2,1)S(1)}, bf16[512,1024]{1,0:T(8,128)(2,1)}, u32[]{:S(2)}) copy-start(bf16[512,1024]{1,0:T(8,128)(2,1)} %shard_map.98) | copy-start | bytes 3145732
  97.0 20.8 %copy-start.7 = (bf16[512,1024]{1,0:T(8,128)(2,1)S(1)}, bf16[512,1024]{1,0:T(8,128)(2,1)}, u32[]{:S(2)}) copy-start(bf16[512,1024]{1,0:T(8,128)(2,1)} %shard_map.99) | copy-start | bytes 3145732
  103.5 59.3 %collective-permute-start.13 = (bf16[512,2048]{1,0:T(8,128)(2,1)}, bf16[512,2048]{1,0:T(8,128)(2,1)}, u32[]{:S(2)}, u32[]{:S(2)}) collective-permute-start(bf16[512,2048]{1,0:T(8,128)(2,1)} %shard_map.100), channel_id=1, source_target_pairs={{0,2},{1,3},{6,4},{7,5},{8,10},{9,11},{14,12},{15,13},{16,18},{17,... | collective-permute-start | bytes 6291464 | tf_op jit(solution)/shard_map/ppermute | solution.py:252
  106.2 33.0 %collective-permute-start.10 = (bf16[512,1024]{1,0:T(8,128)(2,1)S(1)}, bf16[512,1024]{1,0:T(8,128)(2,1)S(1)}, u32[]{:S(2)}, u32[]{:S(2)}) collective-permute-start(bf16[512,1024]{1,0:T(8,128)(2,1)S(1)} %copy-done.9), channel_id=1, source_target_pairs={{0,1},{1,0},{2,3},{3,2},{4,5},{5,4},{6,7},{7,6},{8,9},{9,8},{10,11... | collective-permute-start | bytes 3145736 | tf_op jit(solution)/shard_map/ppermute | solution.py:252
  120.5 59.4 %collective-permute-start.9 = (bf16[512,2048]{1,0:T(8,128)(2,1)}, bf16[512,2048]{1,0:T(8,128)(2,1)}, u32[]{:S(2)}, u32[]{:S(2)}) collective-permute-start(bf16[512,2048]{1,0:T(8,128)(2,1)} %collective-permute-done.4.refs_2_), channel_id=1, source_target_pairs={{2,0},{3,1},{4,6},{5,7},{10,8},{11,9},{12,14},{13,15},{18,16},{19,... | collective-permute-start | bytes 6291464 | tf_op jit(solution)/shard_map/ppermute | solution.py:252
  121.8 19.9 %collective-permute-start.14 = (bf16[512,1024]{1,0:T(8,128)(2,1)}, bf16[512,1024]{1,0:T(8,128)(2,1)}, u32[]{:S(2)}, u32[]{:S(2)}) collective-permute-start(bf16[512,1024]{1,0:T(8,128)(2,1)} %add_convert_fusion.1), channel_id=1, source_target_pairs={{2,4},{3,5},{4,2},{5,3},{10,12},{11,13},{12,10},{13,11},{18,20},{1... | collective-permute-start | bytes 3145736 | tf_op jit(solution)/shard_map/ppermute | solution.py:252
  123.5 43.8 %collective-permute-start.12 = (bf16[512,1024]{1,0:T(8,128)(2,1)}, bf16[512,1024]{1,0:T(8,128)(2,1)}, u32[]{:S(2)}, u32[]{:S(2)}) collective-permute-start(bf16[512,1024]{1,0:T(8,128)(2,1)} %add_convert_fusion), channel_id=1, source_target_pairs={{2,4},{3,5},{4,2},{5,3},{10,12},{11,13},{12,10},{13,11},{18,20},{1... | collective-permute-start | bytes 3145736 | tf_op jit(solution)/shard_map/ppermute | solution.py:252
  139.3 49.2 %collective-permute-start.18 = (bf16[512,1536]{1,0:T(8,128)(2,1)}, bf16[512,1536]{1,0:T(8,128)(2,1)}, u32[]{:S(2)}, u32[]{:S(2)}) collective-permute-start(bf16[512,1536]{1,0:T(8,128)(2,1)} %get-tuple-element.92), channel_id=1, source_target_pairs={{0,1},{1,0},{2,3},{3,2},{4,5},{5,4},{6,7},{7,6},{8,9},{9,8},{10,11... | collective-permute-start | bytes 4718600 | tf_op jit(solution)/shard_map/ppermute | solution.py:252
  141.7 21.2 %copy-start.3 = (bf16[512,2048]{1,0:T(8,128)(2,1)S(1)}, bf16[512,2048]{1,0:T(8,128)(2,1)}, u32[]{:S(2)}) copy-start(bf16[512,2048]{1,0:T(8,128)(2,1)} %shard_map.100) | copy-start | bytes 6291460
  146.7 54.6 %collective-permute-start.17 = (bf16[512,1024]{1,0:T(8,128)(2,1)}, bf16[512,1024]{1,0:T(8,128)(2,1)}, u32[]{:S(2)}, u32[]{:S(2)}) collective-permute-start(bf16[512,1024]{1,0:T(8,128)(2,1)} %shard_map.102), channel_id=1, source_target_pairs={{0,2},{1,3},{2,0},{3,1},{4,6},{5,7},{6,4},{7,5},{8,10},{9,11},{10,... | collective-permute-start | bytes 3145736 | tf_op jit(solution)/shard_map/ppermute | solution.py:252
  166.6 34.7 %collective-permute-start.16 = (bf16[512,1024]{1,0:T(8,128)(2,1)}, bf16[512,1024]{1,0:T(8,128)(2,1)S(1)}, u32[]{:S(2)}, u32[]{:S(2)}) collective-permute-start(bf16[512,1024]{1,0:T(8,128)(2,1)} %get-tuple-element.97), channel_id=1, source_target_pairs={{2,4},{3,5},{4,2},{5,3},{10,12},{11,13},{12,10},{13,11},{18,20},{1... | collective-permute-start | bytes 3145736 | tf_op jit(solution)/shard_map/ppermute | solution.py:252
  172.2 41.0 %collective-permute-start.19 = (bf16[512,1024]{1,0:T(8,128)(2,1)}, bf16[512,1024]{1,0:T(8,128)(2,1)}, u32[]{:S(2)}, u32[]{:S(2)}) collective-permute-start(bf16[512,1024]{1,0:T(8,128)(2,1)} %shard_map.103), channel_id=1, source_target_pairs={{0,2},{1,3},{2,0},{3,1},{4,6},{5,7},{6,4},{7,5},{8,10},{9,11},{10,... | collective-permute-start | bytes 3145736 | tf_op jit(solution)/shard_map/ppermute | solution.py:252
  179.9 33.2 %collective-permute-start.20 = (bf16[512,1024]{1,0:T(8,128)(2,1)}, bf16[512,1024]{1,0:T(8,128)(2,1)}, u32[]{:S(2)}, u32[]{:S(2)}) collective-permute-start(bf16[512,1024]{1,0:T(8,128)(2,1)} %get-tuple-element.98), channel_id=1, source_target_pairs={{2,4},{3,5},{4,2},{5,3},{10,12},{11,13},{12,10},{13,11},{18,20},{1... | collective-permute-start | bytes 3145736 | tf_op jit(solution)/shard_map/ppermute | solution.py:252
  188.5 15.2 %collective-permute-start.15 = (bf16[512,512]{1,0:T(8,128)(2,1)}, bf16[512,512]{1,0:T(8,128)(2,1)S(1)}, u32[]{:S(2)}, u32[]{:S(2)}) collective-permute-start(bf16[512,512]{1,0:T(8,128)(2,1)} %get-tuple-element.105), channel_id=1, source_target_pairs={{0,1},{1,0},{2,3},{3,2},{4,5},{5,4},{6,7},{7,6},{8,9},{9,8},{10,11... | collective-permute-start | bytes 1572872 | tf_op jit(solution)/shard_map/ppermute | solution.py:252
  218.3 15.7 %all-to-all-start = ((f32[8,1,128]{2,1,0:T(1,128)}), f32[8,1,128]{2,1,0:T(1,128)S(1)}, u32[]{:S(2)}, u32[]{:S(2)}) async-start(f32[8,1,128]{2,1,0:T(1,128)} %broadcast_in_dim.3), calls=%async_computation | async-start | bytes 8192 | tf_op jit(solution)/shard_map/all_to_all | solution.py:419
  242.0 17.0 %copy-start.8 = (f32[512,512]{1,0:T(8,128)S(1)}, f32[512,512]{1,0:T(8,128)}, u32[]{:S(2)}) copy-start(f32[512,512]{1,0:T(8,128)} %param.12) | copy-start | bytes 3145732
  242.0 2.7 collective-permute-start.21
  245.0 14.0 %collective-permute-start.22 = (bf16[512,512]{1,0:T(8,128)(2,1)S(1)}, bf16[512,512]{1,0:T(8,128)(2,1)S(1)}, u32[]{:S(2)}, u32[]{:S(2)}) collective-permute-start(bf16[512,512]{1,0:T(8,128)(2,1)S(1)} %add_convert_fusion.2), channel_id=1, source_target_pairs={{0,16},{8,24},{16,0},{24,8},{1,17},{9,25},{17,1},{25,9},{2,18},{10... | collective-permute-start | bytes 1572872 | tf_op jit(solution)/shard_map/ppermute | solution.py:252
  263.1 1.9 collective-permute-start.23
  263.1 14.3 %collective-permute-start.24 = (bf16[512,512]{1,0:T(8,128)(2,1)S(1)}, bf16[512,512]{1,0:T(8,128)(2,1)S(1)}, u32[]{:S(2)}, u32[]{:S(2)}) collective-permute-start(bf16[512,512]{1,0:T(8,128)(2,1)S(1)} %get-tuple-element.123), channel_id=1, source_target_pairs={{0,16},{8,24},{16,0},{24,8},{1,17},{9,25},{17,1},{25,9},{2,18},{10... | collective-permute-start | bytes 1572872 | tf_op jit(solution)/shard_map/ppermute | solution.py:252
  277.4 1.9 collective-permute-start.25
  (6 other events, 12.5 us)

commit v4 on v3

--- a/solution.py
+++ b/solution.py
@@ -82,6 +82,53 @@
     )
 
 
+def front_body(picked, at_ref, weight_ref, *refs):
+    del at_ref
+    half_ref, early_ref, mate_ref = refs[picked + 2 :]
+    half_ref[...] = weight_ref[...].astype(BF16)
+    for refs, out_ref in ((refs[:picked], early_ref), (refs[picked : picked + 2], mate_ref)):
+        offset = 0
+        for ref in refs:
+            out_ref[:, offset : offset + ref.shape[1]] = ref[...]
+            offset += ref.shape[1]
+
+
+def front(weight, mate, blocks, quarter):
+    rows, width = weight.shape
+    height = blocks[0][0].shape[0]
+    steps = 4
+    sizes = [size for _, size, _ in blocks] + [quarter] * 2
+    ats = [jnp.int32(i) for _, _, i in blocks] + [mate, 2 + mate]
+    arrays = [v for v, _, _ in blocks] + [weight] * 2
+    return call(
+        functools.partial(front_body, len(blocks)),
+        (steps,),
+        jnp.stack(ats),
+        [pl.BlockSpec((rows // steps, width), lambda j, at: (j, 0))]
+        + [
+            pl.BlockSpec(
+                (v.shape[0] // steps, size),
+                functools.partial(lambda k, j, at: (j, at[k]), k),
+            )
+            for k, (v, size) in enumerate(zip(arrays, sizes))
+        ],
+        [
+            pl.BlockSpec((rows // steps, width), lambda j, at: (j, 0)),
+            pl.BlockSpec((height // steps, sum(sizes[:-2])), lambda j, at: (j, 0)),
+            pl.BlockSpec((rows // steps, 2 * quarter), lambda j, at: (j, 0)),
+        ],
+        [
+            jax.ShapeDtypeStruct((rows, width), BF16),
+            jax.ShapeDtypeStruct((height, sum(sizes[:-2])), BF16),
+            jax.ShapeDtypeStruct((rows, 2 * quarter), F32),
+        ],
+        [],
+        {},
+        0,
+        (weight, *arrays),
+    )
+
+
 def product_body(chunks, added, split, at_ref, x_ref, x_other_ref, *refs):
     del at_ref
     own, other = refs[0:chunks], refs[chunks : 2 * chunks]
@@ -310,20 +357,18 @@
     def chunk_blocks(c):
         return [(cotangent, quarter, q) for q in range(c, reps, 2)]
 
-    half = weight.astype(BF16)
+    half, early, w_mate = front(
+        weight, 1 - core, chunk_blocks(0) + column_blocks(far, 1 - y), quarter
+    )
     if outer > 1:
         half = lax.all_gather(half, "fsdp", axis=0, tiled=True, axis_index_groups=outer_groups)
     w_near = lax.ppermute(half, "fsdp", ends)
     w_mid = lax.ppermute(half, "fsdp", centre)
-    early = pick(chunk_blocks(0) + column_blocks(far, 1 - y), 1)
     cot_other = [lax.ppermute(early, "fsdp", across), None]
     x_at = 2 * quarter // unit
 
     chip_at = rep // 2
-    order.last = (half, early)
-    mate = order.tie(1 - core)
-    blocks = [(weight, quarter, 2 * x + mate) for x in range(reps // 2)]
-    w_mate = done(lax.ppermute(pick(blocks, 1), "rep", swap[1]))
+    w_mate = done(lax.ppermute(w_mate, "rep", swap[1]))
     other = order.tie(1 - y)
     cot_other[1] = lax.ppermute(
         pick(chunk_blocks(1) + column_blocks(second, other), 1), "fsdp", across
@@ -413,8 +458,14 @@
         gradient.append(total / (tokens * n))
         squares.append(jnp.sum(gradient[c] * gradient[c]))
         if c == 0:
+            step_base = anchor - (1.0 - RATE_INNER * DECAY) / reps * (w_chip + w_x)
+            moment_base = MOMENTUM * outer_moment + step_base
+            synced_base = anchor - RATE_OUTER * (step_base + MOMENTUM * moment_base)
+            synced_base = order.tie(synced_base.astype(BF16))
+            synced_there = lax.ppermute(synced_base, "rep", swap[2])
             back = done(place(back, done(came_late), [far * PAIR + 1 - y], rows))
 
+    synced_there = done(synced_there)
     square = jnp.broadcast_to(squares[0] + squares[1], (n, 128))
     square = lax.all_to_all(square, "fsdp", 0, 0, tiled=True)
     factor = jnp.minimum(1.0, 1.0 / (jnp.sqrt(jnp.sum(square[:, 0])) + 1e-06))
@@ -430,37 +481,30 @@
         second_new = BETA_TWO * second_moment + (1.0 - BETA_TWO) * clipped * clipped
         return (first_new / (jnp.sqrt(second_new) + ADAM_EPS)).astype(BF16)
 
-    u_mate = start(update(1 - core), swap[1], "rep")
-    u_own = update(core)
+    u_mate, u_own = lax.optimization_barrier((update(1 - core), update(core)))
+    u_mate = start(u_mate, swap[1], "rep")
     u_mate = done(u_mate)
-    u_here, u_there = (
-        (owned(u_own, x).astype(F32) + owned(u_mate, x).astype(F32)) for x in (chip_at, 1 - chip_at)
-    )
-    u_x = start(u_there.astype(BF16), swap[2], "rep")
-    u_x = done(u_x)
-    update_sum = u_here + u_x.astype(F32)
-    weight_sum = w_chip + w_x
-    updated_sum = (1.0 - RATE_INNER * DECAY) * weight_sum - RATE_INNER * update_sum
-    outer_step = anchor - updated_sum / reps
-    moment_out = MOMENTUM * outer_moment + outer_step
-    synced = (anchor - RATE_OUTER * (outer_step + MOMENTUM * moment_out)).astype(BF16)
-
-    quarters = {0: synced}
-    quarters[2] = start(synced, swap[2], "rep")
-    quarters[1] = start(synced, swap[1], "rep")
-    quarters[1] = done(quarters[1])
-    quarters[2] = done(quarters[2])
-    quarters[3] = start(quarters[2], swap[1], "rep")
-    even = {k: jnp.where(core == 0, quarters[k], quarters[k ^ 1]) for k in (0, 2)}
-    odd = {k: jnp.where(core == 0, quarters[k ^ 1], quarters[k]) for k in (0, 2)}
-    first_chip = rep // 2 == 0
+    u_chip = (u_own.astype(F32) + u_mate.astype(F32)).astype(BF16)
+    u_x = done(start(u_chip, swap[2], "rep"))
+    update_sum = u_chip.astype(F32) + u_x.astype(F32)
+    scale = RATE_INNER / reps
+    moment_out = moment_base + scale * jnp.where(
+        chip_at == 0, update_sum[:, :quarter], update_sum[:, quarter:]
+    )
+    base = jnp.concatenate(
+        [
+            jnp.where(chip_at == 0, synced_base, synced_there),
+            jnp.where(chip_at == 0, synced_there, synced_base),
+        ],
+        axis=1,
+    )
+    synced = base.astype(F32) - RATE_OUTER * (1.0 + MOMENTUM) * scale * update_sum
+    synced = synced.astype(BF16)
+    synced_mate = done(start(synced, swap[1], "rep"))
+    even = jnp.where(core == 0, synced, synced_mate)
+    odd = jnp.where(core == 0, synced_mate, synced)
     whole = jnp.concatenate(
-        [
-            jnp.where(first_chip, even[0], even[2]),
-            jnp.where(first_chip, odd[0], odd[2]),
-            jnp.where(first_chip, even[2], even[0]),
-            jnp.where(first_chip, odd[2], odd[0]),
-        ],
+        [v[:, x * quarter : (x + 1) * quarter] for x in range(reps // 2) for v in (even, odd)],
         axis=1,
     ).astype(F32)
     return (back, whole, moment_out)

time: 283 us -> 272 us (0.961)
  waiting for transfers between devices: 92.2 us -> 87 us
  starting transfers between devices: 64.9 us -> 60.7 us
  other arithmetic: 40.6 us -> 37.6 us
    ppermute x20 -> x18, starting transfers between devices: 47.2 us -> 40.9 us  [start(): return lax.ppermute(self.last, axis, pairs)]
    ppermute x20 -> x18, waiting for transfers between devices: 49.5 us -> 44.4 us  [start(): return lax.ppermute(self.last, axis, pairs)]
    convert_element_type x4 -> x3, other arithmetic: 10.7 us -> 6.65 us  [the longest x1 3.68 us: shards(): synced_base = order.tie(synced_base.astype(BF16))]
    pallas_call x14 -> x13, Pallas kernels: 70.8 us -> 70.6 us  [call(): pl.pallas_call(body, grid_spec=pltpu.PrefetchScalarGridSpec(num_scalar_pr...]
  transfers between devices with their start and end apart: 27 -> 26, of which waited for: 11 -> 9; matrix products, arithmetic and copies ran while one was open for 9% -> 13% of each run, Pallas kernels for 23% -> 24%
where the time goes in v4:
time: 272 us; the launch traced here: 271 us
  waiting for transfers between devices  87 us (32%)
  Pallas kernels  70.6 us (26%)
  starting transfers between devices  60.7 us (22%)
  other arithmetic  37.6 us (14%)
  local copies, waits for them, and re-layouts  12.3 us (5%)
  between operations  2.88 us (1%)
    pallas_call x13, Pallas kernels, call(): pl.pallas_call(body, grid_spec=pltpu.PrefetchScalarGridSpec(num_scalar_pr...  70.6 us
    ppermute x18, waiting for transfers between devices, start(): return lax.ppermute(self.last, axis, pairs)  44.4 us
    ppermute x18, starting transfers between devices, start(): return lax.ppermute(self.last, axis, pairs)  40.9 us
    ppermute x1, waiting for transfers between devices, shards(): cot_other = [lax.ppermute(early, 'fsdp', across), None]  24.3 us
    ppermute x1, waiting for transfers between devices, shards(): lax.ppermute(pick(chunk_blocks(1) + column_blocks(second, other), 1), 'fs...  17 us
    all_to_all x1, starting transfers between devices, shards(): square = lax.all_to_all(square, 'fsdp', 0, 0, tiled=True)  9.2 us
    dynamic_slice x1, local copies, waits for them, and re-layouts, owned(): return lax.dynamic_slice(value, (0, r * quarter), (value.shape[0], quarter))  6.86 us
    convert_element_type x1, other arithmetic, update(): return (first_new / (jnp.sqrt(second_new) + ADAM_EPS)).astype(BF16)  6.58 us
  transfers between devices with their start and end apart: 26, of which 9 were waited for; matrix products, arithmetic and copies ran while one was open for 13% of the time, Pallas kernels for 24%

profile of v4, /device:TPU:0, one launch (start us, length us, event | category | flops | bytes accessed | tf_op | source)
XLA Modules:
  0.0 270.9 jit_solution(11033543184317488289)
XLA Ops:
  1.4 6.7 %shard_map.94 = (bf16[512,2048]{1,0:T(8,128)(2,1)}, bf16[512,1536]{1,0:T(8,128)(2,1)}, f32[512,1024]{1,0:T(8,128)}) custom-call(s32[5]{0:T(128)} %stack.89.at_ref, f32[512,2048]{1,0:T(8,128)} %bitcast.47, bf16[512,2048]{1,0:T(8,128)(2,1)} %refs_1_.9, bf16[512,2048]{1,0:T(8,128)(2,1)} %refs_1_.9, bf16[512,4096]{1,0:T(8,128)(2,1)} %x_ref.11, ...), custom_call_target="tpu_custom_call" | custom-call | bytes 23068672 | tf_op jit(solution)/shard_map/pallas_call | solution.py:34
  8.5 2.6 collective-permute-start
  14.6 2.7 %bitcast_add_fusion.1 = f32[512,512]{1,0:T(8,128)} fusion(f32[512,1024]{1,0:T(8,128)} %collective-permute-done.2, s32[]{:T(128)S(6)} %select_n.106, f32[1,512,2048]{2,1,0:T(8,128)} %param.9, s32[]{:T(128)S(6)} %select_n.105), kind=kLoop, calls=%fused_computation.37 | loop fusion | flops 262144 | bytes 3145736 | tf_op jit(solution)/shard_map/add | solution.py:377
  19.5 3.3 %shard_map.96 = bf16[512,1536]{1,0:T(8,128)(2,1)} custom-call(s32[3]{0:T(128)} %pad_add_fusion.2.at_ref, bf16[512,2048]{1,0:T(8,128)(2,1)} %refs_1_.9, bf16[512,2048]{1,0:T(8,128)(2,1)} %refs_1_.9, bf16[512,4096]{1,0:T(8,128)(2,1)} %x_ref.11), custom_call_target="tpu_custom_call" | custom-call | bytes 6291456 | tf_op jit(solution)/shard_map/pallas_call | solution.py:34
  24.3 24.3 %collective-permute-done.1.x_other_ref.refs_1_.refs_2_.refs_0_ = bf16[512,1536]{1,0:T(8,128)(2,1)S(1)} collective-permute-done((bf16[512,1536]{1,0:T(8,128)(2,1)}, bf16[512,1536]{1,0:T(8,128)(2,1)S(1)}, u32[]{:S(2)}, u32[]{:S(2)}) %collective-permute-start.1) | collective-permute-done | bytes 1572896 | tf_op jit(solution)/shard_map/ppermute | solution.py:367
  49.7 4.5 %shard_map.95 = bf16[512,1024]{1,0:T(8,128)(2,1)} custom-call(s32[2]{0:T(128)} %pad_add_fusion.1.at_ref, bf16[512,4096]{1,0:T(8,128)(2,1)} %x_ref.11, bf16[512,1536]{1,0:T(8,128)(2,1)} %copy-done, bf16[512,2048]{1,0:T(8,128)(2,1)} %refs_1_.9, bf16[512,1536]{1,0:T(8,128)(2,1)} %copy-done), custom_call_target="tpu_custom_call" | custom-call | flops 1073741824 | bytes 4194304 | tf_op jit(solution)/shard_map/pallas_call | solution.py:34
  61.6 2.9 %shard_map.97 = bf16[512,1024]{1,0:T(8,128)(2,1)} custom-call(s32[2]{0:T(128)} %pad_add_fusion.3.at_ref, bf16[512,4096]{1,0:T(8,128)(2,1)} %x_ref.11, bf16[512,4096]{1,0:T(8,128)(2,1)} %x_ref.11), custom_call_target="tpu_custom_call" | custom-call | bytes 4194304 | tf_op jit(solution)/shard_map/pallas_call | solution.py:34
  64.5 17.0 %collective-permute-done.5.refs_1_.x_other_ref.refs_3_ = bf16[512,1536]{1,0:T(8,128)(2,1)S(1)} collective-permute-done((bf16[512,1536]{1,0:T(8,128)(2,1)}, bf16[512,1536]{1,0:T(8,128)(2,1)S(1)}, u32[]{:S(2)}, u32[]{:S(2)}) %collective-permute-start.5) | collective-permute-done | bytes 1572896 | tf_op jit(solution)/shard_map/ppermute | solution.py:373
  82.7 4.5 %shard_map.98 = bf16[512,1024]{1,0:T(8,128)(2,1)} custom-call(s32[2]{0:T(128)} %pad_add_fusion.1.at_ref, bf16[512,4096]{1,0:T(8,128)(2,1)} %x_ref.11, bf16[512,1536]{1,0:T(8,128)(2,1)} %copy-done, bf16[512,2048]{1,0:T(8,128)(2,1)} %refs_1_.9, bf16[512,1536]{1,0:T(8,128)(2,1)} %copy-done.1), custom_call_target="tpu_custom_call" | custom-call | flops 1073741824 | bytes 4194304 | tf_op jit(solution)/shard_map/pallas_call | solution.py:34
  87.2 2.2 collective-permute-start.7
  91.5 6.5 %shard_map.99 = bf16[512,2048]{1,0:T(8,128)(2,1)} custom-call(s32[2]{0:T(128)} %pad_add_fusion.at_ref, bf16[512,4096]{1,0:T(8,128)(2,1)} %x_ref.11, bf16[512,1536]{1,0:T(8,128)(2,1)} %copy-done.1, bf16[512,2048]{1,0:T(8,128)(2,1)} %refs_1_.9, bf16[512,2048]{1,0:T(8,128)(2,1)} %refs_1_.9, bf16[512,1536]{1,0:T(8,128)(2,1)} %copy-done, bf16[512,1536]{1,0:T(8,128)(2,1)} %copy-done.1), custom_call_target="tpu_custom_call" | custom-call | flops 2147483648 | bytes 8388608 | tf_op jit(solution)/shard_map/pallas_call | solution.py:34
  98.0 2.7 collective-permute-start.13
  100.7 12.5 %collective-permute-done.7 = bf16[512,1024]{1,0:T(8,128)(2,1)S(1)} collective-permute-done((bf16[512,1024]{1,0:T(8,128)(2,1)}, bf16[512,1024]{1,0:T(8,128)(2,1)S(1)}, u32[]{:S(2)}, u32[]{:S(2)}) %collective-permute-start.7) | collective-permute-done | bytes 1048608 | tf_op jit(solution)/shard_map/ppermute | solution.py:299
  121.7 13.6 %shard_map.100 = (bf16[512,4096]{1,0:T(8,128)(2,1)}, bf16[512,1536]{1,0:T(8,128)(2,1)}) custom-call(s32[3]{0:T(128)} %pad_add_fusion.5.at_ref, bf16[512,2048]{1,0:T(8,128)(2,1)} %refs_1_.9, bf16[512,1536]{1,0:T(8,128)(2,1)} %copy-done, bf16[512,1536]{1,0:T(8,128)(2,1)} %copy-done.1, bf16[512,2048]{1,0:T(8,128)(2,1)} %get-tuple-element.67.refs_2_, ...), custom_call_target="tpu_custom_call" | custom-call | flops 6442450944 | bytes 23068672 | tf_op jit(solution)/shard_map/pallas_call | solution.py:34
  135.2 3.8 %collective-permute-done.10.x_other_ref = bf16[512,1024]{1,0:T(8,128)(2,1)S(1)} collective-permute-done((bf16[512,1024]{1,0:T(8,128)(2,1)S(1)}, bf16[512,1024]{1,0:T(8,128)(2,1)S(1)}, u32[]{:S(2)}, u32[]{:S(2)}) %collective-permute-start.10) | collective-permute-done | bytes 1048608 | tf_op jit(solution)/shard_map/ppermute | solution.py:299
  141.4 5.0 %shard_map.101 = bf16[512,1024]{1,0:T(8,128)(2,1)} custom-call(s32[2]{0:T(128)} %pad_add_fusion.4.at_ref, bf16[512,4096]{1,0:T(8,128)(2,1)} %x_ref.11, bf16[512,1024]{1,0:T(8,128)(2,1)} %copy-done.2, bf16[512,2048]{1,0:T(8,128)(2,1)} %refs_1_.9, bf16[512,1536]{1,0:T(8,128)(2,1)} %copy-done, bf16[512,1024]{1,0:T(8,128)(2,1)} %collective-permute-done.14.refs_2_), custom_call_target="tpu_custom_call" | custom-call | flops 1073741824 | bytes 4194304 | tf_op jit(solution)/shard_map/pallas_call | solution.py:34
  146.4 9.1 %collective-permute-start.17 = (bf16[512,1024]{1,0:T(8,128)(2,1)}, bf16[512,1024]{1,0:T(8,128)(2,1)}, u32[]{:S(2)}, u32[]{:S(2)}) collective-permute-start(bf16[512,1024]{1,0:T(8,128)(2,1)} %shard_map.101), channel_id=1, source_target_pairs={{0,2},{1,3},{2,0},{3,1},{4,6},{5,7},{6,4},{7,5},{8,10},{9,11},{10,... | collective-permute-start | bytes 3145736 | tf_op jit(solution)/shard_map/ppermute | solution.py:299
  155.6 2.6 collective-permute-done.13
  165.0 4.9 %shard_map.102 = bf16[512,1024]{1,0:T(8,128)(2,1)} custom-call(s32[2]{0:T(128)} %pad_add_fusion.4.at_ref, bf16[512,4096]{1,0:T(8,128)(2,1)} %x_ref.11, bf16[512,1024]{1,0:T(8,128)(2,1)} %copy-done.2, bf16[512,2048]{1,0:T(8,128)(2,1)} %refs_1_.9, bf16[512,1536]{1,0:T(8,128)(2,1)} %copy-done.1, bf16[512,1024]{1,0:T(8,128)(2,1)} %collective-permute-done.12.refs_2_), custom_call_target="tpu_custom_call" | custom-call | flops 1073741824 | bytes 4194304 | tf_op jit(solution)/shard_map/pallas_call | solution.py:34
  169.9 9.3 %collective-permute-start.21 = (bf16[512,1024]{1,0:T(8,128)(2,1)}, bf16[512,1024]{1,0:T(8,128)(2,1)}, u32[]{:S(2)}, u32[]{:S(2)}) collective-permute-start(bf16[512,1024]{1,0:T(8,128)(2,1)} %shard_map.102), channel_id=1, source_target_pairs={{0,2},{1,3},{2,0},{3,1},{4,6},{5,7},{6,4},{7,5},{8,10},{9,11},{10,... | collective-permute-start | bytes 3145736 | tf_op jit(solution)/shard_map/ppermute | solution.py:299
  179.1 3.7 %subtract_convert_fusion.1 = (bf16[512,512]{1,0:T(8,128)(2,1)}, f32[512,512]{1,0:T(8,128)}) fusion(f32[512,512]{1,0:T(8,128)S(1)} %copy-done.11, f32[512,512]{1,0:T(8,128)S(1)} %copy-done.5, f32[512,512]{1,0:T(8,128)} %collective-permute-done.3, f32[512,1024]{1,0:T(8,128)} %collective-permute-done.2, s32[]{:T(128)S(6)} %select_n.111, ...), kind=kLoop, calls=%fused_computation.46 | loop fusion | flops 2883584 | bytes 6815752 | tf_op jit(solution)/shard_map/convert_element_type | solution.py:464
  182.8 6.4 %shard_map.103 = (bf16[512,4096]{1,0:T(8,128)(2,1)}, bf16[512,512]{1,0:T(8,128)(2,1)}) custom-call(s32[1]{0:T(128)} %bitcast.15.at_ref, bf16[512,2048]{1,0:T(8,128)(2,1)} %refs_1_.9, bf16[512,1536]{1,0:T(8,128)(2,1)} %copy-done, bf16[512,1536]{1,0:T(8,128)(2,1)} %copy-done.1, ...), custom_call_target="tpu_custom_call", output_to_operand_aliasing={{0}: (6, {})} | custom-call | flops 2147483648 | bytes 18874368 | tf_op jit(solution)/shard_map/pallas_call | solution.py:34
  189.8 6.3 %shard_map.106 = (f32[512,1024]{1,0:T(8,128)}, f32[512,1024]{1,0:T(8,128)}) custom-call(s32[2]{0:T(128)} %pad_add_fusion.7.at_ref, bf16[512,4096]{1,0:T(8,128)(2,1)} %x_ref.11, bf16[512,1024]{1,0:T(8,128)(2,1)} %copy-done.2, bf16[512,2048]{1,0:T(8,128)(2,1)} %refs_1_.9, bf16[512,2048]{1,0:T(8,128)(2,1)} %refs_1_.9, bf16[512,1536]{1,0:T(8,128)(2,1)} %copy-done, ...), custom_call_target="tpu_custom_call" | custom-call | flops 2147483648 | bytes 16777216 | tf_op jit(solution)/shard_map/pallas_call | solution.py:34
  196.1 4.2 %shard_map.104.held_ref = bf16[512,4096]{1,0:T(8,128)(2,1)} custom-call(s32[3]{0:T(128)} %pad_add_fusion.6.at_ref, bf16[512,1536]{1,0:T(8,128)(2,1)} %collective-permute-done.18.came_ref, bf16[512,4096]{1,0:T(8,128)(2,1)} %get-tuple-element.110.held_ref), custom_call_target="tpu_custom_call", output_to_operand_aliasing={{}: (2, {})} | custom-call | bytes 16777216 | tf_op jit(solution)/shard_map/pallas_call | solution.py:34
  201.9 2.4 multiply_reduce_fusion.1
  206.9 3.4 %multiply_reduce_fusion = f32[]{:T(128)} fusion(bf16[512,1024]{1,0:T(8,128)(2,1)} %collective-permute-done.20, f32[512,1024]{1,0:T(8,128)} %get-tuple-element.122, bf16[512,1024]{1,0:T(8,128)(2,1)} %collective-permute-done.21), kind=kLoop, calls=%fused_computation.20 | loop fusion | flops 3670015 | bytes 4194308 | tf_op jit(solution)/shard_map/reduce_sum | solution.py:459
  212.2 9.2 %all-to-all-start = ((f32[8,1,128]{2,1,0:T(1,128)}), f32[8,1,128]{2,1,0:T(1,128)S(1)}, u32[]{:S(2)}, u32[]{:S(2)}) async-start(f32[8,1,128]{2,1,0:T(1,128)} %broadcast_in_dim.3), calls=%async_computation | async-start | bytes 8192 | tf_op jit(solution)/shard_map/all_to_all | solution.py:470
  221.4 6.9 %dynamic-slice_bitcast_fusion.1 = (f32[512,512]{1,0:T(8,128)}, f32[512,512]{1,0:T(8,128)}, f32[512,512]{1,0:T(8,128)}, f32[512,512]{1,0:T(8,128)}, f32[512,512]{...) fusion(f32[1,512,2048]{2,1,0:T(8,128)} %param.11, s32[]{:T(128)S(6)} %select_n.118, ...), kind=kLoop, calls=%fused_computation.39 | loop fusion | bytes 16777232 | tf_op jit(solution)/shard_map/dynamic_slice | solution.py:345
  229.6 6.6 %fusion.10 = (bf16[512,1024]{1,0:T(8,128)(2,1)S(1)}, bf16[512,1024]{1,0:T(8,128)(2,1)S(1)}) fusion(f32[512,512]{1,0:T(8,128)} %get-tuple-element.142, f32[512,512]{1,0:T(8,128)} %get-tuple-element.139, f32[512,512]{1,0:T(8,128)} %get-tuple-element.159, f32[512,512]{1,0:T(8,128)} %get-tuple-element.162, f32[]{:T(128)S(6)} %min.3, pred[]{:T(512)S(6)} %eq.17, ...), kind=kLoop, calls=%fused_computation.26 | loop fusion | flops 19922944 | bytes 18874374 | tf_op jit(solution)/shard_map/convert_element_type | solution.py:482
  236.3 2.6 collective-permute-done.22
  242.2 22.4 %collective-permute-done.23 = bf16[512,1024]{1,0:T(8,128)(2,1)S(1)} collective-permute-done((bf16[512,1024]{1,0:T(8,128)(2,1)S(1)}, bf16[512,1024]{1,0:T(8,128)(2,1)S(1)}, u32[]{:S(2)}, u32[]{:S(2)}) %collective-permute-start.23) | collective-permute-done | bytes 1048608 | tf_op jit(solution)/shard_map/ppermute | solution.py:299
  268.4 2.6 maximum_convert_fusion
  (88 shorter events, 50.7 us)
Async XLA Ops:
  8.0 6.6 %collective-permute-start.2 = (f32[512,1024]{1,0:T(8,128)}, f32[512,1024]{1,0:T(8,128)}, u32[]{:S(2)}, u32[]{:S(2)}) collective-permute-start(f32[512,1024]{1,0:T(8,128)} %get-tuple-element.69), channel_id=1, source_target_pairs={{0,8},{8,0},{16,24},{24,16},{1,9},{9,1},{17,25},{25,17},{2,10},{10... | collective-permute-start | bytes 6291464 | tf_op jit(solution)/shard_map/ppermute | solution.py:371
  8.5 49.2 %collective-permute-start = (bf16[512,2048]{1,0:T(8,128)(2,1)}, bf16[512,2048]{1,0:T(8,128)(2,1)}, u32[]{:S(2)}, u32[]{:S(2)}) collective-permute-start(bf16[512,2048]{1,0:T(8,128)(2,1)} %get-tuple-element.67.refs_2_), channel_id=1, source_target_pairs={{0,2},{1,3},{2,0},{3,1},{4,6},{5,7},{6,4},{7,5},{8,10},{9,11},{10,... | collective-permute-start | bytes 6291464 | tf_op jit(solution)/shard_map/ppermute | solution.py:365
  11.1 37.4 %collective-permute-start.1 = (bf16[512,1536]{1,0:T(8,128)(2,1)}, bf16[512,1536]{1,0:T(8,128)(2,1)S(1)}, u32[]{:S(2)}, u32[]{:S(2)}) collective-permute-start(bf16[512,1536]{1,0:T(8,128)(2,1)} %get-tuple-element.68), channel_id=1, source_target_pairs={{0,1},{1,0},{2,3},{3,2},{4,5},{5,4},{6,7},{7,6},{8,9},{9,8},{10,11... | collective-permute-start | bytes 4718600 | tf_op jit(solution)/shard_map/ppermute | solution.py:367
  12.6 47.0 %collective-permute-start.6 = (bf16[512,2048]{1,0:T(8,128)(2,1)}, bf16[512,2048]{1,0:T(8,128)(2,1)}, u32[]{:S(2)}, u32[]{:S(2)}) collective-permute-start(bf16[512,2048]{1,0:T(8,128)(2,1)} %get-tuple-element.67.refs_2_), channel_id=1, source_target_pairs={{2,4},{3,5},{4,2},{5,3},{10,12},{11,13},{12,10},{13,11},{18,20},{1... | collective-permute-start | bytes 6291464 | tf_op jit(solution)/shard_map/ppermute | solution.py:366
  17.3 40.3 %collective-permute-start.3 = (f32[512,512]{1,0:T(8,128)}, f32[512,512]{1,0:T(8,128)}, u32[]{:S(2)}, u32[]{:S(2)}) collective-permute-start(f32[512,512]{1,0:T(8,128)} %bitcast_add_fusion.1), channel_id=1, source_target_pairs={{0,16},{8,24},{16,0},{24,8},{1,17},{9,25},{17,1},{25,9},{2,18},{10... | collective-permute-start | bytes 3145736 | tf_op jit(solution)/shard_map/ppermute | solution.py:379
  22.8 58.7 %collective-permute-start.5 = (bf16[512,1536]{1,0:T(8,128)(2,1)}, bf16[512,1536]{1,0:T(8,128)(2,1)S(1)}, u32[]{:S(2)}, u32[]{:S(2)}) collective-permute-start(bf16[512,1536]{1,0:T(8,128)(2,1)} %shard_map.96), channel_id=1, source_target_pairs={{0,1},{1,0},{2,3},{3,2},{4,5},{5,4},{6,7},{7,6},{8,9},{9,8},{10,11... | collective-permute-start | bytes 4718600 | tf_op jit(solution)/shard_map/ppermute | solution.py:373
  54.3 35.2 %collective-permute-start.8 = (bf16[512,1024]{1,0:T(8,128)(2,1)}, bf16[512,1024]{1,0:T(8,128)(2,1)S(1)}, u32[]{:S(2)}, u32[]{:S(2)}) collective-permute-start(bf16[512,1024]{1,0:T(8,128)(2,1)} %shard_map.95), channel_id=1, source_target_pairs={{0,2},{1,3},{6,4},{7,5},{8,10},{9,11},{14,12},{15,13},{16,18},{17,... | collective-permute-start | bytes 3145736 | tf_op jit(solution)/shard_map/ppermute | solution.py:299
  57.7 57.0 %collective-permute-start.4 = (bf16[512,2048]{1,0:T(8,128)(2,1)}, bf16[512,2048]{1,0:T(8,128)(2,1)}, u32[]{:S(2)}, u32[]{:S(2)}) collective-permute-start(bf16[512,2048]{1,0:T(8,128)(2,1)} %collective-permute-done.refs_3_), channel_id=1, source_target_pairs={{2,4},{3,5},{4,2},{5,3},{10,12},{11,13},{12,10},{13,11},{18,20},{1... | collective-permute-start | bytes 6291464 | tf_op jit(solution)/shard_map/ppermute | solution.py:299
  59.7 59.7 %collective-permute-start.11 = (bf16[512,2048]{1,0:T(8,128)(2,1)}, bf16[512,2048]{1,0:T(8,128)(2,1)}, u32[]{:S(2)}, u32[]{:S(2)}) collective-permute-start(bf16[512,2048]{1,0:T(8,128)(2,1)} %collective-permute-done.6.refs_4_), channel_id=1, source_target_pairs={{2,0},{3,1},{4,6},{5,7},{10,8},{11,9},{12,14},{13,15},{18,16},{19,... | collective-permute-start | bytes 6291464 | tf_op jit(solution)/shard_map/ppermute | solution.py:299
  64.5 24.9 %copy-start.8 = (bf16[512,1024]{1,0:T(8,128)(2,1)S(1)}, bf16[512,1024]{1,0:T(8,128)(2,1)}, u32[]{:S(2)}) copy-start(bf16[512,1024]{1,0:T(8,128)(2,1)} %shard_map.95) | copy-start | bytes 3145732
  87.2 26.1 %collective-permute-start.7 = (bf16[512,1024]{1,0:T(8,128)(2,1)}, bf16[512,1024]{1,0:T(8,128)(2,1)S(1)}, u32[]{:S(2)}, u32[]{:S(2)}) collective-permute-start(bf16[512,1024]{1,0:T(8,128)(2,1)} %shard_map.98), channel_id=1, source_target_pairs={{0,2},{1,3},{6,4},{7,5},{8,10},{9,11},{14,12},{15,13},{16,18},{17,... | collective-permute-start | bytes 3145736 | tf_op jit(solution)/shard_map/ppermute | solution.py:299
  91.5 21.7 %copy-start.9 = (bf16[512,1024]{1,0:T(8,128)(2,1)S(1)}, bf16[512,1024]{1,0:T(8,128)(2,1)}, u32[]{:S(2)}) copy-start(bf16[512,1024]{1,0:T(8,128)(2,1)} %shard_map.98) | copy-start | bytes 3145732
  98.0 18.0 %copy-start.10 = (bf16[512,1024]{1,0:T(8,128)(2,1)S(1)}, bf16[512,1024]{1,0:T(8,128)(2,1)}, u32[]{:S(2)}) copy-start(bf16[512,1024]{1,0:T(8,128)(2,1)} %shard_map.97) | copy-start | bytes 3145732
  98.0 60.2 %collective-permute-start.13 = (bf16[512,2048]{1,0:T(8,128)(2,1)}, bf16[512,2048]{1,0:T(8,128)(2,1)}, u32[]{:S(2)}, u32[]{:S(2)}) collective-permute-start(bf16[512,2048]{1,0:T(8,128)(2,1)} %shard_map.99), channel_id=1, source_target_pairs={{0,2},{1,3},{6,4},{7,5},{8,10},{9,11},{14,12},{15,13},{16,18},{17,... | collective-permute-start | bytes 6291464 | tf_op jit(solution)/shard_map/ppermute | solution.py:299
  114.7 55.2 %collective-permute-start.9 = (bf16[512,2048]{1,0:T(8,128)(2,1)}, bf16[512,2048]{1,0:T(8,128)(2,1)}, u32[]{:S(2)}, u32[]{:S(2)}) collective-permute-start(bf16[512,2048]{1,0:T(8,128)(2,1)} %collective-permute-done.4.refs_2_), channel_id=1, source_target_pairs={{2,0},{3,1},{4,6},{5,7},{10,8},{11,9},{12,14},{13,15},{18,16},{19,... | collective-permute-start | bytes 6291464 | tf_op jit(solution)/shard_map/ppermute | solution.py:299
  116.0 23.1 %collective-permute-start.10 = (bf16[512,1024]{1,0:T(8,128)(2,1)S(1)}, bf16[512,1024]{1,0:T(8,128)(2,1)S(1)}, u32[]{:S(2)}, u32[]{:S(2)}) collective-permute-start(bf16[512,1024]{1,0:T(8,128)(2,1)S(1)} %copy-done.10), channel_id=1, source_target_pairs={{0,1},{1,0},{2,3},{3,2},{4,5},{5,4},{6,7},{7,6},{8,9},{9,8},{10,11... | collective-permute-start | bytes 3145736 | tf_op jit(solution)/shard_map/ppermute | solution.py:299
  117.7 23.7 %collective-permute-start.14 = (bf16[512,1024]{1,0:T(8,128)(2,1)}, bf16[512,1024]{1,0:T(8,128)(2,1)}, u32[]{:S(2)}, u32[]{:S(2)}) collective-permute-start(bf16[512,1024]{1,0:T(8,128)(2,1)} %add_convert_fusion.2), channel_id=1, source_target_pairs={{2,4},{3,5},{4,2},{5,3},{10,12},{11,13},{12,10},{13,11},{18,20},{1... | collective-permute-start | bytes 3145736 | tf_op jit(solution)/shard_map/ppermute | solution.py:299
  119.4 43.8 %collective-permute-start.12 = (bf16[512,1024]{1,0:T(8,128)(2,1)}, bf16[512,1024]{1,0:T(8,128)(2,1)}, u32[]{:S(2)}, u32[]{:S(2)}) collective-permute-start(bf16[512,1024]{1,0:T(8,128)(2,1)} %add_convert_fusion.1), channel_id=1, source_target_pairs={{2,4},{3,5},{4,2},{5,3},{10,12},{11,13},{12,10},{13,11},{18,20},{1... | collective-permute-start | bytes 3145736 | tf_op jit(solution)/shard_map/ppermute | solution.py:299
  139.0 50.1 %collective-permute-start.18 = (bf16[512,1536]{1,0:T(8,128)(2,1)}, bf16[512,1536]{1,0:T(8,128)(2,1)}, u32[]{:S(2)}, u32[]{:S(2)}) collective-permute-start(bf16[512,1536]{1,0:T(8,128)(2,1)} %get-tuple-element.95), channel_id=1, source_target_pairs={{0,1},{1,0},{2,3},{3,2},{4,5},{5,4},{6,7},{7,6},{8,9},{9,8},{10,11... | collective-permute-start | bytes 4718600 | tf_op jit(solution)/shard_map/ppermute | solution.py:299
  141.4 16.8 %copy-start.3 = (bf16[512,2048]{1,0:T(8,128)(2,1)S(1)}, bf16[512,2048]{1,0:T(8,128)(2,1)}, u32[]{:S(2)}) copy-start(bf16[512,2048]{1,0:T(8,128)(2,1)} %shard_map.99) | copy-start | bytes 6291460
  146.4 53.9 %collective-permute-start.17 = (bf16[512,1024]{1,0:T(8,128)(2,1)}, bf16[512,1024]{1,0:T(8,128)(2,1)}, u32[]{:S(2)}, u32[]{:S(2)}) collective-permute-start(bf16[512,1024]{1,0:T(8,128)(2,1)} %shard_map.101), channel_id=1, source_target_pairs={{0,2},{1,3},{2,0},{3,1},{4,6},{5,7},{6,4},{7,5},{8,10},{9,11},{10,... | collective-permute-start | bytes 3145736 | tf_op jit(solution)/shard_map/ppermute | solution.py:299
  161.9 38.4 %collective-permute-start.16 = (bf16[512,1024]{1,0:T(8,128)(2,1)}, bf16[512,1024]{1,0:T(8,128)(2,1)S(1)}, u32[]{:S(2)}, u32[]{:S(2)}) collective-permute-start(bf16[512,1024]{1,0:T(8,128)(2,1)} %get-tuple-element.100), channel_id=1, source_target_pairs={{2,4},{3,5},{4,2},{5,3},{10,12},{11,13},{12,10},{13,11},{18,20},{1... | collective-permute-start | bytes 3145736 | tf_op jit(solution)/shard_map/ppermute | solution.py:299
  163.2 15.9 %copy-start.5 = (f32[512,512]{1,0:T(8,128)S(1)}, f32[512,512]{1,0:T(8,128)}, u32[]{:S(2)}) copy-start(f32[512,512]{1,0:T(8,128)} %param.13) | copy-start | bytes 3145732
  163.2 15.9 %copy-start.11 = (f32[512,512]{1,0:T(8,128)S(1)}, f32[512,512]{1,0:T(8,128)}, u32[]{:S(2)}) copy-start(f32[512,512]{1,0:T(8,128)} %param.12) | copy-start | bytes 3145732
  163.2 43.7 %collective-permute-start.20 = (bf16[512,1024]{1,0:T(8,128)(2,1)}, bf16[512,1024]{1,0:T(8,128)(2,1)}, u32[]{:S(2)}, u32[]{:S(2)}) collective-permute-start(bf16[512,1024]{1,0:T(8,128)(2,1)} %get-tuple-element.101), channel_id=1, source_target_pairs={{2,4},{3,5},{4,2},{5,3},{10,12},{11,13},{12,10},{13,11},{18,20},{1... | collective-permute-start | bytes 3145736 | tf_op jit(solution)/shard_map/ppermute | solution.py:299
  169.9 37.1 %collective-permute-start.21 = (bf16[512,1024]{1,0:T(8,128)(2,1)}, bf16[512,1024]{1,0:T(8,128)(2,1)}, u32[]{:S(2)}, u32[]{:S(2)}) collective-permute-start(bf16[512,1024]{1,0:T(8,128)(2,1)} %shard_map.102), channel_id=1, source_target_pairs={{0,2},{1,3},{2,0},{3,1},{4,6},{5,7},{6,4},{7,5},{8,10},{9,11},{10,... | collective-permute-start | bytes 3145736 | tf_op jit(solution)/shard_map/ppermute | solution.py:299
  189.2 15.1 %collective-permute-start.15 = (bf16[512,512]{1,0:T(8,128)(2,1)}, bf16[512,512]{1,0:T(8,128)(2,1)S(1)}, u32[]{:S(2)}, u32[]{:S(2)}) collective-permute-start(bf16[512,512]{1,0:T(8,128)(2,1)} %get-tuple-element.108), channel_id=1, source_target_pairs={{0,1},{1,0},{2,3},{3,2},{4,5},{5,4},{6,7},{7,6},{8,9},{9,8},{10,11... | collective-permute-start | bytes 1572872 | tf_op jit(solution)/shard_map/ppermute | solution.py:299
  200.3 28.0 %collective-permute-start.19 = (bf16[512,512]{1,0:T(8,128)(2,1)}, bf16[512,512]{1,0:T(8,128)(2,1)}, u32[]{:S(2)}, u32[]{:S(2)}) collective-permute-start(bf16[512,512]{1,0:T(8,128)(2,1)} %get-tuple-element.116), channel_id=1, source_target_pairs={{0,16},{8,24},{16,0},{24,8},{1,17},{9,25},{17,1},{25,9},{2,18},{10... | collective-permute-start | bytes 1572872 | tf_op jit(solution)/shard_map/ppermute | solution.py:465
  212.2 16.1 %all-to-all-start = ((f32[8,1,128]{2,1,0:T(1,128)}), f32[8,1,128]{2,1,0:T(1,128)S(1)}, u32[]{:S(2)}, u32[]{:S(2)}) async-start(f32[8,1,128]{2,1,0:T(1,128)} %broadcast_in_dim.3), calls=%async_computation | async-start | bytes 8192 | tf_op jit(solution)/shard_map/all_to_all | solution.py:470
  236.2 2.7 %collective-permute-start.22 = (bf16[512,1024]{1,0:T(8,128)(2,1)S(1)}, bf16[512,1024]{1,0:T(8,128)(2,1)S(1)}, u32[]{:S(2)}, u32[]{:S(2)}) collective-permute-start(bf16[512,1024]{1,0:T(8,128)(2,1)S(1)} %get-tuple-element.125), channel_id=1, source_target_pairs={{0,8},{8,0},{16,24},{24,16},{1,9},{9,1},{17,25},{25,17},{2,10},{10... | collective-permute-start | bytes 3145736 | tf_op jit(solution)/shard_map/ppermute | solution.py:299
  239.3 25.3 %collective-permute-start.23 = (bf16[512,1024]{1,0:T(8,128)(2,1)S(1)}, bf16[512,1024]{1,0:T(8,128)(2,1)S(1)}, u32[]{:S(2)}, u32[]{:S(2)}) collective-permute-start(bf16[512,1024]{1,0:T(8,128)(2,1)S(1)} %add_convert_fusion), channel_id=1, source_target_pairs={{0,16},{8,24},{16,0},{24,8},{1,17},{9,25},{17,1},{25,9},{2,18},{10... | collective-permute-start | bytes 3145736 | tf_op jit(solution)/shard_map/ppermute | solution.py:299
  265.2 2.7 %collective-permute-start.24 = (bf16[512,1024]{1,0:T(8,128)(2,1)S(1)}, bf16[512,1024]{1,0:T(8,128)(2,1)S(1)}, u32[]{:S(2)}, u32[]{:S(2)}) collective-permute-start(bf16[512,1024]{1,0:T(8,128)(2,1)S(1)} %get-tuple-element.129), channel_id=1, source_target_pairs={{0,8},{8,0},{16,24},{24,16},{1,9},{9,1},{17,25},{25,17},{2,10},{10... | collective-permute-start | bytes 3145736 | tf_op jit(solution)/shard_map/ppermute | solution.py:299
  (7 other events, 14.0 us)

commit v5 on v4

--- a/solution.py
+++ b/solution.py
@@ -470,22 +470,26 @@
     square = lax.all_to_all(square, "fsdp", 0, 0, tiled=True)
     factor = jnp.minimum(1.0, 1.0 / (jnp.sqrt(jnp.sum(square[:, 0])) + 1e-06))
 
-    def update(parity):
-        quarters = [2 * x + parity for x in range(reps // 2)]
-        first, second_moment = (
-            jnp.concatenate([owned(v[0], q) for q in quarters], axis=1)
-            for v in (adam_first, adam_second)
-        )
-        clipped = jnp.where(parity == 0, gradient[0], gradient[1]) * factor
+    def update(parity, x):
+        first, second_moment = (owned(v[0], 2 * x + parity) for v in (adam_first, adam_second))
+        mine = [owned(g, x) for g in gradient]
+        clipped = jnp.where(parity == 0, mine[0], mine[1]) * factor
         first_new = BETA_ONE * first + (1.0 - BETA_ONE) * clipped
         second_new = BETA_TWO * second_moment + (1.0 - BETA_TWO) * clipped * clipped
         return (first_new / (jnp.sqrt(second_new) + ADAM_EPS)).astype(BF16)
 
-    u_mate, u_own = lax.optimization_barrier((update(1 - core), update(core)))
-    u_mate = start(u_mate, swap[1], "rep")
-    u_mate = done(u_mate)
-    u_chip = (u_own.astype(F32) + u_mate.astype(F32)).astype(BF16)
-    u_x = done(start(u_chip, swap[2], "rep"))
+    u_mate, u_own = [], []
+    for x in range(reps // 2):
+        pair = lax.optimization_barrier((update(1 - core, x), update(core, x)))
+        u_mate.append(start(pair[0], swap[1], "rep"))
+        u_own.append(pair[1])
+    u_chip, u_x = [], []
+    for x in range(reps // 2):
+        came = done(u_mate[x])
+        u_chip.append((u_own[x].astype(F32) + came.astype(F32)).astype(BF16))
+        u_x.append(start(u_chip[x], swap[2], "rep"))
+    u_chip = jnp.concatenate(u_chip, axis=1)
+    u_x = jnp.concatenate([done(v) for v in u_x], axis=1)
     update_sum = u_chip.astype(F32) + u_x.astype(F32)
     scale = RATE_INNER / reps
     moment_out = moment_base + scale * jnp.where(

time: 272 us -> 270 us (level)
  local copies, waits for them, and re-layouts: 12.3 us -> 5.26 us
  waiting for transfers between devices: 87 us -> 91.7 us
    dynamic_slice x1 -> x0, local copies, waits for them, and re-layouts: 6.86 us -> none  [owned(): return lax.dynamic_slice(value, (0, r * quarter), (value.shape[0], quarter))]
    all_to_all x1, waiting for transfers between devices: 0.01 us -> 6.38 us  [shards(): square = lax.all_to_all(square, 'fsdp', 0, 0, tiled=True)]
    ppermute x18 -> x20, waiting for transfers between devices: 44.4 us -> 42.6 us  [start(): return lax.ppermute(self.last, axis, pairs)]
    ppermute x18 -> x20, starting transfers between devices: 40.9 us -> 42.1 us  [start(): return lax.ppermute(self.last, axis, pairs)]
  transfers between devices with their start and end apart: 26 -> 28, of which waited for: 9 -> 11; matrix products, arithmetic and copies ran while one was open for 13% -> 11% of each run, Pallas kernels for 24% -> 24%
where the time goes in v5:
time: 270 us; the launch traced here: 269 us
  waiting for transfers between devices  91.7 us (34%)
  Pallas kernels  70.4 us (26%)
  starting transfers between devices  60.8 us (23%)
  other arithmetic  38.3 us (14%)
  local copies, waits for them, and re-layouts  5.26 us (2%)
  between operations  2.85 us (1%)
    pallas_call x13, Pallas kernels, call(): pl.pallas_call(body, grid_spec=pltpu.PrefetchScalarGridSpec(num_scalar_pr...  70.4 us
    ppermute x20, waiting for transfers between devices, start(): return lax.ppermute(self.last, axis, pairs)  42.6 us
    ppermute x20, starting transfers between devices, start(): return lax.ppermute(self.last, axis, pairs)  42.1 us
    ppermute x1, waiting for transfers between devices, shards(): cot_other = [lax.ppermute(early, 'fsdp', across), None]  24.4 us
    ppermute x1, waiting for transfers between devices, shards(): lax.ppermute(pick(chunk_blocks(1) + column_blocks(second, other), 1), 'fs...  17 us
    all_to_all x1, starting transfers between devices, shards(): square = lax.all_to_all(square, 'fsdp', 0, 0, tiled=True)  8.23 us
    reduce_sum x2, other arithmetic, shards(): squares.append(jnp.sum(gradient[c] * gradient[c]))  8.08 us
    all_to_all x1, waiting for transfers between devices, shards(): square = lax.all_to_all(square, 'fsdp', 0, 0, tiled=True)  6.38 us
  transfers between devices with their start and end apart: 28, of which 11 were waited for; matrix products, arithmetic and copies ran while one was open for 11% of the time, Pallas kernels for 24%

profile of v5, /device:TPU:0, one launch (start us, length us, event | category | flops | bytes accessed | tf_op | source)
XLA Modules:
  0.0 269.3 jit_solution(16581376606214041869)
XLA Ops:
  1.4 6.7 %shard_map.94 = (bf16[512,2048]{1,0:T(8,128)(2,1)}, bf16[512,1536]{1,0:T(8,128)(2,1)}, f32[512,1024]{1,0:T(8,128)}) custom-call(s32[5]{0:T(128)} %stack.89.at_ref, f32[512,2048]{1,0:T(8,128)} %bitcast.71, bf16[512,2048]{1,0:T(8,128)(2,1)} %refs_1_.9, bf16[512,2048]{1,0:T(8,128)(2,1)} %refs_1_.9, bf16[512,4096]{1,0:T(8,128)(2,1)} %x_ref.11, ...), custom_call_target="tpu_custom_call" | custom-call | bytes 23068672 | tf_op jit(solution)/shard_map/pallas_call | solution.py:34
  8.5 2.6 collective-permute-start
  14.6 2.7 %bitcast_add_fusion.5 = f32[512,512]{1,0:T(8,128)} fusion(f32[512,1024]{1,0:T(8,128)} %collective-permute-done.2, s32[]{:T(128)S(6)} %select_n.114, f32[1,512,2048]{2,1,0:T(8,128)} %param.9, s32[]{:T(128)S(6)} %select_n.113), kind=kLoop, calls=%fused_computation.42 | loop fusion | flops 262144 | bytes 3145736 | tf_op jit(solution)/shard_map/add | solution.py:377
  19.4 3.3 %shard_map.96 = bf16[512,1536]{1,0:T(8,128)(2,1)} custom-call(s32[3]{0:T(128)} %pad_add_fusion.2.at_ref, bf16[512,2048]{1,0:T(8,128)(2,1)} %refs_1_.9, bf16[512,2048]{1,0:T(8,128)(2,1)} %refs_1_.9, bf16[512,4096]{1,0:T(8,128)(2,1)} %x_ref.11), custom_call_target="tpu_custom_call" | custom-call | bytes 6291456 | tf_op jit(solution)/shard_map/pallas_call | solution.py:34
  24.2 24.4 %collective-permute-done.1.x_other_ref.refs_1_.refs_2_.refs_0_ = bf16[512,1536]{1,0:T(8,128)(2,1)S(1)} collective-permute-done((bf16[512,1536]{1,0:T(8,128)(2,1)}, bf16[512,1536]{1,0:T(8,128)(2,1)S(1)}, u32[]{:S(2)}, u32[]{:S(2)}) %collective-permute-start.1) | collective-permute-done | bytes 1572896 | tf_op jit(solution)/shard_map/ppermute | solution.py:367
  49.7 4.5 %shard_map.95 = bf16[512,1024]{1,0:T(8,128)(2,1)} custom-call(s32[2]{0:T(128)} %pad_add_fusion.1.at_ref, bf16[512,4096]{1,0:T(8,128)(2,1)} %x_ref.11, bf16[512,1536]{1,0:T(8,128)(2,1)} %copy-done, bf16[512,2048]{1,0:T(8,128)(2,1)} %refs_1_.9, bf16[512,1536]{1,0:T(8,128)(2,1)} %copy-done), custom_call_target="tpu_custom_call" | custom-call | flops 1073741824 | bytes 4194304 | tf_op jit(solution)/shard_map/pallas_call | solution.py:34
  61.5 2.9 %shard_map.97 = bf16[512,1024]{1,0:T(8,128)(2,1)} custom-call(s32[2]{0:T(128)} %pad_add_fusion.3.at_ref, bf16[512,4096]{1,0:T(8,128)(2,1)} %x_ref.11, bf16[512,4096]{1,0:T(8,128)(2,1)} %x_ref.11), custom_call_target="tpu_custom_call" | custom-call | bytes 4194304 | tf_op jit(solution)/shard_map/pallas_call | solution.py:34
  64.5 17.0 %collective-permute-done.5.refs_1_.x_other_ref.refs_3_ = bf16[512,1536]{1,0:T(8,128)(2,1)S(1)} collective-permute-done((bf16[512,1536]{1,0:T(8,128)(2,1)}, bf16[512,1536]{1,0:T(8,128)(2,1)S(1)}, u32[]{:S(2)}, u32[]{:S(2)}) %collective-permute-start.5) | collective-permute-done | bytes 1572896 | tf_op jit(solution)/shard_map/ppermute | solution.py:373
  82.7 4.5 %shard_map.98 = bf16[512,1024]{1,0:T(8,128)(2,1)} custom-call(s32[2]{0:T(128)} %pad_add_fusion.1.at_ref, bf16[512,4096]{1,0:T(8,128)(2,1)} %x_ref.11, bf16[512,1536]{1,0:T(8,128)(2,1)} %copy-done, bf16[512,2048]{1,0:T(8,128)(2,1)} %refs_1_.9, bf16[512,1536]{1,0:T(8,128)(2,1)} %copy-done.1), custom_call_target="tpu_custom_call" | custom-call | flops 1073741824 | bytes 4194304 | tf_op jit(solution)/shard_map/pallas_call | solution.py:34
  87.2 2.2 collective-permute-start.7
  91.5 6.5 %shard_map.99 = bf16[512,2048]{1,0:T(8,128)(2,1)} custom-call(s32[2]{0:T(128)} %pad_add_fusion.at_ref, bf16[512,4096]{1,0:T(8,128)(2,1)} %x_ref.11, bf16[512,1536]{1,0:T(8,128)(2,1)} %copy-done.1, bf16[512,2048]{1,0:T(8,128)(2,1)} %refs_1_.9, bf16[512,2048]{1,0:T(8,128)(2,1)} %refs_1_.9, bf16[512,1536]{1,0:T(8,128)(2,1)} %copy-done, bf16[512,1536]{1,0:T(8,128)(2,1)} %copy-done.1), custom_call_target="tpu_custom_call" | custom-call | flops 2147483648 | bytes 8388608 | tf_op jit(solution)/shard_map/pallas_call | solution.py:34
  97.9 2.7 %collective-permute-start.13 = (bf16[512,2048]{1,0:T(8,128)(2,1)}, bf16[512,2048]{1,0:T(8,128)(2,1)}, u32[]{:S(2)}, u32[]{:S(2)}) collective-permute-start(bf16[512,2048]{1,0:T(8,128)(2,1)} %shard_map.99), channel_id=1, source_target_pairs={{0,2},{1,3},{6,4},{7,5},{8,10},{9,11},{14,12},{15,13},{16,18},{17,... | collective-permute-start | bytes 6291464 | tf_op jit(solution)/shard_map/ppermute | solution.py:299
  100.7 12.6 %collective-permute-done.7 = bf16[512,1024]{1,0:T(8,128)(2,1)S(1)} collective-permute-done((bf16[512,1024]{1,0:T(8,128)(2,1)}, bf16[512,1024]{1,0:T(8,128)(2,1)S(1)}, u32[]{:S(2)}, u32[]{:S(2)}) %collective-permute-start.7) | collective-permute-done | bytes 1048608 | tf_op jit(solution)/shard_map/ppermute | solution.py:299
  121.7 13.5 %shard_map.100 = (bf16[512,4096]{1,0:T(8,128)(2,1)}, bf16[512,1536]{1,0:T(8,128)(2,1)}) custom-call(s32[3]{0:T(128)} %pad_add_fusion.5.at_ref, bf16[512,2048]{1,0:T(8,128)(2,1)} %refs_1_.9, bf16[512,1536]{1,0:T(8,128)(2,1)} %copy-done, bf16[512,1536]{1,0:T(8,128)(2,1)} %copy-done.1, bf16[512,2048]{1,0:T(8,128)(2,1)} %get-tuple-element.73.refs_2_, ...), custom_call_target="tpu_custom_call" | custom-call | flops 6442450944 | bytes 23068672 | tf_op jit(solution)/shard_map/pallas_call | solution.py:34
  135.3 3.8 %collective-permute-done.10.x_other_ref = bf16[512,1024]{1,0:T(8,128)(2,1)S(1)} collective-permute-done((bf16[512,1024]{1,0:T(8,128)(2,1)S(1)}, bf16[512,1024]{1,0:T(8,128)(2,1)S(1)}, u32[]{:S(2)}, u32[]{:S(2)}) %collective-permute-start.10) | collective-permute-done | bytes 1048608 | tf_op jit(solution)/shard_map/ppermute | solution.py:299
  141.4 5.0 %shard_map.101 = bf16[512,1024]{1,0:T(8,128)(2,1)} custom-call(s32[2]{0:T(128)} %pad_add_fusion.4.at_ref, bf16[512,4096]{1,0:T(8,128)(2,1)} %x_ref.11, bf16[512,1024]{1,0:T(8,128)(2,1)} %copy-done.2, bf16[512,2048]{1,0:T(8,128)(2,1)} %refs_1_.9, bf16[512,1536]{1,0:T(8,128)(2,1)} %copy-done, bf16[512,1024]{1,0:T(8,128)(2,1)} %collective-permute-done.14.refs_2_), custom_call_target="tpu_custom_call" | custom-call | flops 1073741824 | bytes 4194304 | tf_op jit(solution)/shard_map/pallas_call | solution.py:34
  146.4 9.2 %collective-permute-start.17 = (bf16[512,1024]{1,0:T(8,128)(2,1)}, bf16[512,1024]{1,0:T(8,128)(2,1)}, u32[]{:S(2)}, u32[]{:S(2)}) collective-permute-start(bf16[512,1024]{1,0:T(8,128)(2,1)} %shard_map.101), channel_id=1, source_target_pairs={{0,2},{1,3},{2,0},{3,1},{4,6},{5,7},{6,4},{7,5},{8,10},{9,11},{10,... | collective-permute-start | bytes 3145736 | tf_op jit(solution)/shard_map/ppermute | solution.py:299
  155.6 2.6 collective-permute-done.13
  165.0 4.9 %shard_map.102 = bf16[512,1024]{1,0:T(8,128)(2,1)} custom-call(s32[2]{0:T(128)} %pad_add_fusion.4.at_ref, bf16[512,4096]{1,0:T(8,128)(2,1)} %x_ref.11, bf16[512,1024]{1,0:T(8,128)(2,1)} %copy-done.2, bf16[512,2048]{1,0:T(8,128)(2,1)} %refs_1_.9, bf16[512,1536]{1,0:T(8,128)(2,1)} %copy-done.1, bf16[512,1024]{1,0:T(8,128)(2,1)} %collective-permute-done.12.refs_2_), custom_call_target="tpu_custom_call" | custom-call | flops 1073741824 | bytes 4194304 | tf_op jit(solution)/shard_map/pallas_call | solution.py:34
  170.0 9.1 %collective-permute-start.21 = (bf16[512,1024]{1,0:T(8,128)(2,1)}, bf16[512,1024]{1,0:T(8,128)(2,1)}, u32[]{:S(2)}, u32[]{:S(2)}) collective-permute-start(bf16[512,1024]{1,0:T(8,128)(2,1)} %shard_map.102), channel_id=1, source_target_pairs={{0,2},{1,3},{2,0},{3,1},{4,6},{5,7},{6,4},{7,5},{8,10},{9,11},{10,... | collective-permute-start | bytes 3145736 | tf_op jit(solution)/shard_map/ppermute | solution.py:299
  179.1 3.7 %subtract_convert_fusion.1 = (bf16[512,512]{1,0:T(8,128)(2,1)}, f32[512,512]{1,0:T(8,128)}) fusion(f32[512,512]{1,0:T(8,128)S(1)} %copy-done.10, f32[512,512]{1,0:T(8,128)S(1)} %copy-done.4, f32[512,512]{1,0:T(8,128)} %collective-permute-done.3, f32[512,1024]{1,0:T(8,128)} %collective-permute-done.2, s32[]{:T(128)S(6)} %select_n.119, ...), kind=kLoop, calls=%fused_computation.45 | loop fusion | flops 2883584 | bytes 6815752 | tf_op jit(solution)/shard_map/convert_element_type | solution.py:464
  183.5 6.3 %shard_map.103 = (bf16[512,4096]{1,0:T(8,128)(2,1)}, bf16[512,512]{1,0:T(8,128)(2,1)}) custom-call(s32[1]{0:T(128)} %bitcast.15.at_ref, bf16[512,2048]{1,0:T(8,128)(2,1)} %refs_1_.9, bf16[512,1536]{1,0:T(8,128)(2,1)} %copy-done, bf16[512,1536]{1,0:T(8,128)(2,1)} %copy-done.1, ...), custom_call_target="tpu_custom_call", output_to_operand_aliasing={{0}: (6, {})} | custom-call | flops 2147483648 | bytes 18874368 | tf_op jit(solution)/shard_map/pallas_call | solution.py:34
  189.9 6.3 %shard_map.106 = (f32[512,1024]{1,0:T(8,128)}, f32[512,1024]{1,0:T(8,128)}) custom-call(s32[2]{0:T(128)} %pad_add_fusion.7.at_ref, bf16[512,4096]{1,0:T(8,128)(2,1)} %x_ref.11, bf16[512,1024]{1,0:T(8,128)(2,1)} %copy-done.2, bf16[512,2048]{1,0:T(8,128)(2,1)} %refs_1_.9, bf16[512,2048]{1,0:T(8,128)(2,1)} %refs_1_.9, bf16[512,1536]{1,0:T(8,128)(2,1)} %copy-done, ...), custom_call_target="tpu_custom_call" | custom-call | flops 2147483648 | bytes 16777216 | tf_op jit(solution)/shard_map/pallas_call | solution.py:34
  196.2 4.0 %shard_map.104.held_ref = bf16[512,4096]{1,0:T(8,128)(2,1)} custom-call(s32[3]{0:T(128)} %pad_add_fusion.6.at_ref, bf16[512,1536]{1,0:T(8,128)(2,1)} %collective-permute-done.18.came_ref, bf16[512,4096]{1,0:T(8,128)(2,1)} %get-tuple-element.116.held_ref), custom_call_target="tpu_custom_call", output_to_operand_aliasing={{}: (2, {})} | custom-call | bytes 16777216 | tf_op jit(solution)/shard_map/pallas_call | solution.py:34
  201.8 3.4 %multiply_reduce_fusion.1 = (f32[]{:T(128)}, f32[512,1024]{1,0:T(8,128)S(1)}) fusion(bf16[512,1024]{1,0:T(8,128)(2,1)} %copy-done.8, f32[512,1024]{1,0:T(8,128)} %get-tuple-element.127, bf16[512,1024]{1,0:T(8,128)(2,1)} %collective-permute-done.17), kind=kLoop, calls=%fused_computation.4 | loop fusion | flops 3670015 | bytes 6291460 | tf_op jit(solution)/shard_map/reduce_sum | solution.py:459
  207.9 4.7 %multiply_reduce_fusion = (f32[]{:T(128)}, f32[512,1024]{1,0:T(8,128)}) fusion(bf16[512,1024]{1,0:T(8,128)(2,1)} %collective-permute-done.20, f32[512,1024]{1,0:T(8,128)} %get-tuple-element.128, bf16[512,1024]{1,0:T(8,128)(2,1)} %collective-permute-done.21), kind=kLoop, calls=%fused_computation.3 | loop fusion | flops 3670015 | bytes 6291460 | tf_op jit(solution)/shard_map/reduce_sum | solution.py:459
  214.4 8.2 %all-to-all-start = ((f32[8,1,128]{2,1,0:T(1,128)}), f32[8,1,128]{2,1,0:T(1,128)S(1)}, u32[]{:S(2)}, u32[]{:S(2)}) async-start(f32[8,1,128]{2,1,0:T(1,128)} %broadcast_in_dim.3), calls=%async_computation | async-start | bytes 8192 | tf_op jit(solution)/shard_map/all_to_all | solution.py:470
  222.6 6.4 %all-to-all-done = f32[8,1,128]{2,1,0:T(1,128)S(1)} async-done(((f32[8,1,128]{2,1,0:T(1,128)}), f32[8,1,128]{2,1,0:T(1,128)S(1)}, u32[]{:S(2)}, u32[]{:S(2)}) %all-to-all-start) | async-done | bytes 4128 | tf_op jit(solution)/shard_map/all_to_all | solution.py:470
  230.4 5.4 %fusion.23 = (bf16[512,512]{1,0:T(8,128)(2,1)S(1)}, bf16[512,512]{1,0:T(8,128)(2,1)S(1)}, bf16[512,512]{1,0:T(8,128)(2,1)S(1)}, bf16[512,512]{1,0:T(8,128)(2,1)S(1)}) fusion(f32[1,512,2048]{2,1,0:T(8,128)} %param.11, s32[]{:T(128)S(6)} %select_n.125, f32[1,512,2048]{2,1,0:T(8,128)} %param.10, f32[512,1024]{1,0:T(8,128)} %get-tuple-element.144, ...), kind=kLoop, calls=%fused_computation.53 | loop fusion | flops 12582912 | bytes 14680086 | tf_op jit(solution)/shard_map/convert_element_type | solution.py:479
  241.5 11.2 %collective-permute-done.24 = bf16[512,512]{1,0:T(8,128)(2,1)S(1)} collective-permute-done((bf16[512,512]{1,0:T(8,128)(2,1)S(1)}, bf16[512,512]{1,0:T(8,128)(2,1)S(1)}, u32[]{:S(2)}, u32[]{:S(2)}) %collective-permute-start.24) | collective-permute-done | bytes 524320 | tf_op jit(solution)/shard_map/ppermute | solution.py:299
  252.7 10.4 %collective-permute-done.25 = bf16[512,512]{1,0:T(8,128)(2,1)S(1)} collective-permute-done((bf16[512,512]{1,0:T(8,128)(2,1)S(1)}, bf16[512,512]{1,0:T(8,128)(2,1)S(1)}, u32[]{:S(2)}, u32[]{:S(2)}) %collective-permute-start.25) | collective-permute-done | bytes 524320 | tf_op jit(solution)/shard_map/ppermute | solution.py:299
  266.8 2.6 maximum_convert_fusion
  (90 shorter events, 53.0 us)
Async XLA Ops:
  8.0 6.6 %collective-permute-start.2 = (f32[512,1024]{1,0:T(8,128)}, f32[512,1024]{1,0:T(8,128)}, u32[]{:S(2)}, u32[]{:S(2)}) collective-permute-start(f32[512,1024]{1,0:T(8,128)} %get-tuple-element.75), channel_id=1, source_target_pairs={{0,8},{8,0},{16,24},{24,16},{1,9},{9,1},{17,25},{25,17},{2,10},{10... | collective-permute-start | bytes 6291464 | tf_op jit(solution)/shard_map/ppermute | solution.py:371
  8.5 49.2 %collective-permute-start = (bf16[512,2048]{1,0:T(8,128)(2,1)}, bf16[512,2048]{1,0:T(8,128)(2,1)}, u32[]{:S(2)}, u32[]{:S(2)}) collective-permute-start(bf16[512,2048]{1,0:T(8,128)(2,1)} %get-tuple-element.73.refs_2_), channel_id=1, source_target_pairs={{0,2},{1,3},{2,0},{3,1},{4,6},{5,7},{6,4},{7,5},{8,10},{9,11},{10,... | collective-permute-start | bytes 6291464 | tf_op jit(solution)/shard_map/ppermute | solution.py:365
  11.1 37.4 %collective-permute-start.1 = (bf16[512,1536]{1,0:T(8,128)(2,1)}, bf16[512,1536]{1,0:T(8,128)(2,1)S(1)}, u32[]{:S(2)}, u32[]{:S(2)}) collective-permute-start(bf16[512,1536]{1,0:T(8,128)(2,1)} %get-tuple-element.74), channel_id=1, source_target_pairs={{0,1},{1,0},{2,3},{3,2},{4,5},{5,4},{6,7},{7,6},{8,9},{9,8},{10,11... | collective-permute-start | bytes 4718600 | tf_op jit(solution)/shard_map/ppermute | solution.py:367
  12.6 47.0 %collective-permute-start.6 = (bf16[512,2048]{1,0:T(8,128)(2,1)}, bf16[512,2048]{1,0:T(8,128)(2,1)}, u32[]{:S(2)}, u32[]{:S(2)}) collective-permute-start(bf16[512,2048]{1,0:T(8,128)(2,1)} %get-tuple-element.73.refs_2_), channel_id=1, source_target_pairs={{2,4},{3,5},{4,2},{5,3},{10,12},{11,13},{12,10},{13,11},{18,20},{1... | collective-permute-start | bytes 6291464 | tf_op jit(solution)/shard_map/ppermute | solution.py:366
  17.3 40.3 %collective-permute-start.3 = (f32[512,512]{1,0:T(8,128)}, f32[512,512]{1,0:T(8,128)}, u32[]{:S(2)}, u32[]{:S(2)}) collective-permute-start(f32[512,512]{1,0:T(8,128)} %bitcast_add_fusion.5), channel_id=1, source_target_pairs={{0,16},{8,24},{16,0},{24,8},{1,17},{9,25},{17,1},{25,9},{2,18},{10... | collective-permute-start | bytes 3145736 | tf_op jit(solution)/shard_map/ppermute | solution.py:379
  22.7 58.8 %collective-permute-start.5 = (bf16[512,1536]{1,0:T(8,128)(2,1)}, bf16[512,1536]{1,0:T(8,128)(2,1)S(1)}, u32[]{:S(2)}, u32[]{:S(2)}) collective-permute-start(bf16[512,1536]{1,0:T(8,128)(2,1)} %shard_map.96), channel_id=1, source_target_pairs={{0,1},{1,0},{2,3},{3,2},{4,5},{5,4},{6,7},{7,6},{8,9},{9,8},{10,11... | collective-permute-start | bytes 4718600 | tf_op jit(solution)/shard_map/ppermute | solution.py:373
  54.3 35.2 %collective-permute-start.8 = (bf16[512,1024]{1,0:T(8,128)(2,1)}, bf16[512,1024]{1,0:T(8,128)(2,1)S(1)}, u32[]{:S(2)}, u32[]{:S(2)}) collective-permute-start(bf16[512,1024]{1,0:T(8,128)(2,1)} %shard_map.95), channel_id=1, source_target_pairs={{0,2},{1,3},{6,4},{7,5},{8,10},{9,11},{14,12},{15,13},{16,18},{17,... | collective-permute-start | bytes 3145736 | tf_op jit(solution)/shard_map/ppermute | solution.py:299
  57.7 57.0 %collective-permute-start.4 = (bf16[512,2048]{1,0:T(8,128)(2,1)}, bf16[512,2048]{1,0:T(8,128)(2,1)}, u32[]{:S(2)}, u32[]{:S(2)}) collective-permute-start(bf16[512,2048]{1,0:T(8,128)(2,1)} %collective-permute-done.refs_3_), channel_id=1, source_target_pairs={{2,4},{3,5},{4,2},{5,3},{10,12},{11,13},{12,10},{13,11},{18,20},{1... | collective-permute-start | bytes 6291464 | tf_op jit(solution)/shard_map/ppermute | solution.py:299
  59.7 59.7 %collective-permute-start.11 = (bf16[512,2048]{1,0:T(8,128)(2,1)}, bf16[512,2048]{1,0:T(8,128)(2,1)}, u32[]{:S(2)}, u32[]{:S(2)}) collective-permute-start(bf16[512,2048]{1,0:T(8,128)(2,1)} %collective-permute-done.6.refs_4_), channel_id=1, source_target_pairs={{2,0},{3,1},{4,6},{5,7},{10,8},{11,9},{12,14},{13,15},{18,16},{19,... | collective-permute-start | bytes 6291464 | tf_op jit(solution)/shard_map/ppermute | solution.py:299
  64.5 25.0 %copy-start.6 = (bf16[512,1024]{1,0:T(8,128)(2,1)S(1)}, bf16[512,1024]{1,0:T(8,128)(2,1)}, u32[]{:S(2)}) copy-start(bf16[512,1024]{1,0:T(8,128)(2,1)} %shard_map.95) | copy-start | bytes 3145732
  87.2 26.1 %collective-permute-start.7 = (bf16[512,1024]{1,0:T(8,128)(2,1)}, bf16[512,1024]{1,0:T(8,128)(2,1)S(1)}, u32[]{:S(2)}, u32[]{:S(2)}) collective-permute-start(bf16[512,1024]{1,0:T(8,128)(2,1)} %shard_map.98), channel_id=1, source_target_pairs={{0,2},{1,3},{6,4},{7,5},{8,10},{9,11},{14,12},{15,13},{16,18},{17,... | collective-permute-start | bytes 3145736 | tf_op jit(solution)/shard_map/ppermute | solution.py:299
  91.5 21.8 %copy-start.7 = (bf16[512,1024]{1,0:T(8,128)(2,1)S(1)}, bf16[512,1024]{1,0:T(8,128)(2,1)}, u32[]{:S(2)}) copy-start(bf16[512,1024]{1,0:T(8,128)(2,1)} %shard_map.98) | copy-start | bytes 3145732
  97.9 18.0 %copy-start.9 = (bf16[512,1024]{1,0:T(8,128)(2,1)S(1)}, bf16[512,1024]{1,0:T(8,128)(2,1)}, u32[]{:S(2)}) copy-start(bf16[512,1024]{1,0:T(8,128)(2,1)} %shard_map.97) | copy-start | bytes 3145732
  97.9 60.3 %collective-permute-start.13 = (bf16[512,2048]{1,0:T(8,128)(2,1)}, bf16[512,2048]{1,0:T(8,128)(2,1)}, u32[]{:S(2)}, u32[]{:S(2)}) collective-permute-start(bf16[512,2048]{1,0:T(8,128)(2,1)} %shard_map.99), channel_id=1, source_target_pairs={{0,2},{1,3},{6,4},{7,5},{8,10},{9,11},{14,12},{15,13},{16,18},{17,... | collective-permute-start | bytes 6291464 | tf_op jit(solution)/shard_map/ppermute | solution.py:299
  114.7 55.3 %collective-permute-start.9 = (bf16[512,2048]{1,0:T(8,128)(2,1)}, bf16[512,2048]{1,0:T(8,128)(2,1)}, u32[]{:S(2)}, u32[]{:S(2)}) collective-permute-start(bf16[512,2048]{1,0:T(8,128)(2,1)} %collective-permute-done.4.refs_2_), channel_id=1, source_target_pairs={{2,0},{3,1},{4,6},{5,7},{10,8},{11,9},{12,14},{13,15},{18,16},{19,... | collective-permute-start | bytes 6291464 | tf_op jit(solution)/shard_map/ppermute | solution.py:299
  116.0 23.1 %collective-permute-start.10 = (bf16[512,1024]{1,0:T(8,128)(2,1)S(1)}, bf16[512,1024]{1,0:T(8,128)(2,1)S(1)}, u32[]{:S(2)}, u32[]{:S(2)}) collective-permute-start(bf16[512,1024]{1,0:T(8,128)(2,1)S(1)} %copy-done.9), channel_id=1, source_target_pairs={{0,1},{1,0},{2,3},{3,2},{4,5},{5,4},{6,7},{7,6},{8,9},{9,8},{10,11... | collective-permute-start | bytes 3145736 | tf_op jit(solution)/shard_map/ppermute | solution.py:299
  117.7 23.6 %collective-permute-start.14 = (bf16[512,1024]{1,0:T(8,128)(2,1)}, bf16[512,1024]{1,0:T(8,128)(2,1)}, u32[]{:S(2)}, u32[]{:S(2)}) collective-permute-start(bf16[512,1024]{1,0:T(8,128)(2,1)} %add_convert_fusion.1), channel_id=1, source_target_pairs={{2,4},{3,5},{4,2},{5,3},{10,12},{11,13},{12,10},{13,11},{18,20},{1... | collective-permute-start | bytes 3145736 | tf_op jit(solution)/shard_map/ppermute | solution.py:299
  119.4 43.9 %collective-permute-start.12 = (bf16[512,1024]{1,0:T(8,128)(2,1)}, bf16[512,1024]{1,0:T(8,128)(2,1)}, u32[]{:S(2)}, u32[]{:S(2)}) collective-permute-start(bf16[512,1024]{1,0:T(8,128)(2,1)} %add_convert_fusion), channel_id=1, source_target_pairs={{2,4},{3,5},{4,2},{5,3},{10,12},{11,13},{12,10},{13,11},{18,20},{1... | collective-permute-start | bytes 3145736 | tf_op jit(solution)/shard_map/ppermute | solution.py:299
  139.1 50.7 %collective-permute-start.18 = (bf16[512,1536]{1,0:T(8,128)(2,1)}, bf16[512,1536]{1,0:T(8,128)(2,1)}, u32[]{:S(2)}, u32[]{:S(2)}) collective-permute-start(bf16[512,1536]{1,0:T(8,128)(2,1)} %get-tuple-element.101), channel_id=1, source_target_pairs={{0,1},{1,0},{2,3},{3,2},{4,5},{5,4},{6,7},{7,6},{8,9},{9,8},{10,11... | collective-permute-start | bytes 4718600 | tf_op jit(solution)/shard_map/ppermute | solution.py:299
  141.4 16.8 %copy-start.3 = (bf16[512,2048]{1,0:T(8,128)(2,1)S(1)}, bf16[512,2048]{1,0:T(8,128)(2,1)}, u32[]{:S(2)}) copy-start(bf16[512,2048]{1,0:T(8,128)(2,1)} %shard_map.99) | copy-start | bytes 6291460
  146.4 53.8 %collective-permute-start.17 = (bf16[512,1024]{1,0:T(8,128)(2,1)}, bf16[512,1024]{1,0:T(8,128)(2,1)}, u32[]{:S(2)}, u32[]{:S(2)}) collective-permute-start(bf16[512,1024]{1,0:T(8,128)(2,1)} %shard_map.101), channel_id=1, source_target_pairs={{0,2},{1,3},{2,0},{3,1},{4,6},{5,7},{6,4},{7,5},{8,10},{9,11},{10,... | collective-permute-start | bytes 3145736 | tf_op jit(solution)/shard_map/ppermute | solution.py:299
  161.9 38.3 %collective-permute-start.16 = (bf16[512,1024]{1,0:T(8,128)(2,1)}, bf16[512,1024]{1,0:T(8,128)(2,1)S(1)}, u32[]{:S(2)}, u32[]{:S(2)}) collective-permute-start(bf16[512,1024]{1,0:T(8,128)(2,1)} %get-tuple-element.106), channel_id=1, source_target_pairs={{2,4},{3,5},{4,2},{5,3},{10,12},{11,13},{12,10},{13,11},{18,20},{1... | collective-permute-start | bytes 3145736 | tf_op jit(solution)/shard_map/ppermute | solution.py:299
  163.3 44.6 %collective-permute-start.20 = (bf16[512,1024]{1,0:T(8,128)(2,1)}, bf16[512,1024]{1,0:T(8,128)(2,1)}, u32[]{:S(2)}, u32[]{:S(2)}) collective-permute-start(bf16[512,1024]{1,0:T(8,128)(2,1)} %get-tuple-element.107), channel_id=1, source_target_pairs={{2,4},{3,5},{4,2},{5,3},{10,12},{11,13},{12,10},{13,11},{18,20},{1... | collective-permute-start | bytes 3145736 | tf_op jit(solution)/shard_map/ppermute | solution.py:299
  170.0 37.9 %collective-permute-start.21 = (bf16[512,1024]{1,0:T(8,128)(2,1)}, bf16[512,1024]{1,0:T(8,128)(2,1)}, u32[]{:S(2)}, u32[]{:S(2)}) collective-permute-start(bf16[512,1024]{1,0:T(8,128)(2,1)} %shard_map.102), channel_id=1, source_target_pairs={{0,2},{1,3},{2,0},{3,1},{4,6},{5,7},{6,4},{7,5},{8,10},{9,11},{10,... | collective-permute-start | bytes 3145736 | tf_op jit(solution)/shard_map/ppermute | solution.py:299
  189.8 15.5 %collective-permute-start.15 = (bf16[512,512]{1,0:T(8,128)(2,1)}, bf16[512,512]{1,0:T(8,128)(2,1)S(1)}, u32[]{:S(2)}, u32[]{:S(2)}) collective-permute-start(bf16[512,512]{1,0:T(8,128)(2,1)} %get-tuple-element.114), channel_id=1, source_target_pairs={{0,1},{1,0},{2,3},{3,2},{4,5},{5,4},{6,7},{7,6},{8,9},{9,8},{10,11... | collective-permute-start | bytes 1572872 | tf_op jit(solution)/shard_map/ppermute | solution.py:299
  200.2 22.4 %collective-permute-start.19 = (bf16[512,512]{1,0:T(8,128)(2,1)}, bf16[512,512]{1,0:T(8,128)(2,1)}, u32[]{:S(2)}, u32[]{:S(2)}) collective-permute-start(bf16[512,512]{1,0:T(8,128)(2,1)} %get-tuple-element.122), channel_id=1, source_target_pairs={{0,16},{8,24},{16,0},{24,8},{1,17},{9,25},{17,1},{25,9},{2,18},{10... | collective-permute-start | bytes 1572872 | tf_op jit(solution)/shard_map/ppermute | solution.py:465
  214.4 14.6 %all-to-all-start = ((f32[8,1,128]{2,1,0:T(1,128)}), f32[8,1,128]{2,1,0:T(1,128)S(1)}, u32[]{:S(2)}, u32[]{:S(2)}) async-start(f32[8,1,128]{2,1,0:T(1,128)} %broadcast_in_dim.3), calls=%async_computation | async-start | bytes 8192 | tf_op jit(solution)/shard_map/all_to_all | solution.py:470
  235.8 2.0 collective-permute-start.22
  235.8 3.6 %collective-permute-start.23 = (bf16[512,512]{1,0:T(8,128)(2,1)S(1)}, bf16[512,512]{1,0:T(8,128)(2,1)S(1)}, u32[]{:S(2)}, u32[]{:S(2)}) collective-permute-start(bf16[512,512]{1,0:T(8,128)(2,1)S(1)} %get-tuple-element.133), channel_id=1, source_target_pairs={{0,8},{8,0},{16,24},{24,16},{1,9},{9,1},{17,25},{25,17},{2,10},{10... | collective-permute-start | bytes 1572872 | tf_op jit(solution)/shard_map/ppermute | solution.py:299
  237.9 14.8 %collective-permute-start.24 = (bf16[512,512]{1,0:T(8,128)(2,1)S(1)}, bf16[512,512]{1,0:T(8,128)(2,1)S(1)}, u32[]{:S(2)}, u32[]{:S(2)}) collective-permute-start(bf16[512,512]{1,0:T(8,128)(2,1)S(1)} %add_convert_fusion.3), channel_id=1, source_target_pairs={{0,16},{8,24},{16,0},{24,8},{1,17},{9,25},{17,1},{25,9},{2,18},{10... | collective-permute-start | bytes 1572872 | tf_op jit(solution)/shard_map/ppermute | solution.py:299
  239.6 23.5 %collective-permute-start.25 = (bf16[512,512]{1,0:T(8,128)(2,1)S(1)}, bf16[512,512]{1,0:T(8,128)(2,1)S(1)}, u32[]{:S(2)}, u32[]{:S(2)}) collective-permute-start(bf16[512,512]{1,0:T(8,128)(2,1)S(1)} %add_convert_fusion.2), channel_id=1, source_target_pairs={{0,16},{8,24},{16,0},{24,8},{1,17},{9,25},{17,1},{25,9},{2,18},{10... | collective-permute-start | bytes 1572872 | tf_op jit(solution)/shard_map/ppermute | solution.py:299
  263.6 2.7 %collective-permute-start.26 = (bf16[512,1024]{1,0:T(8,128)(2,1)S(1)}, bf16[512,1024]{1,0:T(8,128)(2,1)S(1)}, u32[]{:S(2)}, u32[]{:S(2)}) collective-permute-start(bf16[512,1024]{1,0:T(8,128)(2,1)S(1)} %get-tuple-element.141), channel_id=1, source_target_pairs={{0,8},{8,0},{16,24},{24,16},{1,9},{9,1},{17,25},{25,17},{2,10},{10... | collective-permute-start | bytes 3145736 | tf_op jit(solution)/shard_map/ppermute | solution.py:299
  (8 other events, 40.0 us)
